TPU v7x, 32 devices: a whole 2x2x4 slice. The times are simulated.
32 devices in a mesh: vis: 8 (over y, x, core), wav: 4 (over z).
Axes of the slice: x: 2, y: 2, z: 4, core: 2. Of those that a mesh axis runs over, the one named last changes fastest.
Arguments:
- image: float32 [4096, 4096], P('vis', 'wav'), may hold values from -6 to 6
- kernel_v: bfloat16 [1024, 64, 256], P(('vis', 'wav')), may hold values from -0.5 to 0.5
- kernel_u: bfloat16 [1024, 64, 256], P(('vis', 'wav')), may hold values from -0.5 to 0.5
- measured: bfloat16 [1024, 2, 256], P(('vis', 'wav')), may hold values from -4 to 4
- dest_owner: int32 [1024, 1], P(('vis', 'wav')), may hold values from 0 to 7; in each aligned block of 32 rows (0 to 31, 32 to 63, ...) at most 8 rows name the same one
- patch_slot: int32 [1024], P(('vis', 'wav')), may hold values from 0 to 127
- thresholds: float32 [4], replicated, may hold values from 0.1 to 1
Outputs:
- restored: float32 [4096, 4096], P('vis', 'wav')
- residual: float32 [1024, 2, 256], P(('vis', 'wav'))
Inputs may be any that keep to these rules, and one draw needn't show every extreme that they name: `dest_owner`: the vis index of the owner of the block's uv cells; the 32 blocks of one device name one owner at most 8 times, a bound that some block reaches. `patch_slot`: the block's kernel block among the 128 of its owner's tile in the band of the block's wav index.
All inputs are finite; a program needn't handle non-finite values.
Results may differ from a plain program's by a relative error of at most 0.0017.
Values may be sent and summed in bfloat16 or wider, within the bound.
No kernel may reach another device: no remote copies, remote signals or barrier semaphores. Data moves between devices by JAX's collectives and lax.ppermute only.
A program may use at most 128 MiB of HBM per device.

v0:
```python
import math

import jax
import jax.numpy as jnp
import numpy as np
from jax import lax
from jax.experimental import pallas as pl
from jax.experimental.pallas import tpu as pltpu
from jax.sharding import PartitionSpec as P


PATCH = 64
HIGH = lax.Precision.HIGH
F32 = jnp.float32
BF16 = jnp.bfloat16
F16 = jnp.float16


def turns(rows, cols, period):
    angle = (rows * cols % period).astype(F32) * (2.0 * math.pi / period)
    return jnp.cos(angle), jnp.sin(angle)


def iota(size):
    return jnp.arange(size, dtype=jnp.int32)


def spread_matrix(groups, size):
    width = groups * size
    c = iota(width)
    return (c[:, None] == (c % size * groups + c // size)[None, :]).astype(F32)


def rows_forward(x, groups):
    rows = x.shape[1]
    count = groups * rows
    cos_g, sin_g = (np.cos(2 * np.pi * np.outer(np.arange(groups), np.arange(groups)) / groups), np.sin(2 * np.pi * np.outer(np.arange(groups), np.arange(groups)) / groups))
    mixed_re = jnp.einsum("kv,vnm->knm", jnp.asarray(cos_g, F32), x, precision=HIGH)
    mixed_im = -jnp.einsum("kv,vnm->knm", jnp.asarray(sin_g, F32), x, precision=HIGH)
    cos_t, sin_t = turns(iota(groups)[:, None], iota(rows)[None, :], count)
    cos_t, sin_t = cos_t[:, :, None], sin_t[:, :, None]
    both = jnp.concatenate([mixed_re * cos_t + mixed_im * sin_t, mixed_im * cos_t - mixed_re * sin_t], -1)
    cos_r, sin_r = turns(iota(rows)[:, None], iota(rows)[None, :], rows)
    p = jnp.einsum("kn,vnm->vkm", cos_r, both, precision=HIGH)
    q = jnp.einsum("kn,vnm->vkm", sin_r, both, precision=HIGH)
    m = x.shape[2]
    return jnp.concatenate([p[..., :m] + q[..., m:], p[..., m:] - q[..., :m]], -1)


def rows_inverse(y, groups):
    rows = y.shape[1]
    m = y.shape[2] // 2
    count = groups * rows
    cos_r, sin_r = turns(iota(rows)[:, None], iota(rows)[None, :], rows)
    p = jnp.einsum("kn,vnm->vkm", cos_r, y, precision=HIGH)
    q = jnp.einsum("kn,vnm->vkm", sin_r, y, precision=HIGH)
    re, im = p[..., :m] - q[..., m:], p[..., m:] + q[..., :m]
    cos_t, sin_t = turns(iota(groups)[:, None], iota(rows)[None, :], count)
    cos_t, sin_t = cos_t[:, :, None], sin_t[:, :, None]
    re, im = re * cos_t - im * sin_t, im * cos_t + re * sin_t
    cos_g, sin_g = (np.cos(2 * np.pi * np.outer(np.arange(groups), np.arange(groups)) / groups), np.sin(2 * np.pi * np.outer(np.arange(groups), np.arange(groups)) / groups))
    out = jnp.einsum("vk,knm->vnm", jnp.asarray(cos_g, F32), re, precision=HIGH)
    return out - jnp.einsum("vk,knm->vnm", jnp.asarray(sin_g, F32), im, precision=HIGH)


def column_matrix(wavs, m, down, scale):
    size = wavs * m
    cos_c, sin_c = turns(iota(size)[:, None], iota(size)[None, :], size)
    cos_c = (cos_c * scale).reshape(wavs, 1, m, down, 1, PATCH)
    sin_c = (sin_c * scale).reshape(wavs, 1, m, down, 1, PATCH)
    from_re = jnp.concatenate([cos_c, -sin_c], 4)
    from_im = jnp.concatenate([sin_c, cos_c], 4)
    return jnp.concatenate([from_re, from_im], 1).reshape(2 * size, 2 * size)


def split(x):
    high = lax.reduce_precision(x, 8, 7)
    return high.astype(BF16), (x - high).astype(BF16)


def bits(size):
    return size.bit_length() - 1


def cosine(count, period):
    part = (count & (period - 1)).astype(F32) * (1.0 / period)
    part = 0.25 - jnp.abs(part - jnp.where(part > 0.5, 1.0, 0.0))
    square = part * part
    terms = [(-1) ** i * (2 * math.pi) ** (2 * i + 1) / math.factorial(2 * i + 1) for i in range(7)]
    value = jnp.full_like(part, terms[-1])
    for term in terms[-2::-1]:
        value = value * square + term
    return value * part


def grid_of(shape):
    return [lax.broadcasted_iota(jnp.int32, shape, axis) for axis in (0, 1)]


def row_table(size, first):
    k, n = grid_of((2 * size, size))
    return split(cosine(((k + first) & (size - 1)) * n - (k >> bits(size)) * (size // 4), size))


def row_table_back(size, first):
    r, k = grid_of((2 * size, size))
    return split(cosine(((k + first) & (size - 1)) * (r & (size - 1)) - (r >> bits(size)) * (size // 4), size))


def column_table(wavs, m, first, turned):
    size = wavs * m
    row, col = grid_of((2 * size, 2 * size))[:: -1 if turned else 1]
    n = (row >> bits(2 * m)) * m + (row & (m - 1)) + first * m
    k = (col >> bits(2 * PATCH)) * PATCH + (col & (PATCH - 1))
    quarter = (col >> bits(PATCH) & 1) - (row >> bits(m) & 1)
    return split(cosine((n & (size - 1)) * k + quarter * (size // 4), size))


def twist_table(groups, rows):
    n, k = grid_of((rows, 2 * groups))
    count = groups * rows
    return cosine(n * (k & (groups - 1)) - (k >> bits(groups)) * (count // 4), count)


def in_vmem(count):
    return [pl.BlockSpec(memory_space=pltpu.VMEM)] * count


VMEM_LIMIT = 12 * 1024 * 1024
ROOT = math.sqrt(0.5)


AT_ONCE = 8
HALVES = ((0, 1, 7, 2, 6), (4, 3, 5))
ORDER = HALVES[0] + HALVES[1]


def call(kernel, out_shapes, scratch, *args, smem=0):
    return pl.pallas_call(
        kernel,
        in_specs=[pl.BlockSpec(memory_space=pltpu.SMEM)] * smem + in_vmem(len(args) - smem),
        out_specs=in_vmem(len(out_shapes)),
        out_shape=[jax.ShapeDtypeStruct(shape, kind) for shape, kind in out_shapes],
        scratch_shapes=[pltpu.VMEM(shape, kind) for shape, kind in scratch],
        compiler_params=pltpu.CompilerParams(vmem_limit_bytes=VMEM_LIMIT),
    )(*args)


def spread_kernel(image_ref, out_ref):
    groups, _, m = out_ref.shape
    width = groups * m
    high = image_ref[...].astype(BF16)
    low = (image_ref[...] - high.astype(F32)).astype(BF16)
    c = lax.broadcasted_iota(jnp.int32, (width, 2 * m), 0)
    place = lax.broadcasted_iota(jnp.int32, (width, 2 * m), 1)
    for v in range(0, groups, 2):
        table = (c == (place & (m - 1)) * groups + (place >> bits(m)) + v).astype(F32).astype(BF16)
        out = jnp.dot(high, table, preferred_element_type=F32) + jnp.dot(low, table, preferred_element_type=F32)
        out_ref[v] = out[:, :m]
        out_ref[v + 1] = out[:, m:]


def rows_forward_kernel(x_ref, high_ref, low_ref, twist_ref, *y_refs, half):
    rows, m = x_ref.shape[1:]
    wavs = len(y_refs)
    part = rows // wavs
    x = [x_ref[i].astype(F32) for i in range(8)]
    e0, e1, f0, f1 = x[0] + x[4], x[0] - x[4], x[2] + x[6], x[2] - x[6]
    g0, g1, h0, h1 = x[1] + x[5], x[1] - x[5], x[3] + x[7], x[3] - x[7]
    gm, gp = (g1 - h1) * ROOT, (g1 + h1) * ROOT
    zero = jnp.zeros_like(e0)
    mixed = {
        0: (e0 + f0 + g0 + h0, zero),
        1: (e1 + gm, -f1 - gp),
        2: (e0 - f0, h0 - g0),
        3: (e1 - gm, f1 - gp),
        4: (e0 + f0 - g0 - h0, zero),
    }
    for spot, k in enumerate(HALVES[half]):
        if k > 4:
            continue
        re, im = mixed[k]
        if k:
            cos_t, sin_t = twist_ref[:, k : k + 1], twist_ref[:, 8 + k : 9 + k]
            re, im = re * cos_t + im * sin_t, im * cos_t - re * sin_t
        both = jnp.concatenate([re, im], 1)
        high = both.astype(BF16)
        low = (both - high.astype(F32)).astype(BF16)
        out = jnp.dot(high_ref[...], high, preferred_element_type=F32)
        out += jnp.dot(high_ref[...], low, preferred_element_type=F32)
        out += jnp.dot(low_ref[...], high, preferred_element_type=F32)
        p_re, p_im, q_re, q_im = out[:rows, :m], out[:rows, m:], out[rows:, :m], out[rows:, m:]
        here = jnp.concatenate([p_re + q_im, p_im - q_re], 1)
        for w in range(wavs):
            y_refs[w][spot] = here[w * part : (w + 1) * part]
        if k in (1, 2, 3):
            there = jnp.concatenate([p_re - q_im, -p_im - q_re], 1)
            there = pltpu.roll(there, rows - 1, 0)
            for w in range(wavs):
                y_refs[w][spot + 1] = there[w * part : (w + 1) * part]


def rows_forward_fast(x, wavs, table, twist, half):
    _, rows, m = x.shape
    kernel = lambda *refs: rows_forward_kernel(*refs, half=half)
    return call(kernel, [((len(HALVES[half]), rows // wavs, 2 * m), F32)] * wavs, [], x, *table, twist)


def shares_kernel(a_ref, b_ref, *refs, wavs):
    y_refs = refs[:wavs]
    high_ref, low_ref, cos_ref, sin_ref, far_ref, near_ref, z_ref, head_ref, rest_ref = refs[wavs:]
    groups, part, double = y_refs[0].shape
    down = z_ref.shape[0]
    wide = 2 * PATCH
    low = 8
    blocks = near_ref.shape[1]
    scale = 1.0 / (8 * down * PATCH)
    for w in range(wavs):
        y = y_refs[w][...].astype(F32).reshape(groups * part, double)
        high = y.astype(BF16)
        head_ref[:, w * double : (w + 1) * double] = high
        rest_ref[:, w * double : (w + 1) * double] = (y - high.astype(F32)).astype(BF16)
    for a in range(0, down, 2):
        spot = (slice(None), pl.ds(a * wide, 2 * wide))
        z = jnp.dot(head_ref[...], high_ref[spot], preferred_element_type=F32)
        z += jnp.dot(rest_ref[...], high_ref[spot], preferred_element_type=F32)
        z += jnp.dot(head_ref[...], low_ref[spot], preferred_element_type=F32)
        z = z * scale
        z_ref[a] = z[:, :wide].reshape(groups, part, wide)
        z_ref[a + 1] = z[:, wide:].reshape(groups, part, wide)
    for core, out_ref in ((1, far_ref), (0, near_ref)):

        @pl.loop(0, 4 * blocks // AT_ONCE)
        def _(step):
            chip, first = step // (blocks // AT_ONCE), step % (blocks // AT_ONCE) * AT_ONCE
            for i in range(AT_ONCE):
                at = first + i
                n = (2 * chip + core) * blocks + at
                start = pl.multiple_of(b_ref[n] * low, low)
                tile = z_ref[a_ref[n], :, pl.ds(start, low), :].reshape(groups * low, wide)
                out_ref[chip, at] = tile * cos_ref[pl.ds(n, 1), :] + pltpu.roll(tile, PATCH, 1) * sin_ref[pl.ds(n, 1), :]


def shares_fast(a_block, b_block, ys, table, cos_k, sin_k):
    groups, part, double = ys[0].shape
    wavs = len(ys)
    width = wavs * double
    blocks = a_block.shape[0] // 8
    out = ((4, blocks, groups * 8, 2 * PATCH), F32)
    scratch = [((width // (2 * PATCH), groups, part, 2 * PATCH), F32)] + [((groups * part, width), BF16)] * 2
    kernel = lambda *refs: shares_kernel(*refs, wavs=wavs)
    return call(kernel, [out, out], scratch, a_block, b_block, *ys, *table, cos_k, sin_k, smem=2)


def gather_kernel(a_ref, b_ref, *refs):
    high_ref, low_ref, cos_ref, sin_ref = refs[5:9]
    y_refs, (g_ref, head_ref) = refs[9:-2], refs[-2:]
    groups, part, double = y_refs[0].shape
    down = g_ref.shape[0]
    wide = 2 * PATCH
    low = 8
    blocks = refs[0].shape[0]
    g_ref[...] = jnp.zeros_like(g_ref)

    def add(term_ref, mask, first):
        tiles = []
        for i in range(AT_ONCE):
            n = mask * blocks + first + i
            tile = term_ref[first + i].astype(F32)
            tiles.append(tile * cos_ref[pl.ds(n, 1), :] - pltpu.roll(tile, PATCH, 1) * sin_ref[pl.ds(n, 1), :])
        for i in range(AT_ONCE):
            n = mask * blocks + first + i
            start = pl.multiple_of(b_ref[n] * low, low)
            g_ref[a_ref[n], :, pl.ds(start, low), :] += tiles[i].reshape(groups, low, wide)

    steps = blocks // AT_ONCE
    for chip in range(4):
        pl.loop(0, steps)(lambda step: add(refs[chip], 2 * chip, step * AT_ONCE))
    pl.loop(0, 4 * steps)(lambda step: add(refs[4].at[step // steps], 2 * (step // steps) + 1, step % steps * AT_ONCE))

    for a in range(down):
        head_ref[:, a * wide : (a + 1) * wide] = g_ref[a].reshape(groups * part, wide).astype(BF16)
    scale = 1.0 / (8 * down * PATCH)
    for w, y_ref in enumerate(y_refs):
        spot = (slice(None), pl.ds(w * double, double))
        y = jnp.dot(head_ref[...], high_ref[spot], preferred_element_type=F32)
        y += jnp.dot(head_ref[...], low_ref[spot], preferred_element_type=F32)
        y_ref[...] = (y * scale).astype(BF16).reshape(groups, part, double)


def gather_fast(a_block, b_block, terms, table, cos_k, sin_k, wavs, part, m, half):
    width = 2 * wavs * m
    groups = len(HALVES[half])
    out = [((groups, part, 2 * m), BF16)] * wavs
    scratch = [((width // (2 * PATCH), groups, part, 2 * PATCH), F32), ((groups * part, width), BF16)]
    return call(gather_kernel, out, scratch, a_block, b_block, *terms, *table, cos_k, sin_k, smem=2)


def untwist(y_refs, spot, k, high_ref, low_ref, twist_ref):
    y = jnp.concatenate([ref[spot] for ref in y_refs], 0)
    rows, m = y.shape[0], y.shape[1] // 2
    out = jnp.dot(high_ref[...], y, preferred_element_type=F32)
    out += jnp.dot(low_ref[...], y, preferred_element_type=F32)
    re, im = out[:rows, :m] - out[rows:, m:], out[:rows, m:] + out[rows:, :m]
    if k:
        cos_t, sin_t = twist_ref[:, k : k + 1], twist_ref[:, 8 + k : 9 + k]
        re, im = re * cos_t - im * sin_t, im * cos_t + re * sin_t
    return re, im


def rows_inverse_first(*refs):
    y_refs, (high_ref, low_ref, twist_ref, out_ref) = refs[:-4], refs[-4:]
    (re4, _), (re3, im3), (re5, im5) = [
        untwist(y_refs, spot, k, high_ref, low_ref, twist_ref) for spot, k in enumerate(HALVES[1])
    ]
    out_ref[0] = re4
    out_ref[1] = re3 + re5
    out_ref[2] = im3 - im5


def rows_inverse_last(*refs):
    y_refs, (first_ref, high_ref, low_ref, twist_ref, x_ref) = refs[:-5], refs[-5:]
    (re0, _), (re1, im1), (re7, im7), (re2, im2), (re6, im6) = [
        untwist(y_refs, spot, k, high_ref, low_ref, twist_ref) for spot, k in enumerate(HALVES[0])
    ]
    re4, r3, i3 = [first_ref[i] for i in range(3)]
    even, odd = re0 + re4, re0 - re4
    r1, r2, i1, i2 = re1 + re7, re2 + re6, im1 - im7, im2 - im6
    rm, ip = (r1 - r3) * ROOT, (i1 + i3) * ROOT
    x_ref[0] = (even + r2 + (r1 + r3)).astype(BF16)
    x_ref[4] = (even + r2 - (r1 + r3)).astype(BF16)
    x_ref[2] = (even - r2 - (i1 - i3)).astype(BF16)
    x_ref[6] = (even - r2 + (i1 - i3)).astype(BF16)
    x_ref[1] = (odd + rm - ip - i2).astype(BF16)
    x_ref[7] = (odd + rm + ip + i2).astype(BF16)
    x_ref[3] = (odd - rm - ip + i2).astype(BF16)
    x_ref[5] = (odd - rm + ip - i2).astype(BF16)


HALO = 8
LANES = 128


def step_kernel(image_ref, grad_ref, spread_ref, out_ref, first_ref, last_ref):
    _, width = image_ref.shape
    grad = jnp.concatenate([grad_ref[i] for i in range(grad_ref.shape[0])], 1)
    out_ref[...] = image_ref[...] - jnp.dot(grad, spread_ref[...], preferred_element_type=F32)
    first_ref[...] = out_ref[:, :LANES].T[:HALO]
    last_ref[...] = out_ref[:, width - LANES :].T[LANES - HALO :]


def haar_kernel(field_ref, left_ref, right_ref, limit_ref, out_ref, edge_ref, *, bases):
    every, width = field_ref.shape
    rows = 64
    span = width + LANES
    middle = jnp.zeros((LANES - 2 * HALO, every), F32)
    edge_ref[...] = jnp.concatenate([right_ref[...], middle, left_ref[...]], 0).T
    even = lax.broadcasted_iota(jnp.int32, (rows, span), 0) % 2 == 0

    def mix(x, even):
        other = jnp.where(even, pltpu.roll(x, rows - 1, 0), pltpu.roll(x, 1, 0))
        return jnp.where(even, x, -x) + other

    def ahead(x, by):
        return pltpu.roll(x, span - by, 1)

    def behind(x, by):
        return pltpu.roll(x, by, 1)

    def mean(u):
        spot = 0
        level = []
        for period in (2, 4, 8):
            forward = ahead(u, period // 2)
            parts = [u + forward, u - forward]
            limits = []
            for _ in range(0, bases, period):
                limits.append(limit_ref[spot : spot + 1, :])
                spot += 1
            limited = []
            for x in parts if period == 8 else parts[1:]:
                total = None
                for limit in limits:
                    x_soft = x - jnp.minimum(jnp.maximum(x, -limit), limit)
                    total = x_soft if total is None else total + x_soft
                limited.append(total)
            level.append(limited)
            u = parts[0]
        s3, d3 = level[2]
        back = (s3 + d3) + behind(s3 - d3, 4)
        for by, (d,) in ((2, level[1]), (1, level[0])):
            back = back * 0.5
            back = (back + d) + behind(back - d, by)
        return back[:, :width] * (0.25 / bases)

    @pl.loop(0, every // rows)
    def _(step):
        spot = (pl.ds(pl.multiple_of(step * rows, rows), rows), slice(None))
        field = jnp.concatenate([field_ref[spot], edge_ref[spot]], 1)
        out_ref[spot] = mix(mean(mix(field, even)), even[:, :width])


def haar_limits(width, thresholds):
    bases = thresholds.shape[0]
    span = width + LANES
    place = iota(span)
    place = jnp.where(place < width + LANES // 2, place, place - span) + 8
    out = []
    for period in (2, 4, 8):
        scale = math.sqrt(2.0 * period)
        for start in range(0, bases, period):
            index = place % period + start
            limit = jnp.full((span,), 3e38, F32)
            for s in range(start, min(start + period, bases)):
                limit = jnp.where(index == s, thresholds[s] * scale, limit)
            out.append(limit)
    return jnp.stack(out)


def haar_mean(field, halo_left, halo_right, thresholds):
    bases = thresholds.shape[0]
    rows, width = field.shape
    limits = haar_limits(width, thresholds)
    step = LANES
    return pl.pallas_call(
        lambda *refs: haar_kernel(*refs, bases=bases),
        grid=(rows // step,),
        in_specs=[
            pl.BlockSpec((step, width), lambda i: (i, 0)),
            pl.BlockSpec((HALO, step), lambda i: (0, i)),
            pl.BlockSpec((HALO, step), lambda i: (0, i)),
            pl.BlockSpec(limits.shape, lambda i: (0, 0)),
        ],
        out_specs=pl.BlockSpec((step, width), lambda i: (i, 0)),
        out_shape=jax.ShapeDtypeStruct((rows, width), F32),
        scratch_shapes=[pltpu.VMEM((step, LANES), F32)],
        compiler_params=pltpu.CompilerParams(vmem_limit_bytes=VMEM_LIMIT),
        name="haar",
    )(field, halo_left, halo_right, limits)


def phases(owner, a_block, v, rows, img):
    cos_k, sin_k = turns(v, owner[:, None] * rows + a_block[:, None] * PATCH + iota(PATCH)[None, :], img)
    return jnp.concatenate([cos_k, cos_k], 1), jnp.concatenate([sin_k, -sin_k], 1)


def shards_fast(image, kernel_v, kernel_u, measured, dest_owner, patch_slot, thresholds):
    vis = lax.axis_size("vis")
    wavs = lax.axis_size("wav")
    v, w = lax.axis_index("vis"), lax.axis_index("wav")
    rows, cols = image.shape
    img = rows * vis
    m = cols // vis
    across = cols // PATCH
    blocks = kernel_v.shape[0]
    part = rows // wavs

    def flip(x, mask):
        return lax.ppermute(x, "vis", [(i, i ^ mask) for i in range(vis)])

    def ahead(x, by):
        return lax.ppermute(x, "wav", [(i, (i + by) % wavs) for i in range(wavs)])

    def exchange(parts):
        out = [parts[0]]
        for s in range(1, wavs):
            out.append(ahead(parts[wavs - s], wavs - s))
        return out

    def to_chips(parts):
        out = []
        for chip in (1, 2, 3):
            out.append(flip(parts[chip - 1], 2 * chip))
        return out

    x = call(spread_kernel, [((vis, rows, m), F32)], [], image)[0].astype(F16)
    x = lax.all_to_all(x, "vis", split_axis=0, concat_axis=0, tiled=True).astype(F32)

    forward_table, twist = row_table(rows, w * part), twist_table(vis, rows)
    sent, spectra = [], []
    for half in (0, 1):
        y = rows_forward_fast(x, wavs, forward_table, twist, half)
        sent.append([part_y.astype(F16) for part_y in y])
        spectra.append(exchange(sent[half]))
    spectra[0], _ = lax.optimization_barrier((spectra[0], sent[1]))

    ids = jnp.stack([dest_owner[:, 0], patch_slot])
    ids, _ = lax.optimization_barrier((ids, sent[1]))
    for mask in (1, 2, 4):
        ids = jnp.concatenate([ids, flip(ids, mask)], 1)
    owner, slot = ids[0], ids[1]
    a_block, b_block = slot // across, slot % across
    cos_k, sin_k = phases(owner, a_block, v, rows, img)

    table = column_table(wavs, m, w, False)
    patches = []
    for half in (0, 1):
        y = []
        for part_y in spectra[half]:
            y.append(part_y.astype(F32))
        far, near = shares_fast(a_block, b_block, y, table, cos_k, sin_k)
        near = near + flip(far.astype(F16), 1).astype(F32)
        ready = [near[0]] + [near[chip].astype(F16) for chip in (1, 2, 3)]
        if half == 0:
            spectra[1], ready = lax.optimization_barrier((spectra[1], ready))
        total = ready[0]
        for came in to_chips(ready[1:]):
            total = total + came.astype(F32)
        patches.append(total.astype(BF16))

    order = jnp.asarray(ORDER)
    side = kernel_u.reshape(blocks, 8, vis, -1)[:, :, order].transpose(0, 2, 1, 3).reshape(kernel_u.shape).astype(F32)
    cut = 8 * len(HALVES[0])
    sides = [side[:, :cut], side[:, cut:]]
    model = 0.0
    for patch, side in zip(patches, sides):
        part_re = jnp.einsum("nba,nat->nbt", patch[..., :PATCH], kernel_v, preferred_element_type=F32)
        part_im = jnp.einsum("nba,nat->nbt", patch[..., PATCH:], kernel_v, preferred_element_type=F32)
        model = model + jnp.stack([jnp.sum(part_re * side, 1), jnp.sum(part_im * side, 1)], 1)
    misfit = model - measured.astype(F32)

    table_back = column_table(wavs, m, w, True)
    grads = {}
    for half in (1, 0):
        side = sides[half]
        w_re = (misfit[:, 0, None, :] * side).astype(BF16)
        w_im = (misfit[:, 1, None, :] * side).astype(BF16)
        term_re = jnp.einsum("nbt,nat->nba", w_re, kernel_v, preferred_element_type=F32)
        term_im = jnp.einsum("nbt,nat->nba", w_im, kernel_v, preferred_element_type=F32)
        terms = jnp.concatenate([term_re, term_im], -1).astype(BF16)
        if half == 0:
            terms, chips = lax.optimization_barrier((terms, chips))
        chips = [terms] + to_chips([terms] * 3)
        other = flip(jnp.stack(chips), 1)
        grad = gather_fast(a_block, b_block, chips + [other], table_back, cos_k, sin_k, wavs, part, m, half)
        grads[half] = exchange(grad)

    back_table = row_table_back(rows, w * part)
    first = call(rows_inverse_first, [((3, rows, m), F32)], [], *grads[1], *back_table, twist)
    grad = call(rows_inverse_last, [((vis, rows, m), BF16)], [], *grads[0], *first, *back_table, twist)[0]
    grad = lax.all_to_all(grad, "vis", split_axis=0, concat_axis=0, tiled=True)
    edge = ((HALO, rows), F32)
    back = spread_matrix(vis, m).T.astype(BF16)
    shifted, first_cols, last_cols = call(step_kernel, [((rows, cols), F32), edge, edge], [], image, grad, back)
    right = ahead(first_cols, wavs - 1)
    left = ahead(last_cols, 1)
    return haar_mean(shifted, left, right, thresholds), misfit


def shards(image, kernel_v, kernel_u, measured, dest_owner, patch_slot, thresholds):
    vis = lax.axis_size("vis")
    wavs = lax.axis_size("wav")
    v = lax.axis_index("vis")
    rows, cols = image.shape
    img = rows * vis
    m = cols // vis
    down = rows // PATCH
    across = cols // PATCH
    blocks = kernel_v.shape[0]
    low = PATCH // vis
    part = rows // wavs
    if vis == 8 and m == LANES and low == 8 and part % 8 == 0 and rows & (rows - 1) == 0:
        return shards_fast(image, kernel_v, kernel_u, measured, dest_owner, patch_slot, thresholds)
    spread = spread_matrix(vis, m)

    ids = jnp.concatenate([dest_owner, patch_slot[:, None]], 1)
    ids = lax.all_gather(ids, "vis", axis=0, tiled=True)
    owner, slot = ids[:, 0], ids[:, 1]
    a_block, b_block = slot // across, slot % across

    x = jnp.dot(image, spread, precision=HIGH).astype(F16)
    x = x.reshape(rows, vis, m).transpose(1, 0, 2)
    x = lax.all_to_all(x, "vis", split_axis=0, concat_axis=0, tiled=True).astype(F32)
    y = rows_forward(x, vis).astype(F16)
    y = y.reshape(vis, wavs, part, 2 * m).transpose(1, 0, 2, 3)
    y = lax.all_to_all(y, "wav", split_axis=0, concat_axis=0, tiled=True).astype(F32)
    cos_k, sin_k = turns(v, owner[:, None] * rows + a_block[:, None] * PATCH + iota(PATCH)[None, :], img)
    cos_k = jnp.concatenate([cos_k, cos_k], 1)
    sin_k = jnp.concatenate([sin_k, -sin_k], 1)
    y = y.transpose(1, 2, 0, 3).reshape(cols, 2 * wavs * m)
    table = column_matrix(wavs, m, down, 1.0 / img)
    z = jnp.dot(y, table, precision=HIGH)
    z = z.reshape(vis, across, low, down, 2 * PATCH)
    tiles = z[:, b_block, :, a_block, :].reshape(vis * blocks, PATCH, 2 * PATCH)
    tiles = tiles * cos_k[:, None] + jnp.roll(tiles, PATCH, axis=2) * sin_k[:, None]
    tiles = lax.all_to_all(tiles.astype(F16), "vis", split_axis=0, concat_axis=0, tiled=True)
    patch = jnp.sum(tiles.reshape(vis, blocks, PATCH, 2 * PATCH).astype(F32), 0).astype(BF16)

    side_u = kernel_u.reshape(blocks, low, vis, -1).transpose(0, 2, 1, 3).reshape(kernel_u.shape)
    part_re = jnp.einsum("nba,nat->nbt", patch[..., :PATCH], kernel_v, preferred_element_type=F32)
    part_im = jnp.einsum("nba,nat->nbt", patch[..., PATCH:], kernel_v, preferred_element_type=F32)
    side = side_u.astype(F32)
    misfit = jnp.stack([jnp.sum(part_re * side, 1), jnp.sum(part_im * side, 1)], 1) - measured.astype(F32)
    w_re = (misfit[:, 0, None, :] * side).astype(BF16)
    w_im = (misfit[:, 1, None, :] * side).astype(BF16)
    term_re = jnp.einsum("nbt,nat->nba", w_re, kernel_v, preferred_element_type=F32)
    term_im = jnp.einsum("nbt,nat->nba", w_im, kernel_v, preferred_element_type=F32)
    terms = jnp.concatenate([term_re, term_im], -1).astype(BF16)

    terms = lax.all_gather(terms, "vis", axis=0, tiled=True)
    terms = terms.astype(F32)
    terms = terms * cos_k[:, None] - jnp.roll(terms, PATCH, axis=2) * sin_k[:, None]
    terms = terms.reshape(vis * blocks, vis, low, 2 * PATCH)
    flat = jnp.zeros((across * down, vis, low, 2 * PATCH), F32).at[b_block * down + a_block].add(terms)
    grad = flat.reshape(across, down, vis, low, 2 * PATCH).transpose(2, 0, 3, 1, 4).reshape(cols, 2 * rows)
    grad = lax.dot_general(grad, table, (((1,), (1,)), ((), ())), precision=HIGH).astype(BF16)
    grad = grad.reshape(vis, part, wavs, 2 * m).transpose(2, 0, 1, 3)
    grad = lax.all_to_all(grad, "wav", split_axis=0, concat_axis=0, tiled=True)
    grad = grad.astype(F32).transpose(1, 0, 2, 3).reshape(vis, rows, 2 * m)
    grad = rows_inverse(grad, vis).astype(BF16)
    grad = lax.all_to_all(grad, "vis", split_axis=0, concat_axis=0, tiled=True)
    grad = grad.transpose(1, 0, 2).reshape(rows, cols)
    grad = lax.dot_general(grad, spread.astype(BF16), (((1,), (1,)), ((), ())), preferred_element_type=F32)
    shifted = image - grad
    right = lax.ppermute(shifted[:, :HALO].T, "wav", [(i, (i - 1) % wavs) for i in range(wavs)])
    left = lax.ppermute(shifted[:, -HALO:].T, "wav", [(i, (i + 1) % wavs) for i in range(wavs)])
    return haar_mean(shifted, left, right, thresholds), misfit


def solution(mesh):
    both = ("vis", "wav")
    in_specs = (
        P("vis", "wav"),
        P(both, None, None),
        P(both, None, None),
        P(both, None, None),
        P(both, None),
        P(both),
        P(),
    )
    out_specs = (P("vis", "wav"), P(both, None, None))
    return jax.shard_map(shards, mesh=mesh, in_specs=in_specs, out_specs=out_specs, check_vma=False)
```

profile of v0, /device:TPU:2, one launch (start us, length us, event | category | flops | bytes accessed | tf_op | source)
XLA Modules:
  0.0 280.0 jit_solution(2508857416325463479)
XLA Ops:
  0.7 1.7 copy-done.12
  2.3 2.6 shard_map.95
  6.1 4.3 %all-to-all-start = ((f16[8,512,128]{2,1,0:T(8,128)(2,1)}), f16[8,512,128]{2,1,0:T(8,128)(2,1)}, u32[]{:S(2)}, u32[]{:S(2)}) async-start(f16[8,512,128]{2,1,0:T(8,128)(2,1)} %convert_element_type.195), calls=%async_computation | async-start | bytes 2097152 | tf_op jit(solution)/shard_map/all_to_all | solution.py:477
  10.7 5.9 %fusion.13 = (bf16[1024,512]{1,0:T(8,128)(2,1)}, bf16[1024,512]{1,0:T(8,128)(2,1)}, bf16[1024,512]{1,0:T(8,128)(2,1)}, bf16[1024,512]{1,0:T(8,128)(2,1)}) fusion(s32[1024]{0:T(1024)S(1)} %get-tuple-element.119, s32[1024]{0:T(1024)S(1)} %get-tuple-element.118, s32[512]{0:T(512)S(1)} %add_and_fusion.1, s32[1024]{0:T(1024)S(1)} %get-tuple-element.117), kind=kLoop, calls=%fused_computation.37 | loop fusion | flops 29360128 | bytes 4208640 | tf_op jit(solution)/shard_map/convert_element_type | solution.py:78
  16.6 7.8 %all-to-all-done = f16[8,512,128]{2,1,0:T(8,128)(2,1)} async-done(((f16[8,512,128]{2,1,0:T(8,128)(2,1)}), f16[8,512,128]{2,1,0:T(8,128)(2,1)}, u32[]{:S(2)}, u32[]{:S(2)}) %all-to-all-start) | async-done | bytes 1048608 | tf_op jit(solution)/shard_map/all_to_all | solution.py:477
  24.3 1.5 convert_element_type.196.refs_0_
  26.2 2.0 shard_map.96
  32.3 1.5 collective-permute-start.1
  33.8 2.1 collective-permute-done.1
  36.6 9.2 %fusion.1 = (bf16[1024,1024]{1,0:T(8,128)(2,1)}, bf16[1024,1024]{1,0:T(8,128)(2,1)}, bf16[1024,1024]{1,0:T(8,128)(2,1)}, bf16[1024,1024]{1,0:T(8,128)(2,1)}) fusion(s32[1024]{0:T(1024)S(1)} %get-tuple-element.122, s32[1024]{0:T(1024)S(1)} %shift-right-arithmetic_and_fusion, s32[1024]{0:T(1024)S(1)} %get-tuple-element.123, s32[1024]{0:T(1024)S(1)} %get-tuple-element.116), kind=kLoop, calls=%fused_computation.6 | loop fusion | flops 62914560 | bytes 8404992 | tf_op jit(solution)/shard_map/convert_element_type | solution.py:78
  48.2 2.9 %shard_map.97 = (f32[5,128,256]{2,1,0:T(8,128)S(1)}, f32[5,128,256]{2,1,0:T(8,128)S(1)}, f32[5,128,256]{2,1,0:T(8,128)S(1)}, f32[5,128,256]{2,1,0:T(8,128)S(1)}) custom-call(f32[8,512,128]{2,1,0:T(8,128)S(1)} %convert_element_type.196.refs_0_, bf16[1024,512]{1,0:T(8,128)(2,1)S(1)} %copy-done.7, bf16[1024,512]{1,0:T(8,128)(2,1)S(1)} %copy-done.9, ...), custom_call_target="tpu_custom_call" | custom-call | tf_op jit(solution)/shard_map/pallas_call | solution.py:139
  51.2 4.1 %collective-permute-start.6 = (f16[5,128,256]{2,1,0:T(8,128)(2,1)S(1)}, f16[5,128,256]{2,1,0:T(8,128)(2,1)S(1)}, u32[]{:S(2)}, u32[]{:S(2)}) collective-permute-start(f16[5,128,256]{2,1,0:T(8,128)(2,1)S(1)} %convert_element_type.206), channel_id=1, source_target_pairs={{0,3},{1,0},{2,1},{3,2},{4,7},{5,4},{6,5},{7,6},{8,11},{9,8},{10,9... | collective-permute-start | bytes 983048 | tf_op jit(solution)/shard_map/ppermute | solution.py:462
  57.7 5.7 %collective-permute-done.6 = f16[5,128,256]{2,1,0:T(8,128)(2,1)S(1)} collective-permute-done((f16[5,128,256]{2,1,0:T(8,128)(2,1)S(1)}, f16[5,128,256]{2,1,0:T(8,128)(2,1)S(1)}, u32[]{:S(2)}, u32[]{:S(2)}) %collective-permute-start.6) | collective-permute-done | bytes 327712 | tf_op jit(solution)/shard_map/ppermute | solution.py:462
  63.4 18.7 %collective-permute-done.7 = f16[5,128,256]{2,1,0:T(8,128)(2,1)S(1)} collective-permute-done((f16[5,128,256]{2,1,0:T(8,128)(2,1)S(1)}, f16[5,128,256]{2,1,0:T(8,128)(2,1)S(1)}, u32[]{:S(2)}, u32[]{:S(2)}) %collective-permute-start.7) | collective-permute-done | bytes 327712 | tf_op jit(solution)/shard_map/ppermute | solution.py:462
  82.4 8.7 %shard_map.98 = (f32[4,32,40,128]{3,2,1,0:T(8,128)S(1)}, f32[4,32,40,128]{3,2,1,0:T(8,128)S(1)}) custom-call(s32[256]{0:T(256)S(1)} %get-tuple-element.87.refs_0_.a_ref, s32[256]{0:T(256)S(1)} %get-tuple-element.111.refs_1_.b_ref, f32[5,128,256]{2,1,0:T(8,128)S(1)} %convert_element_type.209.refs_2_, f32[5,128,256]{2,1,0:T(8,128)S(1)} %convert_element_type.210.refs_3_, ...), custom_call_target="tpu_custom_call" | custom-call | tf_op jit(solution)/shard_map/pallas_call | solution.py:139
  92.1 2.9 %collective-permute-start.4 = (f16[3,128,256]{2,1,0:T(8,128)(2,1)S(1)}, f16[3,128,256]{2,1,0:T(8,128)(2,1)S(1)}, u32[]{:S(2)}, u32[]{:S(2)}) collective-permute-start(f16[3,128,256]{2,1,0:T(8,128)(2,1)S(1)} %copy-done.22), channel_id=1, source_target_pairs={{0,2},{1,3},{2,0},{3,1},{4,6},{5,7},{6,4},{7,5},{8,10},{9,11},{10,... | collective-permute-start | bytes 589832 | tf_op jit(solution)/shard_map/ppermute | solution.py:462
  95.0 1.9 collective-permute-start.5
  99.3 13.2 %collective-permute-done.4 = f16[3,128,256]{2,1,0:T(8,128)(2,1)S(1)} collective-permute-done((f16[3,128,256]{2,1,0:T(8,128)(2,1)S(1)}, f16[3,128,256]{2,1,0:T(8,128)(2,1)S(1)}, u32[]{:S(2)}, u32[]{:S(2)}) %collective-permute-start.4) | collective-permute-done | bytes 196640 | tf_op jit(solution)/shard_map/ppermute | solution.py:462
  115.2 1.5 collective-permute-start.11
  118.6 2.9 %gather_fusion = bf16[8,32,8,256]{3,2,1,0:T(8,128)(2,1)} fusion(bf16[32,8,8,256]{3,1,2,0:T(8,128)(2,1)} %copy.18, s32[1024]{0:T(1024)S(1)} %pad_clamp_fusion), kind=kCustom, calls=%fused_computation | custom fusion | bytes 2097184 | tf_op jit(solution)/shard_map/gather | solution.py:512
  125.6 6.5 %shard_map.99 = (f32[4,32,24,128]{3,2,1,0:T(8,128)S(1)}, f32[4,32,24,128]{3,2,1,0:T(8,128)S(1)}) custom-call(s32[256]{0:T(256)S(1)} %get-tuple-element.87.refs_0_.a_ref, s32[256]{0:T(256)S(1)} %get-tuple-element.111.refs_1_.b_ref, f32[3,128,256]{2,1,0:T(8,128)S(1)} %convert_element_type.229.refs_2_, f32[3,128,256]{2,1,0:T(8,128)S(1)} %convert_element_type.230.refs_3_, ...), custom_call_target="tpu_custom_call" | custom-call | tf_op jit(solution)/shard_map/pallas_call | solution.py:139
  135.7 1.5 collective-permute-start.14
  137.2 1.5 collective-permute-start.15
  139.7 3.9 %collective-permute-done.14 = f16[32,24,128]{2,1,0:T(8,128)(2,1)S(1)} collective-permute-done((f16[32,24,128]{2,1,0:T(8,128)(2,1)S(1)}, f16[32,24,128]{2,1,0:T(8,128)(2,1)S(1)}, u32[]{:S(2)}, u32[]{:S(2)}) %collective-permute-start.14) | collective-permute-done | bytes 196640 | tf_op jit(solution)/shard_map/ppermute | solution.py:459
  143.6 3.9 %collective-permute-done.15 = f16[32,24,128]{2,1,0:T(8,128)(2,1)S(1)} collective-permute-done((f16[32,24,128]{2,1,0:T(8,128)(2,1)S(1)}, f16[32,24,128]{2,1,0:T(8,128)(2,1)S(1)}, u32[]{:S(2)}, u32[]{:S(2)}) %collective-permute-start.15) | collective-permute-done | bytes 196640 | tf_op jit(solution)/shard_map/ppermute | solution.py:459
  151.3 1.5 collective-permute-start.19
  153.9 3.0 %collective-permute-done.17.refs_1_ = bf16[32,24,128]{2,1,0:T(8,128)(2,1)S(1)} collective-permute-done((bf16[32,24,128]{2,1,0:T(8,128)(2,1)S(1)}, bf16[32,24,128]{2,1,0:T(8,128)(2,1)S(1)}, u32[]{:S(2)}, u32[]{:S(2)}) %collective-permute-start.17) | collective-permute-done | bytes 196640 | tf_op jit(solution)/shard_map/ppermute | solution.py:459
  156.9 3.1 %collective-permute-done.18.refs_2_ = bf16[32,24,128]{2,1,0:T(8,128)(2,1)S(1)} collective-permute-done((bf16[32,24,128]{2,1,0:T(8,128)(2,1)S(1)}, bf16[32,24,128]{2,1,0:T(8,128)(2,1)S(1)}, u32[]{:S(2)}, u32[]{:S(2)}) %collective-permute-start.18) | collective-permute-done | bytes 196640 | tf_op jit(solution)/shard_map/ppermute | solution.py:459
  160.5 1.6 collective-permute-start.21
  162.1 1.4 collective-permute-start.22
  163.5 6.2 %collective-permute-done.20.refs_1_ = bf16[32,40,128]{2,1,0:T(8,128)(2,1)S(1)} collective-permute-done((bf16[32,40,128]{2,1,0:T(8,128)(2,1)S(1)}, bf16[32,40,128]{2,1,0:T(8,128)(2,1)S(1)}, u32[]{:S(2)}, u32[]{:S(2)}) %collective-permute-start.20) | collective-permute-done | bytes 327712 | tf_op jit(solution)/shard_map/ppermute | solution.py:459
  169.7 4.5 %collective-permute-done.21.refs_2_ = bf16[32,40,128]{2,1,0:T(8,128)(2,1)S(1)} collective-permute-done((bf16[32,40,128]{2,1,0:T(8,128)(2,1)S(1)}, bf16[32,40,128]{2,1,0:T(8,128)(2,1)S(1)}, u32[]{:S(2)}, u32[]{:S(2)}) %collective-permute-start.21) | collective-permute-done | bytes 327712 | tf_op jit(solution)/shard_map/ppermute | solution.py:459
  175.2 3.4 %collective-permute-done.27.refs_4_ = bf16[4,32,24,128]{3,2,1,0:T(8,128)(2,1)S(1)} collective-permute-done((bf16[4,32,24,128]{3,2,1,0:T(8,128)(2,1)S(1)}, bf16[4,32,24,128]{3,2,1,0:T(8,128)(2,1)S(1)}, u32[]{:S(2)}, u32[]{:S(2)}) %collective-permute-start.27) | collective-permute-done | bytes 786464 | tf_op jit(solution)/shard_map/ppermute | solution.py:459
  178.6 6.1 %shard_map.101 = (bf16[3,128,256]{2,1,0:T(8,128)(2,1)S(1)}, bf16[3,128,256]{2,1,0:T(8,128)(2,1)S(1)}, bf16[3,128,256]{2,1,0:T(8,128)(2,1)S(1)}, bf16[3,128,256]{2,1,0:T(8,128)(2,1)S(1)}) custom-call(s32[256]{0:T(256)S(1)} %get-tuple-element.87.refs_0_.a_ref, s32[256]{0:T(256)S(1)} %get-tuple-element.111.refs_1_.b_ref, ...), custom_call_target="tpu_custom_call" | custom-call | tf_op jit(solution)/shard_map/pallas_call | solution.py:139
  185.1 7.6 %shard_map.100 = (bf16[5,128,256]{2,1,0:T(8,128)(2,1)S(1)}, bf16[5,128,256]{2,1,0:T(8,128)(2,1)S(1)}, bf16[5,128,256]{2,1,0:T(8,128)(2,1)S(1)}, bf16[5,128,256]{2,1,0:T(8,128)(2,1)S(1)}) custom-call(s32[256]{0:T(256)S(1)} %get-tuple-element.87.refs_0_.a_ref, s32[256]{0:T(256)S(1)} %get-tuple-element.111.refs_1_.b_ref, ...), custom_call_target="tpu_custom_call" | custom-call | tf_op jit(solution)/shard_map/pallas_call | solution.py:139
  193.7 2.5 collective-permute-start.25
  196.2 1.5 collective-permute-start.29
  197.8 2.8 %collective-permute-start.30 = (bf16[3,128,256]{2,1,0:T(8,128)(2,1)S(1)}, bf16[3,128,256]{2,1,0:T(8,128)(2,1)S(1)}, u32[]{:S(2)}, u32[]{:S(2)}) collective-permute-start(bf16[3,128,256]{2,1,0:T(8,128)(2,1)S(1)} %get-tuple-element.72), channel_id=1, source_target_pairs={{0,1},{1,2},{2,3},{3,0},{4,5},{5,6},{6,7},{7,4},{8,9},{9,10},{10,1... | collective-permute-start | bytes 589832 | tf_op jit(solution)/shard_map/ppermute | solution.py:462
  200.6 36.8 %collective-permute-done.29.refs_2_ = bf16[3,128,256]{2,1,0:T(8,128)(2,1)S(1)} collective-permute-done((bf16[3,128,256]{2,1,0:T(8,128)(2,1)S(1)}, bf16[3,128,256]{2,1,0:T(8,128)(2,1)S(1)}, u32[]{:S(2)}, u32[]{:S(2)}) %collective-permute-start.29) | collective-permute-done | bytes 196640 | tf_op jit(solution)/shard_map/ppermute | solution.py:462
  237.4 1.8 shard_map.102.refs_4_
  239.3 3.3 %shard_map.103 = bf16[8,512,128]{2,1,0:T(8,128)(2,1)S(1)} custom-call(bf16[5,128,256]{2,1,0:T(8,128)(2,1)S(1)} %get-tuple-element.65.refs_0_, bf16[5,128,256]{2,1,0:T(8,128)(2,1)S(1)} %collective-permute-done.24.refs_1_, bf16[5,128,256]{2,1,0:T(8,128)(2,1)S(1)} %collective-permute-done.25.refs_2_, bf16[5,128,256]{2,1,0:T(8,128)(2,1)S(1)} %collective-permute-done.26.refs_3_, ...), custom_call_target="tpu_custom_call" | custom-call | tf_op jit(solution)/shard_map/pallas_call | solution.py:139
  243.5 5.5 %all-to-all-start.1 = ((bf16[8,512,128]{2,1,0:T(8,128)(2,1)}), bf16[8,512,128]{2,1,0:T(8,128)(2,1)}, u32[]{:S(2)}, u32[]{:S(2)}) async-start(bf16[8,512,128]{2,1,0:T(8,128)(2,1)} %copy-done.15), calls=%async_computation.1 | async-start | bytes 2097152 | tf_op jit(solution)/shard_map/all_to_all | solution.py:541
  256.9 1.7 convert_convert_fusion.spread_ref
  258.7 4.4 %all-to-all-done.1.grad_ref = bf16[8,512,128]{2,1,0:T(8,128)(2,1)} async-done(((bf16[8,512,128]{2,1,0:T(8,128)(2,1)}), bf16[8,512,128]{2,1,0:T(8,128)(2,1)}, u32[]{:S(2)}, u32[]{:S(2)}) %all-to-all-start.1) | async-done | bytes 1048608 | tf_op jit(solution)/shard_map/all_to_all | solution.py:541
  263.1 1.6 copy-done.14
  264.6 2.5 shard_map.104
  267.2 3.8 %collective-permute-start.32 = (f32[8,512]{1,0:T(8,128)S(1)}, f32[8,512]{1,0:T(8,128)S(1)}, u32[]{:S(2)}, u32[]{:S(2)}) collective-permute-start(f32[8,512]{1,0:T(8,128)S(1)} %get-tuple-element.75), channel_id=1, source_target_pairs={{0,3},{1,0},{2,1},{3,2},{4,7},{5,4},{6,5},{7,6},{8,11},{9,8},{10,9... | collective-permute-start | bytes 49160 | tf_op jit(solution)/shard_map/ppermute | solution.py:462
  272.8 7.2 %haar.1 = f32[512,1024]{1,0:T(8,128)} custom-call(f32[512,1024]{1,0:T(8,128)S(1)} %get-tuple-element.73.refs_0_, f32[8,512]{1,0:T(8,128)S(1)} %collective-permute-done.31.refs_1_, f32[8,512]{1,0:T(8,128)S(1)} %collective-permute-done.32.refs_2_, f32[4,1152]{1,0:T(4,128)S(1)} %pad_maximum_fusion.6.refs_3_), custom_call_target="tpu_custom_call" | custom-call | tf_op jit(solution)/shard_map/haar/pallas_call | solution.py:425
  (165 shorter events, 39.2 us)
Async XLA Ops:
  0.6 134.4 %copy-start = (bf16[32,64,256]{2,1,0:T(8,128)(2,1)S(1)}, bf16[32,64,256]{2,1,0:T(8,128)(2,1)}, u32[]{:S(2)}) copy-start(bf16[32,64,256]{2,1,0:T(8,128)(2,1)} %param.9) | copy-start | bytes 3145732
  5.0 5.7 %copy-start.29 = (s32[32]{0:T(128)S(1)}, s32[32]{0:T(128)}, u32[]{:S(2)}) copy-start(s32[32]{0:T(128)} %param.13) | copy-start | bytes 388
  5.0 5.7 %copy-start.30 = (s32[32,1]{0,1:T(1,128)S(1)}, s32[32,1]{0,1:T(1,128)}, u32[]{:S(2)}) copy-start(s32[32,1]{0,1:T(1,128)} %param.12) | copy-start | bytes 388
  6.1 18.2 %all-to-all-start = ((f16[8,512,128]{2,1,0:T(8,128)(2,1)}), f16[8,512,128]{2,1,0:T(8,128)(2,1)}, u32[]{:S(2)}, u32[]{:S(2)}) async-start(f16[8,512,128]{2,1,0:T(8,128)(2,1)} %convert_element_type.195), calls=%async_computation | async-start | bytes 2097152 | tf_op jit(solution)/shard_map/all_to_all | solution.py:477
  31.1 1.2 collective-permute-start
  32.3 3.6 %collective-permute-start.1 = (s32[2,64]{1,0:T(2,128)S(1)}, s32[2,64]{1,0:T(2,128)S(1)}, u32[]{:S(2)}, u32[]{:S(2)}) collective-permute-start(s32[2,64]{1,0:T(2,128)S(1)} %pad_add_fusion.2), channel_id=1, source_target_pairs={{0,8},{4,12},{8,0},{12,4},{16,24},{20,28},{24,16},{28,20},{1,9},{5... | collective-permute-start | bytes 1544 | tf_op jit(solution)/shard_map/ppermute | solution.py:459
  35.9 20.8 %collective-permute-start.2 = (s32[2,128]{1,0:T(2,128)S(1)}, s32[2,128]{1,0:T(2,128)S(1)}, u32[]{:S(2)}, u32[]{:S(2)}) collective-permute-start(s32[2,128]{1,0:T(2,128)S(1)} %pad_add_fusion.3), channel_id=1, source_target_pairs={{0,16},{4,20},{8,24},{12,28},{16,0},{20,4},{24,8},{28,12},{1,17},{... | collective-permute-start | bytes 3080 | tf_op jit(solution)/shard_map/ppermute | solution.py:459
  51.2 12.2 %collective-permute-start.6 = (f16[5,128,256]{2,1,0:T(8,128)(2,1)S(1)}, f16[5,128,256]{2,1,0:T(8,128)(2,1)S(1)}, u32[]{:S(2)}, u32[]{:S(2)}) collective-permute-start(f16[5,128,256]{2,1,0:T(8,128)(2,1)S(1)} %convert_element_type.206), channel_id=1, source_target_pairs={{0,3},{1,0},{2,1},{3,2},{4,7},{5,4},{6,5},{7,6},{8,11},{9,8},{10,9... | collective-permute-start | bytes 983048 | tf_op jit(solution)/shard_map/ppermute | solution.py:462
  55.3 26.8 %collective-permute-start.7 = (f16[5,128,256]{2,1,0:T(8,128)(2,1)S(1)}, f16[5,128,256]{2,1,0:T(8,128)(2,1)S(1)}, u32[]{:S(2)}, u32[]{:S(2)}) collective-permute-start(f16[5,128,256]{2,1,0:T(8,128)(2,1)S(1)} %convert_element_type.207), channel_id=1, source_target_pairs={{0,2},{1,3},{2,0},{3,1},{4,6},{5,7},{6,4},{7,5},{8,10},{9,11},{10,... | collective-permute-start | bytes 983048 | tf_op jit(solution)/shard_map/ppermute | solution.py:462
  55.5 26.6 %collective-permute-start.8 = (f16[5,128,256]{2,1,0:T(8,128)(2,1)S(1)}, f16[5,128,256]{2,1,0:T(8,128)(2,1)S(1)}, u32[]{:S(2)}, u32[]{:S(2)}) collective-permute-start(f16[5,128,256]{2,1,0:T(8,128)(2,1)S(1)} %convert_element_type.208), channel_id=1, source_target_pairs={{0,1},{1,2},{2,3},{3,0},{4,5},{5,6},{6,7},{7,4},{8,9},{9,10},{10,1... | collective-permute-start | bytes 983048 | tf_op jit(solution)/shard_map/ppermute | solution.py:462
  57.6 24.8 %copy-start.3 = (bf16[1024,1024]{1,0:T(8,128)(2,1)S(1)}, bf16[1024,1024]{1,0:T(8,128)(2,1)}, u32[]{:S(2)}) copy-start(bf16[1024,1024]{1,0:T(8,128)(2,1)} %get-tuple-element.97.refs_7_) | copy-start | bytes 6291460
  57.6 24.8 %copy-start.4 = (bf16[1024,1024]{1,0:T(8,128)(2,1)S(1)}, bf16[1024,1024]{1,0:T(8,128)(2,1)}, u32[]{:S(2)}) copy-start(bf16[1024,1024]{1,0:T(8,128)(2,1)} %get-tuple-element.99.refs_6_) | copy-start | bytes 6291460
  57.7 33.3 %copy-start.16 = (f32[256,128]{1,0:T(8,128)}, f32[256,128]{1,0:T(8,128)S(1)}, u32[]{:S(2)}) copy-start(f32[256,128]{1,0:T(8,128)S(1)} %pad_maximum_fusion.5.refs_9_.refs_8_) | copy-start | bytes 393220
  91.2 5.7 %collective-permute-start.9 = (f16[4,32,40,128]{3,2,1,0:T(8,128)(2,1)S(1)}, f16[4,32,40,128]{3,2,1,0:T(8,128)(2,1)S(1)}, u32[]{:S(2)}, u32[]{:S(2)}) collective-permute-start(f16[4,32,40,128]{3,2,1,0:T(8,128)(2,1)S(1)} %convert_element_type.217), channel_id=1, source_target_pairs={{0,4},{4,0},{8,12},{12,8},{16,20},{20,16},{24,28},{28,24},{1,5},{5... | collective-permute-start | bytes 3932168 | tf_op jit(solution)/shard_map/ppermute | solution.py:459
  92.0 7.3 %collective-permute-start.3 = (f16[3,128,256]{2,1,0:T(8,128)(2,1)S(1)}, f16[3,128,256]{2,1,0:T(8,128)(2,1)}, u32[]{:S(2)}, u32[]{:S(2)}) collective-permute-start(f16[3,128,256]{2,1,0:T(8,128)(2,1)S(1)} %copy-done.23), channel_id=1, source_target_pairs={{0,3},{1,0},{2,1},{3,2},{4,7},{5,4},{6,5},{7,6},{8,11},{9,8},{10,9... | collective-permute-start | bytes 589832 | tf_op jit(solution)/shard_map/ppermute | solution.py:462
  92.1 20.4 %collective-permute-start.4 = (f16[3,128,256]{2,1,0:T(8,128)(2,1)S(1)}, f16[3,128,256]{2,1,0:T(8,128)(2,1)S(1)}, u32[]{:S(2)}, u32[]{:S(2)}) collective-permute-start(f16[3,128,256]{2,1,0:T(8,128)(2,1)S(1)} %copy-done.22), channel_id=1, source_target_pairs={{0,2},{1,3},{2,0},{3,1},{4,6},{5,7},{6,4},{7,5},{8,10},{9,11},{10,... | collective-permute-start | bytes 589832 | tf_op jit(solution)/shard_map/ppermute | solution.py:462
  95.0 17.5 %collective-permute-start.5 = (f16[3,128,256]{2,1,0:T(8,128)(2,1)S(1)}, f16[3,128,256]{2,1,0:T(8,128)(2,1)S(1)}, u32[]{:S(2)}, u32[]{:S(2)}) collective-permute-start(f16[3,128,256]{2,1,0:T(8,128)(2,1)S(1)} %copy-done.21), channel_id=1, source_target_pairs={{0,1},{1,2},{2,3},{3,0},{4,5},{5,6},{6,7},{7,4},{8,9},{9,10},{10,1... | collective-permute-start | bytes 589832 | tf_op jit(solution)/shard_map/ppermute | solution.py:462
  97.3 20.0 %copy-start.28 = (s32[8]{0:T(128)S(1)}, s32[8]{0:T(128)}, u32[]{:S(2)}) copy-start(s32[8]{0:T(128)} %constant.227) | copy-start | bytes 100
  97.3 20.0 %copy-start.20 = (bf16[32,64,256]{2,1,0:T(8,128)(2,1)S(1)}, bf16[32,64,256]{2,1,0:T(8,128)(2,1)}, u32[]{:S(2)}) copy-start(bf16[32,64,256]{2,1,0:T(8,128)(2,1)} %param.10) | copy-start | bytes 3145732
  113.8 19.7 %collective-permute-start.10 = (f16[32,40,128]{2,1,0:T(8,128)(2,1)}, f16[32,40,128]{2,1,0:T(8,128)(2,1)}, u32[]{:S(2)}, u32[]{:S(2)}) collective-permute-start(f16[32,40,128]{2,1,0:T(8,128)(2,1)} %get-tuple-element.55), channel_id=1, source_target_pairs={{0,8},{4,12},{8,0},{12,4},{16,24},{20,28},{24,16},{28,20},{1,9},{5... | collective-permute-start | bytes 983048 | tf_op jit(solution)/shard_map/ppermute | solution.py:459
  115.2 18.4 %collective-permute-start.11 = (f16[32,40,128]{2,1,0:T(8,128)(2,1)}, f16[32,40,128]{2,1,0:T(8,128)(2,1)}, u32[]{:S(2)}, u32[]{:S(2)}) collective-permute-start(f16[32,40,128]{2,1,0:T(8,128)(2,1)} %get-tuple-element.56), channel_id=1, source_target_pairs={{0,16},{4,20},{8,24},{12,28},{16,0},{20,4},{24,8},{28,12},{1,17},{... | collective-permute-start | bytes 983048 | tf_op jit(solution)/shard_map/ppermute | solution.py:459
  116.7 16.9 %collective-permute-start.12 = (f16[32,40,128]{2,1,0:T(8,128)(2,1)}, f16[32,40,128]{2,1,0:T(8,128)(2,1)}, u32[]{:S(2)}, u32[]{:S(2)}) collective-permute-start(f16[32,40,128]{2,1,0:T(8,128)(2,1)} %get-tuple-element.57), channel_id=1, source_target_pairs={{0,24},{4,28},{8,16},{12,20},{16,8},{20,12},{24,0},{28,4},{1,25},{... | collective-permute-start | bytes 983048 | tf_op jit(solution)/shard_map/ppermute | solution.py:459
  132.2 3.1 %collective-permute-start.13 = (f16[4,32,24,128]{3,2,1,0:T(8,128)(2,1)S(1)}, f16[4,32,24,128]{3,2,1,0:T(8,128)(2,1)S(1)}, u32[]{:S(2)}, u32[]{:S(2)}) collective-permute-start(f16[4,32,24,128]{3,2,1,0:T(8,128)(2,1)S(1)} %convert_element_type.233), channel_id=1, source_target_pairs={{0,4},{4,0},{8,12},{12,8},{16,20},{20,16},{24,28},{28,24},{1,5},{5... | collective-permute-start | bytes 2359304 | tf_op jit(solution)/shard_map/ppermute | solution.py:459
  135.7 7.8 %collective-permute-start.14 = (f16[32,24,128]{2,1,0:T(8,128)(2,1)S(1)}, f16[32,24,128]{2,1,0:T(8,128)(2,1)S(1)}, u32[]{:S(2)}, u32[]{:S(2)}) collective-permute-start(f16[32,24,128]{2,1,0:T(8,128)(2,1)S(1)} %get-tuple-element.91), channel_id=1, source_target_pairs={{0,8},{4,12},{8,0},{12,4},{16,24},{20,28},{24,16},{28,20},{1,9},{5... | collective-permute-start | bytes 589832 | tf_op jit(solution)/shard_map/ppermute | solution.py:459
  137.2 10.2 %collective-permute-start.15 = (f16[32,24,128]{2,1,0:T(8,128)(2,1)S(1)}, f16[32,24,128]{2,1,0:T(8,128)(2,1)S(1)}, u32[]{:S(2)}, u32[]{:S(2)}) collective-permute-start(f16[32,24,128]{2,1,0:T(8,128)(2,1)S(1)} %get-tuple-element.93), channel_id=1, source_target_pairs={{0,16},{4,20},{8,24},{12,28},{16,0},{20,4},{24,8},{28,12},{1,17},{... | collective-permute-start | bytes 589832 | tf_op jit(solution)/shard_map/ppermute | solution.py:459
  138.7 8.7 %collective-permute-start.16 = (f16[32,24,128]{2,1,0:T(8,128)(2,1)S(1)}, f16[32,24,128]{2,1,0:T(8,128)(2,1)S(1)}, u32[]{:S(2)}, u32[]{:S(2)}) collective-permute-start(f16[32,24,128]{2,1,0:T(8,128)(2,1)S(1)} %get-tuple-element.92), channel_id=1, source_target_pairs={{0,24},{4,28},{8,16},{12,20},{16,8},{20,12},{24,0},{28,4},{1,25},{... | collective-permute-start | bytes 589832 | tf_op jit(solution)/shard_map/ppermute | solution.py:459
  149.3 7.6 %collective-permute-start.17 = (bf16[32,24,128]{2,1,0:T(8,128)(2,1)S(1)}, bf16[32,24,128]{2,1,0:T(8,128)(2,1)S(1)}, u32[]{:S(2)}, u32[]{:S(2)}) collective-permute-start(bf16[32,24,128]{2,1,0:T(8,128)(2,1)S(1)} %pad_maximum_fusion.3.refs_0_), channel_id=1, source_target_pairs={{0,8},{4,12},{8,0},{12,4},{16,24},{20,28},{24,16},{28,20},{1,9},{5... | collective-permute-start | bytes 589832 | tf_op jit(solution)/shard_map/ppermute | solution.py:459
  150.6 9.5 %collective-permute-start.18 = (bf16[32,24,128]{2,1,0:T(8,128)(2,1)S(1)}, bf16[32,24,128]{2,1,0:T(8,128)(2,1)S(1)}, u32[]{:S(2)}, u32[]{:S(2)}) collective-permute-start(bf16[32,24,128]{2,1,0:T(8,128)(2,1)S(1)} %pad_maximum_fusion.3.refs_0_), channel_id=1, source_target_pairs={{0,16},{4,20},{8,24},{12,28},{16,0},{20,4},{24,8},{28,12},{1,17},{... | collective-permute-start | bytes 589832 | tf_op jit(solution)/shard_map/ppermute | solution.py:459
  151.3 8.7 %collective-permute-start.19 = (bf16[32,24,128]{2,1,0:T(8,128)(2,1)S(1)}, bf16[32,24,128]{2,1,0:T(8,128)(2,1)S(1)}, u32[]{:S(2)}, u32[]{:S(2)}) collective-permute-start(bf16[32,24,128]{2,1,0:T(8,128)(2,1)S(1)} %pad_maximum_fusion.3.refs_0_), channel_id=1, source_target_pairs={{0,24},{4,28},{8,16},{12,20},{16,8},{20,12},{24,0},{28,4},{1,25},{... | collective-permute-start | bytes 589832 | tf_op jit(solution)/shard_map/ppermute | solution.py:459
  160.0 9.7 %collective-permute-start.20 = (bf16[32,40,128]{2,1,0:T(8,128)(2,1)S(1)}, bf16[32,40,128]{2,1,0:T(8,128)(2,1)S(1)}, u32[]{:S(2)}, u32[]{:S(2)}) collective-permute-start(bf16[32,40,128]{2,1,0:T(8,128)(2,1)S(1)} %pad_maximum_fusion.2.refs_0_), channel_id=1, source_target_pairs={{0,8},{4,12},{8,0},{12,4},{16,24},{20,28},{24,16},{28,20},{1,9},{5... | collective-permute-start | bytes 983048 | tf_op jit(solution)/shard_map/ppermute | solution.py:459
  160.5 13.7 %collective-permute-start.21 = (bf16[32,40,128]{2,1,0:T(8,128)(2,1)S(1)}, bf16[32,40,128]{2,1,0:T(8,128)(2,1)S(1)}, u32[]{:S(2)}, u32[]{:S(2)}) collective-permute-start(bf16[32,40,128]{2,1,0:T(8,128)(2,1)S(1)} %pad_maximum_fusion.2.refs_0_), channel_id=1, source_target_pairs={{0,16},{4,20},{8,24},{12,28},{16,0},{20,4},{24,8},{28,12},{1,17},{... | collective-permute-start | bytes 983048 | tf_op jit(solution)/shard_map/ppermute | solution.py:459
  162.1 12.1 %collective-permute-start.22 = (bf16[32,40,128]{2,1,0:T(8,128)(2,1)S(1)}, bf16[32,40,128]{2,1,0:T(8,128)(2,1)S(1)}, u32[]{:S(2)}, u32[]{:S(2)}) collective-permute-start(bf16[32,40,128]{2,1,0:T(8,128)(2,1)S(1)} %pad_maximum_fusion.2.refs_0_), channel_id=1, source_target_pairs={{0,24},{4,28},{8,16},{12,20},{16,8},{20,12},{24,0},{28,4},{1,25},{... | collective-permute-start | bytes 983048 | tf_op jit(solution)/shard_map/ppermute | solution.py:459
  174.2 4.4 %copy-start.2 = (bf16[1024,1024]{1,0:T(8,128)(2,1)S(1)}, bf16[1024,1024]{1,0:T(8,128)(2,1)}, u32[]{:S(2)}) copy-start(bf16[1024,1024]{1,0:T(8,128)(2,1)} %get-tuple-element.98.refs_5_) | copy-start | bytes 6291460
  174.4 10.7 %collective-permute-start.23 = (bf16[4,32,40,128]{3,2,1,0:T(8,128)(2,1)S(1)}, bf16[4,32,40,128]{3,2,1,0:T(8,128)(2,1)S(1)}, u32[]{:S(2)}, u32[]{:S(2)}) collective-permute-start(bf16[4,32,40,128]{3,2,1,0:T(8,128)(2,1)S(1)} %pad_maximum_fusion), channel_id=1, source_target_pairs={{0,4},{4,0},{8,12},{12,8},{16,20},{20,16},{24,28},{28,24},{1,5},{5... | collective-permute-start | bytes 3932168 | tf_op jit(solution)/shard_map/ppermute | solution.py:459
  174.6 4.0 %collective-permute-start.27 = (bf16[4,32,24,128]{3,2,1,0:T(8,128)(2,1)S(1)}, bf16[4,32,24,128]{3,2,1,0:T(8,128)(2,1)S(1)}, u32[]{:S(2)}, u32[]{:S(2)}) collective-permute-start(bf16[4,32,24,128]{3,2,1,0:T(8,128)(2,1)S(1)} %pad_maximum_fusion.1), channel_id=1, source_target_pairs={{0,4},{4,0},{8,12},{12,8},{16,20},{20,16},{24,28},{28,24},{1,5},{5... | collective-permute-start | bytes 2359304 | tf_op jit(solution)/shard_map/ppermute | solution.py:459
  184.8 52.6 %copy-start.10 = (bf16[1024,512]{1,0:T(8,128)(2,1)S(1)}, bf16[1024,512]{1,0:T(8,128)(2,1)}, u32[]{:S(2)}) copy-start(bf16[1024,512]{1,0:T(8,128)(2,1)} %get-tuple-element.100.refs_5_.refs_6_) | copy-start | bytes 3145732
  184.8 52.6 %copy-start.11 = (bf16[1024,512]{1,0:T(8,128)(2,1)S(1)}, bf16[1024,512]{1,0:T(8,128)(2,1)}, u32[]{:S(2)}) copy-start(bf16[1024,512]{1,0:T(8,128)(2,1)} %get-tuple-element.101.refs_4_.refs_5_) | copy-start | bytes 3145732
  184.8 13.0 %collective-permute-start.28 = (bf16[3,128,256]{2,1,0:T(8,128)(2,1)S(1)}, bf16[3,128,256]{2,1,0:T(8,128)(2,1)S(1)}, u32[]{:S(2)}, u32[]{:S(2)}) collective-permute-start(bf16[3,128,256]{2,1,0:T(8,128)(2,1)S(1)} %get-tuple-element.70), channel_id=1, source_target_pairs={{0,3},{1,0},{2,1},{3,2},{4,7},{5,4},{6,5},{7,6},{8,11},{9,8},{10,9... | collective-permute-start | bytes 589832 | tf_op jit(solution)/shard_map/ppermute | solution.py:462
  192.7 46.5 %collective-permute-start.24 = (bf16[5,128,256]{2,1,0:T(8,128)(2,1)S(1)}, bf16[5,128,256]{2,1,0:T(8,128)(2,1)S(1)}, u32[]{:S(2)}, u32[]{:S(2)}) collective-permute-start(bf16[5,128,256]{2,1,0:T(8,128)(2,1)S(1)} %get-tuple-element.66), channel_id=1, source_target_pairs={{0,3},{1,0},{2,1},{3,2},{4,7},{5,4},{6,5},{7,6},{8,11},{9,8},{10,9... | collective-permute-start | bytes 983048 | tf_op jit(solution)/shard_map/ppermute | solution.py:462
  193.7 45.5 %collective-permute-start.25 = (bf16[5,128,256]{2,1,0:T(8,128)(2,1)S(1)}, bf16[5,128,256]{2,1,0:T(8,128)(2,1)S(1)}, u32[]{:S(2)}, u32[]{:S(2)}) collective-permute-start(bf16[5,128,256]{2,1,0:T(8,128)(2,1)S(1)} %get-tuple-element.67), channel_id=1, source_target_pairs={{0,2},{1,3},{2,0},{3,1},{4,6},{5,7},{6,4},{7,5},{8,10},{9,11},{10,... | collective-permute-start | bytes 983048 | tf_op jit(solution)/shard_map/ppermute | solution.py:462
  196.2 43.0 %collective-permute-start.26 = (bf16[5,128,256]{2,1,0:T(8,128)(2,1)S(1)}, bf16[5,128,256]{2,1,0:T(8,128)(2,1)S(1)}, u32[]{:S(2)}, u32[]{:S(2)}) collective-permute-start(bf16[5,128,256]{2,1,0:T(8,128)(2,1)S(1)} %get-tuple-element.68), channel_id=1, source_target_pairs={{0,1},{1,2},{2,3},{3,0},{4,5},{5,6},{6,7},{7,4},{8,9},{9,10},{10,1... | collective-permute-start | bytes 983048 | tf_op jit(solution)/shard_map/ppermute | solution.py:462
  196.2 41.1 %collective-permute-start.29 = (bf16[3,128,256]{2,1,0:T(8,128)(2,1)S(1)}, bf16[3,128,256]{2,1,0:T(8,128)(2,1)S(1)}, u32[]{:S(2)}, u32[]{:S(2)}) collective-permute-start(bf16[3,128,256]{2,1,0:T(8,128)(2,1)S(1)} %get-tuple-element.71), channel_id=1, source_target_pairs={{0,2},{1,3},{2,0},{3,1},{4,6},{5,7},{6,4},{7,5},{8,10},{9,11},{10,... | collective-permute-start | bytes 589832 | tf_op jit(solution)/shard_map/ppermute | solution.py:462
  197.8 39.6 %collective-permute-start.30 = (bf16[3,128,256]{2,1,0:T(8,128)(2,1)S(1)}, bf16[3,128,256]{2,1,0:T(8,128)(2,1)S(1)}, u32[]{:S(2)}, u32[]{:S(2)}) collective-permute-start(bf16[3,128,256]{2,1,0:T(8,128)(2,1)S(1)} %get-tuple-element.72), channel_id=1, source_target_pairs={{0,1},{1,2},{2,3},{3,0},{4,5},{5,6},{6,7},{7,4},{8,9},{9,10},{10,1... | collective-permute-start | bytes 589832 | tf_op jit(solution)/shard_map/ppermute | solution.py:462
  239.2 9.8 %copy-start.27 = (f32[4]{0:T(128)S(1)}, f32[4]{0:T(128)}, u32[]{:S(2)}) copy-start(f32[4]{0:T(128)} %param.14) | copy-start | bytes 52
  243.5 19.5 %copy-start.13 = (f32[512,1024]{1,0:T(8,128)S(1)}, f32[512,1024]{1,0:T(8,128)}, u32[]{:S(2)}) copy-start(f32[512,1024]{1,0:T(8,128)} %image_ref.3) | copy-start | bytes 6291460
  243.5 19.5 %all-to-all-start.1 = ((bf16[8,512,128]{2,1,0:T(8,128)(2,1)}), bf16[8,512,128]{2,1,0:T(8,128)(2,1)}, u32[]{:S(2)}, u32[]{:S(2)}) async-start(bf16[8,512,128]{2,1,0:T(8,128)(2,1)} %copy-done.15), calls=%async_computation.1 | async-start | bytes 2097152 | tf_op jit(solution)/shard_map/all_to_all | solution.py:541
  267.2 5.6 %collective-permute-start.31 = (f32[8,512]{1,0:T(8,128)S(1)}, f32[8,512]{1,0:T(8,128)S(1)}, u32[]{:S(2)}, u32[]{:S(2)}) collective-permute-start(f32[8,512]{1,0:T(8,128)S(1)} %get-tuple-element.74), channel_id=1, source_target_pairs={{0,1},{1,2},{2,3},{3,0},{4,5},{5,6},{6,7},{7,4},{8,9},{9,10},{10,1... | collective-permute-start | bytes 49160 | tf_op jit(solution)/shard_map/ppermute | solution.py:462
  267.2 5.5 %collective-permute-start.32 = (f32[8,512]{1,0:T(8,128)S(1)}, f32[8,512]{1,0:T(8,128)S(1)}, u32[]{:S(2)}, u32[]{:S(2)}) collective-permute-start(f32[8,512]{1,0:T(8,128)S(1)} %get-tuple-element.75), channel_id=1, source_target_pairs={{0,3},{1,0},{2,1},{3,2},{4,7},{5,4},{6,5},{7,6},{8,11},{9,8},{10,9... | collective-permute-start | bytes 49160 | tf_op jit(solution)/shard_map/ppermute | solution.py:462
  (18 other events, 33.1 us)
where the time goes:
time: 283 us; the launch traced here: 280 us
  waiting for transfers between devices  119 us (42%)
  Pallas kernels  51.3 us (18%)
  starting transfers between devices  49.2 us (17%)
  other arithmetic  31.3 us (11%)
  local copies, waits for them, and re-layouts  17.9 us (6%)
  between operations  8.62 us (3%)
  matrix products  3.11 us (1%)
    ppermute x14, waiting for transfers between devices, ahead(): return lax.ppermute(x, 'wav', [(i, (i + by) % wavs) for i in range(wavs)])  75.4 us
    pallas_call x10, Pallas kernels, call(): pl.pallas_call(kernel, in_specs=[pl.BlockSpec(memory_space=pltpu.SMEM)] *...  44.1 us
    ppermute x19, waiting for transfers between devices, flip(): return lax.ppermute(x, 'vis', [(i, i ^ mask) for i in range(vis)])  31.1 us
    ppermute x14, starting transfers between devices, ahead(): return lax.ppermute(x, 'wav', [(i, (i + by) % wavs) for i in range(wavs)])  22.3 us
    ppermute x19, starting transfers between devices, flip(): return lax.ppermute(x, 'vis', [(i, i ^ mask) for i in range(vis)])  17.1 us
    convert_element_type x2, other arithmetic, split(): return (high.astype(BF16), (x - high).astype(BF16))  15.1 us
    unnamed x63, local copies, waits for them, and re-layouts  11 us
    all_to_all x1, waiting for transfers between devices, shards_fast(): lax.all_to_all(x, 'vis', split_axis=0, concat_axis=0, tiled=True)  7.77 us
  transfers between devices with their start and end apart: 35, of which 16 were waited for; matrix products, arithmetic and copies ran while one was open for 12% of the time, Pallas kernels for 9%

commit v1 on v0

--- a/solution.py
+++ b/solution.py
@@ -146,7 +146,9 @@
     )(*args)
 
 
-def spread_kernel(image_ref, out_ref):
+def spread_kernel(image_ref, out_ref, first_ref, last_ref):
+    first_ref[...] = image_ref[:, :LANES].T[:HALO]
+    last_ref[...] = image_ref[:, image_ref.shape[1] - LANES :].T[LANES - HALO :]
     groups, _, m = out_ref.shape
     width = groups * m
     high = image_ref[...].astype(BF16)
@@ -341,12 +343,20 @@
 LANES = 128
 
 
-def step_kernel(image_ref, grad_ref, spread_ref, out_ref, first_ref, last_ref):
-    _, width = image_ref.shape
+def step_kernel(image_ref, grad_ref, spread_ref, out_ref):
     grad = jnp.concatenate([grad_ref[i] for i in range(grad_ref.shape[0])], 1)
     out_ref[...] = image_ref[...] - jnp.dot(grad, spread_ref[...], preferred_element_type=F32)
-    first_ref[...] = out_ref[:, :LANES].T[:HALO]
-    last_ref[...] = out_ref[:, width - LANES :].T[LANES - HALO :]
+
+
+def edge_kernel(grad_ref, first_ref, last_ref):
+    groups, _, m = grad_ref.shape
+    row = lax.broadcasted_iota(jnp.int32, (8, m), 0)
+    lane = lax.broadcasted_iota(jnp.int32, (8, m), 1)
+    pick = (lane == jnp.where(row == 0, 0, m - 1)).astype(F32).astype(BF16)
+    for v in range(groups):
+        both = lax.dot_general(pick, grad_ref[v], (((1,), (1,)), ((), ())), preferred_element_type=F32)
+        first_ref[v : v + 1, :] = both[0:1]
+        last_ref[v : v + 1, :] = both[1:2]
 
 
 def haar_kernel(field_ref, left_ref, right_ref, limit_ref, out_ref, edge_ref, *, bases):
@@ -452,7 +462,6 @@
     img = rows * vis
     m = cols // vis
     across = cols // PATCH
-    blocks = kernel_v.shape[0]
     part = rows // wavs
 
     def flip(x, mask):
@@ -473,8 +482,12 @@
             out.append(flip(parts[chip - 1], 2 * chip))
         return out
 
-    x = call(spread_kernel, [((vis, rows, m), F32)], [], image)[0].astype(F16)
-    x = lax.all_to_all(x, "vis", split_axis=0, concat_axis=0, tiled=True).astype(F32)
+    edge = ((HALO, rows), F32)
+    x, first_cols, last_cols = call(spread_kernel, [((vis, rows, m), F32), edge, edge], [], image)
+    x = x.astype(F16)
+    x = lax.all_to_all(x, "vis", split_axis=0, concat_axis=0, tiled=True)
+    x = x.astype(F32)
+    table, table_back = column_table(wavs, m, w, False), column_table(wavs, m, w, True)
 
     forward_table, twist = row_table(rows, w * part), twist_table(vis, rows)
     sent, spectra = [], []
@@ -488,11 +501,12 @@
     ids, _ = lax.optimization_barrier((ids, sent[1]))
     for mask in (1, 2, 4):
         ids = jnp.concatenate([ids, flip(ids, mask)], 1)
+    sky, _ = lax.optimization_barrier(((first_cols, last_cols), sent[1]))
+    sky_right, sky_left = ahead(sky[0], wavs - 1), ahead(sky[1], 1)
     owner, slot = ids[0], ids[1]
     a_block, b_block = slot // across, slot % across
     cos_k, sin_k = phases(owner, a_block, v, rows, img)
 
-    table = column_table(wavs, m, w, False)
     patches = []
     for half in (0, 1):
         y = []
@@ -508,8 +522,10 @@
             total = total + came.astype(F32)
         patches.append(total.astype(BF16))
 
-    order = jnp.asarray(ORDER)
-    side = kernel_u.reshape(blocks, 8, vis, -1)[:, :, order].transpose(0, 2, 1, 3).reshape(kernel_u.shape).astype(F32)
+    place = np.arange(PATCH)
+    chosen = (place % 8) * vis + np.asarray(ORDER)[place // 8]
+    pick = jnp.asarray(chosen[:, None] == place[None, :], BF16)
+    side = jnp.einsum("pb,nbt->npt", pick, kernel_u, preferred_element_type=F32)
     cut = 8 * len(HALVES[0])
     sides = [side[:, :cut], side[:, cut:]]
     model = 0.0
@@ -519,7 +535,6 @@
         model = model + jnp.stack([jnp.sum(part_re * side, 1), jnp.sum(part_im * side, 1)], 1)
     misfit = model - measured.astype(F32)
 
-    table_back = column_table(wavs, m, w, True)
     grads = {}
     for half in (1, 0):
         side = sides[half]
@@ -539,12 +554,12 @@
     first = call(rows_inverse_first, [((3, rows, m), F32)], [], *grads[1], *back_table, twist)
     grad = call(rows_inverse_last, [((vis, rows, m), BF16)], [], *grads[0], *first, *back_table, twist)[0]
     grad = lax.all_to_all(grad, "vis", split_axis=0, concat_axis=0, tiled=True)
-    edge = ((HALO, rows), F32)
     back = spread_matrix(vis, m).T.astype(BF16)
-    shifted, first_cols, last_cols = call(step_kernel, [((rows, cols), F32), edge, edge], [], image, grad, back)
-    right = ahead(first_cols, wavs - 1)
-    left = ahead(last_cols, 1)
-    return haar_mean(shifted, left, right, thresholds), misfit
+    grad_edges = call(edge_kernel, [edge, edge], [], grad)
+    right = ahead(grad_edges[0], wavs - 1)
+    left = ahead(grad_edges[1], 1)
+    shifted = call(step_kernel, [((rows, cols), F32)], [], image, grad, back)[0]
+    return haar_mean(shifted, sky_left - left, sky_right - right, thresholds), misfit
 
 
 def shards(image, kernel_v, kernel_u, measured, dest_owner, patch_slot, thresholds):

time: 283 us -> 270 us (0.954)
  local copies, waits for them, and re-layouts: 17.9 us -> 9.14 us
  other arithmetic: 31.3 us -> 26 us
    convert_element_type x8, other arithmetic: 4.18 us -> 0.32 us  [shards_fast(): y.append(part_y.astype(F32))]
    gather x1 -> x0, local copies, waits for them, and re-layouts: 2.92 us -> none  [shards_fast(): kernel_u.reshape(blocks, 8, vis, -1)[:, :, order].transpose(0, 2, 1, 3)]
    unnamed x63 -> x51, local copies, waits for them, and re-layouts: 11 us -> 8.13 us
    ppermute x14 -> x16, waiting for transfers between devices: 75.4 us -> 76.6 us  [ahead(): return lax.ppermute(x, 'wav', [(i, (i + by) % wavs) for i in range(wavs)])]
    ppermute x14 -> x16, starting transfers between devices: 22.3 us -> 22.5 us  [ahead(): return lax.ppermute(x, 'wav', [(i, (i + by) % wavs) for i in range(wavs)])]
    pallas_call x10 -> x11, Pallas kernels: 44.1 us -> 44 us  [call(): pl.pallas_call(kernel, in_specs=[pl.BlockSpec(memory_space=pltpu.SMEM)] *...]
  transfers between devices with their start and end apart: 35 -> 37, of which waited for: 16 -> 19; matrix products, arithmetic and copies ran while one was open for 12% -> 9% of each run, Pallas kernels for 9% -> 10%
where the time goes in v1:
time: 270 us; the launch traced here: 267 us
  waiting for transfers between devices  120 us (44%)
  Pallas kernels  51.3 us (19%)
  starting transfers between devices  48.2 us (18%)
  other arithmetic  26 us (10%)
  local copies, waits for them, and re-layouts  9.14 us (3%)
  between operations  8.98 us (3%)
  matrix products  3.49 us (1%)
    ppermute x16, waiting for transfers between devices, ahead(): return lax.ppermute(x, 'wav', [(i, (i + by) % wavs) for i in range(wavs)])  76.6 us
    pallas_call x11, Pallas kernels, call(): pl.pallas_call(kernel, in_specs=[pl.BlockSpec(memory_space=pltpu.SMEM)] *...  44 us
    ppermute x19, waiting for transfers between devices, flip(): return lax.ppermute(x, 'vis', [(i, i ^ mask) for i in range(vis)])  33.9 us
    ppermute x16, starting transfers between devices, ahead(): return lax.ppermute(x, 'wav', [(i, (i + by) % wavs) for i in range(wavs)])  22.5 us
    ppermute x19, starting transfers between devices, flip(): return lax.ppermute(x, 'vis', [(i, i ^ mask) for i in range(vis)])  17.1 us
    convert_element_type x2, other arithmetic, split(): return (high.astype(BF16), (x - high).astype(BF16))  15.1 us
    unnamed x51, local copies, waits for them, and re-layouts  8.13 us
    all_to_all x1, waiting for transfers between devices, shards_fast(): x = lax.all_to_all(x, 'vis', split_axis=0, concat_axis=0, tiled=True)  7.77 us
  transfers between devices with their start and end apart: 37, of which 19 were waited for; matrix products, arithmetic and copies ran while one was open for 9% of the time, Pallas kernels for 10%

profile of v1, /device:TPU:2, one launch (start us, length us, event | category | flops | bytes accessed | tf_op | source)
XLA Modules:
  0.0 267.1 jit_solution(8739043460670426671)
XLA Ops:
  0.7 1.7 copy-done.12
  2.3 2.6 shard_map.95
  6.1 4.3 %all-to-all-start = ((f16[8,512,128]{2,1,0:T(8,128)(2,1)}), f16[8,512,128]{2,1,0:T(8,128)(2,1)}, u32[]{:S(2)}, u32[]{:S(2)}) async-start(f16[8,512,128]{2,1,0:T(8,128)(2,1)} %convert_element_type.186), calls=%async_computation | async-start | bytes 2097152 | tf_op jit(solution)/shard_map/all_to_all | solution.py:488
  10.7 5.9 %fusion.13 = (bf16[1024,512]{1,0:T(8,128)(2,1)}, bf16[1024,512]{1,0:T(8,128)(2,1)}, bf16[1024,512]{1,0:T(8,128)(2,1)}, bf16[1024,512]{1,0:T(8,128)(2,1)}) fusion(s32[1024]{0:T(1024)S(1)} %get-tuple-element.125, s32[1024]{0:T(1024)S(1)} %get-tuple-element.124, s32[512]{0:T(512)S(1)} %add_and_fusion.1, s32[1024]{0:T(1024)S(1)} %get-tuple-element.123), kind=kLoop, calls=%fused_computation.36 | loop fusion | flops 29360128 | bytes 4208640 | tf_op jit(solution)/shard_map/convert_element_type | solution.py:78
  16.6 7.8 %all-to-all-done = f16[8,512,128]{2,1,0:T(8,128)(2,1)} async-done(((f16[8,512,128]{2,1,0:T(8,128)(2,1)}), f16[8,512,128]{2,1,0:T(8,128)(2,1)}, u32[]{:S(2)}, u32[]{:S(2)}) %all-to-all-start) | async-done | bytes 1048608 | tf_op jit(solution)/shard_map/all_to_all | solution.py:488
  24.3 1.5 convert_element_type.187.refs_0_
  26.2 2.0 shard_map.96
  32.3 1.5 collective-permute-start.1
  33.8 2.1 collective-permute-done.1
  36.6 9.2 %fusion.1 = (bf16[1024,1024]{1,0:T(8,128)(2,1)}, bf16[1024,1024]{1,0:T(8,128)(2,1)}, bf16[1024,1024]{1,0:T(8,128)(2,1)}, bf16[1024,1024]{1,0:T(8,128)(2,1)}) fusion(s32[1024]{0:T(1024)S(1)} %get-tuple-element.128, s32[1024]{0:T(1024)S(1)} %shift-right-arithmetic_and_fusion, s32[1024]{0:T(1024)S(1)} %get-tuple-element.129, s32[1024]{0:T(1024)S(1)} %get-tuple-element.122), kind=kLoop, calls=%fused_computation.5 | loop fusion | flops 62914560 | bytes 8404992 | tf_op jit(solution)/shard_map/convert_element_type | solution.py:78
  48.2 2.8 %shard_map.97 = (f32[5,128,256]{2,1,0:T(8,128)S(1)}, f32[5,128,256]{2,1,0:T(8,128)S(1)}, f32[5,128,256]{2,1,0:T(8,128)S(1)}, f32[5,128,256]{2,1,0:T(8,128)S(1)}) custom-call(f32[8,512,128]{2,1,0:T(8,128)S(1)} %convert_element_type.187.refs_0_, bf16[1024,512]{1,0:T(8,128)(2,1)S(1)} %copy-done.7, bf16[1024,512]{1,0:T(8,128)(2,1)S(1)} %copy-done.9, ...), custom_call_target="tpu_custom_call" | custom-call | tf_op jit(solution)/shard_map/pallas_call | solution.py:139
  51.0 4.1 %collective-permute-start.6 = (f16[5,128,256]{2,1,0:T(8,128)(2,1)S(1)}, f16[5,128,256]{2,1,0:T(8,128)(2,1)S(1)}, u32[]{:S(2)}, u32[]{:S(2)}) collective-permute-start(f16[5,128,256]{2,1,0:T(8,128)(2,1)S(1)} %convert_element_type.197), channel_id=1, source_target_pairs={{0,3},{1,0},{2,1},{3,2},{4,7},{5,4},{6,5},{7,6},{8,11},{9,8},{10,9... | collective-permute-start | bytes 983048 | tf_op jit(solution)/shard_map/ppermute | solution.py:471
  57.6 5.7 %collective-permute-done.6 = f16[5,128,256]{2,1,0:T(8,128)(2,1)S(1)} collective-permute-done((f16[5,128,256]{2,1,0:T(8,128)(2,1)S(1)}, f16[5,128,256]{2,1,0:T(8,128)(2,1)S(1)}, u32[]{:S(2)}, u32[]{:S(2)}) %collective-permute-start.6) | collective-permute-done | bytes 327712 | tf_op jit(solution)/shard_map/ppermute | solution.py:471
  63.3 18.7 %collective-permute-done.7 = f16[5,128,256]{2,1,0:T(8,128)(2,1)S(1)} collective-permute-done((f16[5,128,256]{2,1,0:T(8,128)(2,1)S(1)}, f16[5,128,256]{2,1,0:T(8,128)(2,1)S(1)}, u32[]{:S(2)}, u32[]{:S(2)}) %collective-permute-start.7) | collective-permute-done | bytes 327712 | tf_op jit(solution)/shard_map/ppermute | solution.py:471
  82.2 8.7 %shard_map.98 = (f32[4,32,40,128]{3,2,1,0:T(8,128)S(1)}, f32[4,32,40,128]{3,2,1,0:T(8,128)S(1)}) custom-call(s32[256]{0:T(256)S(1)} %get-tuple-element.93.refs_0_.a_ref, s32[256]{0:T(256)S(1)} %get-tuple-element.117.refs_1_.b_ref, f32[5,128,256]{2,1,0:T(8,128)S(1)} %convert_element_type.200.refs_2_, f32[5,128,256]{2,1,0:T(8,128)S(1)} %convert_element_type.201.refs_3_, ...), custom_call_target="tpu_custom_call" | custom-call | tf_op jit(solution)/shard_map/pallas_call | solution.py:139
  91.9 2.9 %collective-permute-start.4 = (f16[3,128,256]{2,1,0:T(8,128)(2,1)S(1)}, f16[3,128,256]{2,1,0:T(8,128)(2,1)S(1)}, u32[]{:S(2)}, u32[]{:S(2)}) collective-permute-start(f16[3,128,256]{2,1,0:T(8,128)(2,1)S(1)} %copy-done.18), channel_id=1, source_target_pairs={{0,2},{1,3},{2,0},{3,1},{4,6},{5,7},{6,4},{7,5},{8,10},{9,11},{10,... | collective-permute-start | bytes 589832 | tf_op jit(solution)/shard_map/ppermute | solution.py:471
  94.8 1.9 collective-permute-start.5
  98.5 13.8 %collective-permute-done.4 = f16[3,128,256]{2,1,0:T(8,128)(2,1)S(1)} collective-permute-done((f16[3,128,256]{2,1,0:T(8,128)(2,1)S(1)}, f16[3,128,256]{2,1,0:T(8,128)(2,1)S(1)}, u32[]{:S(2)}, u32[]{:S(2)}) %collective-permute-start.4) | collective-permute-done | bytes 196640 | tf_op jit(solution)/shard_map/ppermute | solution.py:471
  112.3 1.4 collective-permute-start.10
  113.7 1.5 collective-permute-start.11
  115.9 6.5 %shard_map.99 = (f32[4,32,24,128]{3,2,1,0:T(8,128)S(1)}, f32[4,32,24,128]{3,2,1,0:T(8,128)S(1)}) custom-call(s32[256]{0:T(256)S(1)} %get-tuple-element.93.refs_0_.a_ref, s32[256]{0:T(256)S(1)} %get-tuple-element.117.refs_1_.b_ref, f32[3,128,256]{2,1,0:T(8,128)S(1)} %convert_element_type.217.refs_2_, f32[3,128,256]{2,1,0:T(8,128)S(1)} %convert_element_type.218.refs_3_, ...), custom_call_target="tpu_custom_call" | custom-call | tf_op jit(solution)/shard_map/pallas_call | solution.py:139
  123.6 5.7 %collective-permute-done.11 = f16[32,40,128]{2,1,0:T(8,128)(2,1)S(1)} collective-permute-done((f16[32,40,128]{2,1,0:T(8,128)(2,1)S(1)}, f16[32,40,128]{2,1,0:T(8,128)(2,1)S(1)}, u32[]{:S(2)}, u32[]{:S(2)}) %collective-permute-start.11) | collective-permute-done | bytes 327712 | tf_op jit(solution)/shard_map/ppermute | solution.py:468
  132.3 1.5 collective-permute-start.16
  134.2 3.4 %collective-permute-done.14 = f16[32,24,128]{2,1,0:T(8,128)(2,1)S(1)} collective-permute-done((f16[32,24,128]{2,1,0:T(8,128)(2,1)S(1)}, f16[32,24,128]{2,1,0:T(8,128)(2,1)S(1)}, u32[]{:S(2)}, u32[]{:S(2)}) %collective-permute-start.14) | collective-permute-done | bytes 196640 | tf_op jit(solution)/shard_map/ppermute | solution.py:468
  137.7 3.0 %collective-permute-done.15 = f16[32,24,128]{2,1,0:T(8,128)(2,1)S(1)} collective-permute-done((f16[32,24,128]{2,1,0:T(8,128)(2,1)S(1)}, f16[32,24,128]{2,1,0:T(8,128)(2,1)S(1)}, u32[]{:S(2)}, u32[]{:S(2)}) %collective-permute-start.15) | collective-permute-done | bytes 196640 | tf_op jit(solution)/shard_map/ppermute | solution.py:468
  143.2 1.6 collective-permute-start.18
  144.8 1.3 collective-permute-start.19
  148.3 1.5 collective-permute-done.18.refs_2_
  149.8 2.6 collective-permute-done.19.refs_3_
  153.1 1.5 collective-permute-start.21
  155.9 5.1 %collective-permute-done.20.refs_1_ = bf16[32,40,128]{2,1,0:T(8,128)(2,1)S(1)} collective-permute-done((bf16[32,40,128]{2,1,0:T(8,128)(2,1)S(1)}, bf16[32,40,128]{2,1,0:T(8,128)(2,1)S(1)}, u32[]{:S(2)}, u32[]{:S(2)}) %collective-permute-start.20) | collective-permute-done | bytes 327712 | tf_op jit(solution)/shard_map/ppermute | solution.py:468
  161.0 4.7 %collective-permute-done.21.refs_2_ = bf16[32,40,128]{2,1,0:T(8,128)(2,1)S(1)} collective-permute-done((bf16[32,40,128]{2,1,0:T(8,128)(2,1)S(1)}, bf16[32,40,128]{2,1,0:T(8,128)(2,1)S(1)}, u32[]{:S(2)}, u32[]{:S(2)}) %collective-permute-start.21) | collective-permute-done | bytes 327712 | tf_op jit(solution)/shard_map/ppermute | solution.py:468
  166.7 3.4 %collective-permute-done.27.refs_4_ = bf16[4,32,24,128]{3,2,1,0:T(8,128)(2,1)S(1)} collective-permute-done((bf16[4,32,24,128]{3,2,1,0:T(8,128)(2,1)S(1)}, bf16[4,32,24,128]{3,2,1,0:T(8,128)(2,1)S(1)}, u32[]{:S(2)}, u32[]{:S(2)}) %collective-permute-start.27) | collective-permute-done | bytes 786464 | tf_op jit(solution)/shard_map/ppermute | solution.py:468
  170.2 6.1 %shard_map.101 = (bf16[3,128,256]{2,1,0:T(8,128)(2,1)S(1)}, bf16[3,128,256]{2,1,0:T(8,128)(2,1)S(1)}, bf16[3,128,256]{2,1,0:T(8,128)(2,1)S(1)}, bf16[3,128,256]{2,1,0:T(8,128)(2,1)S(1)}) custom-call(s32[256]{0:T(256)S(1)} %get-tuple-element.93.refs_0_.a_ref, s32[256]{0:T(256)S(1)} %get-tuple-element.117.refs_1_.b_ref, ...), custom_call_target="tpu_custom_call" | custom-call | tf_op jit(solution)/shard_map/pallas_call | solution.py:139
  176.6 7.6 %shard_map.100 = (bf16[5,128,256]{2,1,0:T(8,128)(2,1)S(1)}, bf16[5,128,256]{2,1,0:T(8,128)(2,1)S(1)}, bf16[5,128,256]{2,1,0:T(8,128)(2,1)S(1)}, bf16[5,128,256]{2,1,0:T(8,128)(2,1)S(1)}) custom-call(s32[256]{0:T(256)S(1)} %get-tuple-element.93.refs_0_.a_ref, s32[256]{0:T(256)S(1)} %get-tuple-element.117.refs_1_.b_ref, ...), custom_call_target="tpu_custom_call" | custom-call | tf_op jit(solution)/shard_map/pallas_call | solution.py:139
  184.3 3.5 %collective-permute-start.24 = (bf16[5,128,256]{2,1,0:T(8,128)(2,1)S(1)}, bf16[5,128,256]{2,1,0:T(8,128)(2,1)S(1)}, u32[]{:S(2)}, u32[]{:S(2)}) collective-permute-start(bf16[5,128,256]{2,1,0:T(8,128)(2,1)S(1)} %get-tuple-element.71), channel_id=1, source_target_pairs={{0,3},{1,0},{2,1},{3,2},{4,7},{5,4},{6,5},{7,6},{8,11},{9,8},{10,9... | collective-permute-start | bytes 983048 | tf_op jit(solution)/shard_map/ppermute | solution.py:471
  188.4 2.3 collective-permute-start.29
  190.7 1.5 collective-permute-start.30
  192.2 36.7 %collective-permute-done.29.refs_2_ = bf16[3,128,256]{2,1,0:T(8,128)(2,1)S(1)} collective-permute-done((bf16[3,128,256]{2,1,0:T(8,128)(2,1)S(1)}, bf16[3,128,256]{2,1,0:T(8,128)(2,1)S(1)}, u32[]{:S(2)}, u32[]{:S(2)}) %collective-permute-start.29) | collective-permute-done | bytes 196640 | tf_op jit(solution)/shard_map/ppermute | solution.py:471
  228.9 1.8 shard_map.102.refs_4_
  230.8 4.2 %shard_map.103 = bf16[8,512,128]{2,1,0:T(8,128)(2,1)} custom-call(bf16[5,128,256]{2,1,0:T(8,128)(2,1)S(1)} %get-tuple-element.70.refs_0_, bf16[5,128,256]{2,1,0:T(8,128)(2,1)S(1)} %collective-permute-done.24.refs_1_, bf16[5,128,256]{2,1,0:T(8,128)(2,1)S(1)} %collective-permute-done.25.refs_2_, bf16[5,128,256]{2,1,0:T(8,128)(2,1)S(1)} %collective-permute-done.26.refs_3_, ...), custom_call_target="tpu_custom_call" | custom-call | tf_op jit(solution)/shard_map/pallas_call | solution.py:139
  235.0 4.3 %all-to-all-start.1 = ((bf16[8,512,128]{2,1,0:T(8,128)(2,1)}), bf16[8,512,128]{2,1,0:T(8,128)(2,1)S(1)}, u32[]{:S(2)}, u32[]{:S(2)}) async-start(bf16[8,512,128]{2,1,0:T(8,128)(2,1)} %shard_map.103), calls=%async_computation.1 | async-start | bytes 2097152 | tf_op jit(solution)/shard_map/all_to_all | solution.py:556
  247.7 1.7 convert_convert_fusion.spread_ref
  249.9 1.6 collective-permute-start.31
  251.4 1.8 all-to-all-done.1.grad_ref
  254.1 1.5 collective-permute-start.32
  256.4 1.6 copy-done.14
  259.8 7.3 %haar.1 = f32[512,1024]{1,0:T(8,128)} custom-call(f32[512,1024]{1,0:T(8,128)S(1)} %shard_map.104.refs_0_, f32[8,512]{1,0:T(8,128)S(1)} %sub.148.refs_1_, f32[8,512]{1,0:T(8,128)S(1)} %sub.149.refs_2_, f32[4,1152]{1,0:T(4,128)S(1)} %pad_maximum_fusion.6.refs_3_), custom_call_target="tpu_custom_call" | custom-call | tf_op jit(solution)/shard_map/haar/pallas_call | solution.py:435
  (157 shorter events, 32.6 us)
Async XLA Ops:
  0.6 122.0 %copy-start = (bf16[32,64,256]{2,1,0:T(8,128)(2,1)S(1)}, bf16[32,64,256]{2,1,0:T(8,128)(2,1)}, u32[]{:S(2)}) copy-start(bf16[32,64,256]{2,1,0:T(8,128)(2,1)} %param.10) | copy-start | bytes 3145732
  5.0 5.7 %copy-start.23 = (s32[32]{0:T(128)S(1)}, s32[32]{0:T(128)}, u32[]{:S(2)}) copy-start(s32[32]{0:T(128)} %param.13) | copy-start | bytes 388
  5.0 5.7 %copy-start.24 = (s32[32,1]{0,1:T(1,128)S(1)}, s32[32,1]{0,1:T(1,128)}, u32[]{:S(2)}) copy-start(s32[32,1]{0,1:T(1,128)} %param.12) | copy-start | bytes 388
  6.1 18.2 %all-to-all-start = ((f16[8,512,128]{2,1,0:T(8,128)(2,1)}), f16[8,512,128]{2,1,0:T(8,128)(2,1)}, u32[]{:S(2)}, u32[]{:S(2)}) async-start(f16[8,512,128]{2,1,0:T(8,128)(2,1)} %convert_element_type.186), calls=%async_computation | async-start | bytes 2097152 | tf_op jit(solution)/shard_map/all_to_all | solution.py:488
  31.0 1.2 collective-permute-start
  32.3 3.6 %collective-permute-start.1 = (s32[2,64]{1,0:T(2,128)S(1)}, s32[2,64]{1,0:T(2,128)S(1)}, u32[]{:S(2)}, u32[]{:S(2)}) collective-permute-start(s32[2,64]{1,0:T(2,128)S(1)} %pad_add_fusion.2), channel_id=1, source_target_pairs={{0,8},{4,12},{8,0},{12,4},{16,24},{20,28},{24,16},{28,20},{1,9},{5... | collective-permute-start | bytes 1544 | tf_op jit(solution)/shard_map/ppermute | solution.py:468
  35.9 20.7 %collective-permute-start.2 = (s32[2,128]{1,0:T(2,128)S(1)}, s32[2,128]{1,0:T(2,128)S(1)}, u32[]{:S(2)}, u32[]{:S(2)}) collective-permute-start(s32[2,128]{1,0:T(2,128)S(1)} %pad_add_fusion.3), channel_id=1, source_target_pairs={{0,16},{4,20},{8,24},{12,28},{16,0},{20,4},{24,8},{28,12},{1,17},{... | collective-permute-start | bytes 3080 | tf_op jit(solution)/shard_map/ppermute | solution.py:468
  51.0 12.2 %collective-permute-start.6 = (f16[5,128,256]{2,1,0:T(8,128)(2,1)S(1)}, f16[5,128,256]{2,1,0:T(8,128)(2,1)S(1)}, u32[]{:S(2)}, u32[]{:S(2)}) collective-permute-start(f16[5,128,256]{2,1,0:T(8,128)(2,1)S(1)} %convert_element_type.197), channel_id=1, source_target_pairs={{0,3},{1,0},{2,1},{3,2},{4,7},{5,4},{6,5},{7,6},{8,11},{9,8},{10,9... | collective-permute-start | bytes 983048 | tf_op jit(solution)/shard_map/ppermute | solution.py:471
  55.2 26.8 %collective-permute-start.7 = (f16[5,128,256]{2,1,0:T(8,128)(2,1)S(1)}, f16[5,128,256]{2,1,0:T(8,128)(2,1)S(1)}, u32[]{:S(2)}, u32[]{:S(2)}) collective-permute-start(f16[5,128,256]{2,1,0:T(8,128)(2,1)S(1)} %convert_element_type.198), channel_id=1, source_target_pairs={{0,2},{1,3},{2,0},{3,1},{4,6},{5,7},{6,4},{7,5},{8,10},{9,11},{10,... | collective-permute-start | bytes 983048 | tf_op jit(solution)/shard_map/ppermute | solution.py:471
  55.3 26.6 %collective-permute-start.8 = (f16[5,128,256]{2,1,0:T(8,128)(2,1)S(1)}, f16[5,128,256]{2,1,0:T(8,128)(2,1)S(1)}, u32[]{:S(2)}, u32[]{:S(2)}) collective-permute-start(f16[5,128,256]{2,1,0:T(8,128)(2,1)S(1)} %convert_element_type.199), channel_id=1, source_target_pairs={{0,1},{1,2},{2,3},{3,0},{4,5},{5,6},{6,7},{7,4},{8,9},{9,10},{10,1... | collective-permute-start | bytes 983048 | tf_op jit(solution)/shard_map/ppermute | solution.py:471
  57.4 24.8 %copy-start.4 = (bf16[1024,1024]{1,0:T(8,128)(2,1)S(1)}, bf16[1024,1024]{1,0:T(8,128)(2,1)}, u32[]{:S(2)}) copy-start(bf16[1024,1024]{1,0:T(8,128)(2,1)} %get-tuple-element.103.refs_7_) | copy-start | bytes 6291460
  57.4 24.8 %copy-start.5 = (bf16[1024,1024]{1,0:T(8,128)(2,1)S(1)}, bf16[1024,1024]{1,0:T(8,128)(2,1)}, u32[]{:S(2)}) copy-start(bf16[1024,1024]{1,0:T(8,128)(2,1)} %get-tuple-element.105.refs_6_) | copy-start | bytes 6291460
  91.1 5.7 %collective-permute-start.9 = (f16[4,32,40,128]{3,2,1,0:T(8,128)(2,1)S(1)}, f16[4,32,40,128]{3,2,1,0:T(8,128)(2,1)S(1)}, u32[]{:S(2)}, u32[]{:S(2)}) collective-permute-start(f16[4,32,40,128]{3,2,1,0:T(8,128)(2,1)S(1)} %convert_element_type.208), channel_id=1, source_target_pairs={{0,4},{4,0},{8,12},{12,8},{16,20},{20,16},{24,28},{28,24},{1,5},{5... | collective-permute-start | bytes 3932168 | tf_op jit(solution)/shard_map/ppermute | solution.py:468
  91.8 6.7 %collective-permute-start.3 = (f16[3,128,256]{2,1,0:T(8,128)(2,1)S(1)}, f16[3,128,256]{2,1,0:T(8,128)(2,1)S(1)}, u32[]{:S(2)}, u32[]{:S(2)}) collective-permute-start(f16[3,128,256]{2,1,0:T(8,128)(2,1)S(1)} %copy-done.19), channel_id=1, source_target_pairs={{0,3},{1,0},{2,1},{3,2},{4,7},{5,4},{6,5},{7,6},{8,11},{9,8},{10,9... | collective-permute-start | bytes 589832 | tf_op jit(solution)/shard_map/ppermute | solution.py:471
  91.9 20.4 %collective-permute-start.4 = (f16[3,128,256]{2,1,0:T(8,128)(2,1)S(1)}, f16[3,128,256]{2,1,0:T(8,128)(2,1)S(1)}, u32[]{:S(2)}, u32[]{:S(2)}) collective-permute-start(f16[3,128,256]{2,1,0:T(8,128)(2,1)S(1)} %copy-done.18), channel_id=1, source_target_pairs={{0,2},{1,3},{2,0},{3,1},{4,6},{5,7},{6,4},{7,5},{8,10},{9,11},{10,... | collective-permute-start | bytes 589832 | tf_op jit(solution)/shard_map/ppermute | solution.py:471
  94.8 17.5 %collective-permute-start.5 = (f16[3,128,256]{2,1,0:T(8,128)(2,1)S(1)}, f16[3,128,256]{2,1,0:T(8,128)(2,1)S(1)}, u32[]{:S(2)}, u32[]{:S(2)}) collective-permute-start(f16[3,128,256]{2,1,0:T(8,128)(2,1)S(1)} %copy-done.17), channel_id=1, source_target_pairs={{0,1},{1,2},{2,3},{3,0},{4,5},{5,6},{6,7},{7,4},{8,9},{9,10},{10,1... | collective-permute-start | bytes 589832 | tf_op jit(solution)/shard_map/ppermute | solution.py:471
  97.2 18.6 %copy-start.16 = (f16[3,128,256]{2,1,0:T(8,128)(2,1)S(1)}, f16[3,128,256]{2,1,0:T(8,128)(2,1)}, u32[]{:S(2)}) copy-start(f16[3,128,256]{2,1,0:T(8,128)(2,1)} %convert_element_type.192) | copy-start | bytes 589828
  112.3 11.3 %collective-permute-start.10 = (f16[32,40,128]{2,1,0:T(8,128)(2,1)S(1)}, f16[32,40,128]{2,1,0:T(8,128)(2,1)S(1)}, u32[]{:S(2)}, u32[]{:S(2)}) collective-permute-start(f16[32,40,128]{2,1,0:T(8,128)(2,1)S(1)} %get-tuple-element.60), channel_id=1, source_target_pairs={{0,8},{4,12},{8,0},{12,4},{16,24},{20,28},{24,16},{28,20},{1,9},{5... | collective-permute-start | bytes 983048 | tf_op jit(solution)/shard_map/ppermute | solution.py:468
  113.7 15.6 %collective-permute-start.11 = (f16[32,40,128]{2,1,0:T(8,128)(2,1)S(1)}, f16[32,40,128]{2,1,0:T(8,128)(2,1)S(1)}, u32[]{:S(2)}, u32[]{:S(2)}) collective-permute-start(f16[32,40,128]{2,1,0:T(8,128)(2,1)S(1)} %get-tuple-element.61), channel_id=1, source_target_pairs={{0,16},{4,20},{8,24},{12,28},{16,0},{20,4},{24,8},{28,12},{1,17},{... | collective-permute-start | bytes 983048 | tf_op jit(solution)/shard_map/ppermute | solution.py:468
  115.2 14.1 %collective-permute-start.12 = (f16[32,40,128]{2,1,0:T(8,128)(2,1)S(1)}, f16[32,40,128]{2,1,0:T(8,128)(2,1)S(1)}, u32[]{:S(2)}, u32[]{:S(2)}) collective-permute-start(f16[32,40,128]{2,1,0:T(8,128)(2,1)S(1)} %get-tuple-element.62), channel_id=1, source_target_pairs={{0,24},{4,28},{8,16},{12,20},{16,8},{20,12},{24,0},{28,4},{1,25},{... | collective-permute-start | bytes 983048 | tf_op jit(solution)/shard_map/ppermute | solution.py:468
  122.6 6.9 %copy-start.15 = (bf16[32,64,256]{2,1,0:T(8,128)(2,1)S(1)}, bf16[32,64,256]{2,1,0:T(8,128)(2,1)}, u32[]{:S(2)}) copy-start(bf16[32,64,256]{2,1,0:T(8,128)(2,1)} %param.9) | copy-start | bytes 3145732
  122.6 7.3 %collective-permute-start.13 = (f16[4,32,24,128]{3,2,1,0:T(8,128)(2,1)S(1)}, f16[4,32,24,128]{3,2,1,0:T(8,128)(2,1)S(1)}, u32[]{:S(2)}, u32[]{:S(2)}) collective-permute-start(f16[4,32,24,128]{3,2,1,0:T(8,128)(2,1)S(1)} %convert_element_type.221), channel_id=1, source_target_pairs={{0,4},{4,0},{8,12},{12,8},{16,20},{20,16},{24,28},{28,24},{1,5},{5... | collective-permute-start | bytes 2359304 | tf_op jit(solution)/shard_map/ppermute | solution.py:468
  130.3 7.4 %collective-permute-start.14 = (f16[32,24,128]{2,1,0:T(8,128)(2,1)S(1)}, f16[32,24,128]{2,1,0:T(8,128)(2,1)S(1)}, u32[]{:S(2)}, u32[]{:S(2)}) collective-permute-start(f16[32,24,128]{2,1,0:T(8,128)(2,1)S(1)} %get-tuple-element.97), channel_id=1, source_target_pairs={{0,8},{4,12},{8,0},{12,4},{16,24},{20,28},{24,16},{28,20},{1,9},{5... | collective-permute-start | bytes 589832 | tf_op jit(solution)/shard_map/ppermute | solution.py:468
  131.5 9.2 %collective-permute-start.15 = (f16[32,24,128]{2,1,0:T(8,128)(2,1)S(1)}, f16[32,24,128]{2,1,0:T(8,128)(2,1)S(1)}, u32[]{:S(2)}, u32[]{:S(2)}) collective-permute-start(f16[32,24,128]{2,1,0:T(8,128)(2,1)S(1)} %get-tuple-element.99), channel_id=1, source_target_pairs={{0,16},{4,20},{8,24},{12,28},{16,0},{20,4},{24,8},{28,12},{1,17},{... | collective-permute-start | bytes 589832 | tf_op jit(solution)/shard_map/ppermute | solution.py:468
  132.3 8.4 %collective-permute-start.16 = (f16[32,24,128]{2,1,0:T(8,128)(2,1)S(1)}, f16[32,24,128]{2,1,0:T(8,128)(2,1)S(1)}, u32[]{:S(2)}, u32[]{:S(2)}) collective-permute-start(f16[32,24,128]{2,1,0:T(8,128)(2,1)S(1)} %get-tuple-element.98), channel_id=1, source_target_pairs={{0,24},{4,28},{8,16},{12,20},{16,8},{20,12},{24,0},{28,4},{1,25},{... | collective-permute-start | bytes 589832 | tf_op jit(solution)/shard_map/ppermute | solution.py:468
  142.6 5.7 %collective-permute-start.17 = (bf16[32,24,128]{2,1,0:T(8,128)(2,1)S(1)}, bf16[32,24,128]{2,1,0:T(8,128)(2,1)S(1)}, u32[]{:S(2)}, u32[]{:S(2)}) collective-permute-start(bf16[32,24,128]{2,1,0:T(8,128)(2,1)S(1)} %pad_maximum_fusion.3.refs_0_), channel_id=1, source_target_pairs={{0,8},{4,12},{8,0},{12,4},{16,24},{20,28},{24,16},{28,20},{1,9},{5... | collective-permute-start | bytes 589832 | tf_op jit(solution)/shard_map/ppermute | solution.py:468
  143.2 6.6 %collective-permute-start.18 = (bf16[32,24,128]{2,1,0:T(8,128)(2,1)S(1)}, bf16[32,24,128]{2,1,0:T(8,128)(2,1)S(1)}, u32[]{:S(2)}, u32[]{:S(2)}) collective-permute-start(bf16[32,24,128]{2,1,0:T(8,128)(2,1)S(1)} %pad_maximum_fusion.3.refs_0_), channel_id=1, source_target_pairs={{0,16},{4,20},{8,24},{12,28},{16,0},{20,4},{24,8},{28,12},{1,17},{... | collective-permute-start | bytes 589832 | tf_op jit(solution)/shard_map/ppermute | solution.py:468
  144.8 7.6 %collective-permute-start.19 = (bf16[32,24,128]{2,1,0:T(8,128)(2,1)S(1)}, bf16[32,24,128]{2,1,0:T(8,128)(2,1)S(1)}, u32[]{:S(2)}, u32[]{:S(2)}) collective-permute-start(bf16[32,24,128]{2,1,0:T(8,128)(2,1)S(1)} %pad_maximum_fusion.3.refs_0_), channel_id=1, source_target_pairs={{0,24},{4,28},{8,16},{12,20},{16,8},{20,12},{24,0},{28,4},{1,25},{... | collective-permute-start | bytes 589832 | tf_op jit(solution)/shard_map/ppermute | solution.py:468
  152.4 8.6 %collective-permute-start.20 = (bf16[32,40,128]{2,1,0:T(8,128)(2,1)S(1)}, bf16[32,40,128]{2,1,0:T(8,128)(2,1)S(1)}, u32[]{:S(2)}, u32[]{:S(2)}) collective-permute-start(bf16[32,40,128]{2,1,0:T(8,128)(2,1)S(1)} %pad_maximum_fusion.2.refs_0_), channel_id=1, source_target_pairs={{0,8},{4,12},{8,0},{12,4},{16,24},{20,28},{24,16},{28,20},{1,9},{5... | collective-permute-start | bytes 983048 | tf_op jit(solution)/shard_map/ppermute | solution.py:468
  153.1 12.6 %collective-permute-start.21 = (bf16[32,40,128]{2,1,0:T(8,128)(2,1)S(1)}, bf16[32,40,128]{2,1,0:T(8,128)(2,1)S(1)}, u32[]{:S(2)}, u32[]{:S(2)}) collective-permute-start(bf16[32,40,128]{2,1,0:T(8,128)(2,1)S(1)} %pad_maximum_fusion.2.refs_0_), channel_id=1, source_target_pairs={{0,16},{4,20},{8,24},{12,28},{16,0},{20,4},{24,8},{28,12},{1,17},{... | collective-permute-start | bytes 983048 | tf_op jit(solution)/shard_map/ppermute | solution.py:468
  154.7 11.1 %collective-permute-start.22 = (bf16[32,40,128]{2,1,0:T(8,128)(2,1)S(1)}, bf16[32,40,128]{2,1,0:T(8,128)(2,1)S(1)}, u32[]{:S(2)}, u32[]{:S(2)}) collective-permute-start(bf16[32,40,128]{2,1,0:T(8,128)(2,1)S(1)} %pad_maximum_fusion.2.refs_0_), channel_id=1, source_target_pairs={{0,24},{4,28},{8,16},{12,20},{16,8},{20,12},{24,0},{28,4},{1,25},{... | collective-permute-start | bytes 983048 | tf_op jit(solution)/shard_map/ppermute | solution.py:468
  165.9 10.7 %collective-permute-start.23 = (bf16[4,32,40,128]{3,2,1,0:T(8,128)(2,1)S(1)}, bf16[4,32,40,128]{3,2,1,0:T(8,128)(2,1)S(1)}, u32[]{:S(2)}, u32[]{:S(2)}) collective-permute-start(bf16[4,32,40,128]{3,2,1,0:T(8,128)(2,1)S(1)} %pad_maximum_fusion), channel_id=1, source_target_pairs={{0,4},{4,0},{8,12},{12,8},{16,20},{20,16},{24,28},{28,24},{1,5},{5... | collective-permute-start | bytes 3932168 | tf_op jit(solution)/shard_map/ppermute | solution.py:468
  166.2 4.0 %collective-permute-start.27 = (bf16[4,32,24,128]{3,2,1,0:T(8,128)(2,1)S(1)}, bf16[4,32,24,128]{3,2,1,0:T(8,128)(2,1)S(1)}, u32[]{:S(2)}, u32[]{:S(2)}) collective-permute-start(bf16[4,32,24,128]{3,2,1,0:T(8,128)(2,1)S(1)} %pad_maximum_fusion.1), channel_id=1, source_target_pairs={{0,4},{4,0},{8,12},{12,8},{16,20},{20,16},{24,28},{28,24},{1,5},{5... | collective-permute-start | bytes 2359304 | tf_op jit(solution)/shard_map/ppermute | solution.py:468
  176.3 52.6 %copy-start.10 = (bf16[1024,512]{1,0:T(8,128)(2,1)S(1)}, bf16[1024,512]{1,0:T(8,128)(2,1)}, u32[]{:S(2)}) copy-start(bf16[1024,512]{1,0:T(8,128)(2,1)} %get-tuple-element.106.refs_5_.refs_6_) | copy-start | bytes 3145732
  176.3 52.6 %copy-start.11 = (bf16[1024,512]{1,0:T(8,128)(2,1)S(1)}, bf16[1024,512]{1,0:T(8,128)(2,1)}, u32[]{:S(2)}) copy-start(bf16[1024,512]{1,0:T(8,128)(2,1)} %get-tuple-element.107.refs_4_.refs_5_) | copy-start | bytes 3145732
  176.3 14.4 %collective-permute-start.28 = (bf16[3,128,256]{2,1,0:T(8,128)(2,1)S(1)}, bf16[3,128,256]{2,1,0:T(8,128)(2,1)S(1)}, u32[]{:S(2)}, u32[]{:S(2)}) collective-permute-start(bf16[3,128,256]{2,1,0:T(8,128)(2,1)S(1)} %get-tuple-element.75), channel_id=1, source_target_pairs={{0,3},{1,0},{2,1},{3,2},{4,7},{5,4},{6,5},{7,6},{8,11},{9,8},{10,9... | collective-permute-start | bytes 589832 | tf_op jit(solution)/shard_map/ppermute | solution.py:471
  184.3 46.5 %collective-permute-start.24 = (bf16[5,128,256]{2,1,0:T(8,128)(2,1)S(1)}, bf16[5,128,256]{2,1,0:T(8,128)(2,1)S(1)}, u32[]{:S(2)}, u32[]{:S(2)}) collective-permute-start(bf16[5,128,256]{2,1,0:T(8,128)(2,1)S(1)} %get-tuple-element.71), channel_id=1, source_target_pairs={{0,3},{1,0},{2,1},{3,2},{4,7},{5,4},{6,5},{7,6},{8,11},{9,8},{10,9... | collective-permute-start | bytes 983048 | tf_op jit(solution)/shard_map/ppermute | solution.py:471
  187.8 43.0 %collective-permute-start.25 = (bf16[5,128,256]{2,1,0:T(8,128)(2,1)S(1)}, bf16[5,128,256]{2,1,0:T(8,128)(2,1)S(1)}, u32[]{:S(2)}, u32[]{:S(2)}) collective-permute-start(bf16[5,128,256]{2,1,0:T(8,128)(2,1)S(1)} %get-tuple-element.72), channel_id=1, source_target_pairs={{0,2},{1,3},{2,0},{3,1},{4,6},{5,7},{6,4},{7,5},{8,10},{9,11},{10,... | collective-permute-start | bytes 983048 | tf_op jit(solution)/shard_map/ppermute | solution.py:471
  187.8 43.0 %collective-permute-start.26 = (bf16[5,128,256]{2,1,0:T(8,128)(2,1)S(1)}, bf16[5,128,256]{2,1,0:T(8,128)(2,1)S(1)}, u32[]{:S(2)}, u32[]{:S(2)}) collective-permute-start(bf16[5,128,256]{2,1,0:T(8,128)(2,1)S(1)} %get-tuple-element.73), channel_id=1, source_target_pairs={{0,1},{1,2},{2,3},{3,0},{4,5},{5,6},{6,7},{7,4},{8,9},{9,10},{10,1... | collective-permute-start | bytes 983048 | tf_op jit(solution)/shard_map/ppermute | solution.py:471
  188.4 40.5 %collective-permute-start.29 = (bf16[3,128,256]{2,1,0:T(8,128)(2,1)S(1)}, bf16[3,128,256]{2,1,0:T(8,128)(2,1)S(1)}, u32[]{:S(2)}, u32[]{:S(2)}) collective-permute-start(bf16[3,128,256]{2,1,0:T(8,128)(2,1)S(1)} %get-tuple-element.76), channel_id=1, source_target_pairs={{0,2},{1,3},{2,0},{3,1},{4,6},{5,7},{6,4},{7,5},{8,10},{9,11},{10,... | collective-permute-start | bytes 589832 | tf_op jit(solution)/shard_map/ppermute | solution.py:471
  190.7 38.2 %collective-permute-start.30 = (bf16[3,128,256]{2,1,0:T(8,128)(2,1)S(1)}, bf16[3,128,256]{2,1,0:T(8,128)(2,1)S(1)}, u32[]{:S(2)}, u32[]{:S(2)}) collective-permute-start(bf16[3,128,256]{2,1,0:T(8,128)(2,1)S(1)} %get-tuple-element.77), channel_id=1, source_target_pairs={{0,1},{1,2},{2,3},{3,0},{4,5},{5,6},{6,7},{7,4},{8,9},{9,10},{10,1... | collective-permute-start | bytes 589832 | tf_op jit(solution)/shard_map/ppermute | solution.py:471
  235.0 18.2 %all-to-all-start.1 = ((bf16[8,512,128]{2,1,0:T(8,128)(2,1)}), bf16[8,512,128]{2,1,0:T(8,128)(2,1)S(1)}, u32[]{:S(2)}, u32[]{:S(2)}) async-start(bf16[8,512,128]{2,1,0:T(8,128)(2,1)} %shard_map.103), calls=%async_computation.1 | async-start | bytes 2097152 | tf_op jit(solution)/shard_map/all_to_all | solution.py:556
  239.3 17.0 %copy-start.13 = (f32[512,1024]{1,0:T(8,128)S(1)}, f32[512,1024]{1,0:T(8,128)}, u32[]{:S(2)}) copy-start(f32[512,1024]{1,0:T(8,128)} %image_ref.3) | copy-start | bytes 6291460
  249.4 9.8 %collective-permute-start.33 = (f32[8,512]{1,0:T(8,128)S(1)}, f32[8,512]{1,0:T(8,128)S(1)}, u32[]{:S(2)}, u32[]{:S(2)}) collective-permute-start(f32[8,512]{1,0:T(8,128)S(1)} %get-tuple-element.82), channel_id=1, source_target_pairs={{0,3},{1,0},{2,1},{3,2},{4,7},{5,4},{6,5},{7,6},{8,11},{9,8},{10,9... | collective-permute-start | bytes 49160 | tf_op jit(solution)/shard_map/ppermute | solution.py:471
  249.9 9.4 %collective-permute-start.31 = (f32[8,512]{1,0:T(8,128)S(1)}, f32[8,512]{1,0:T(8,128)S(1)}, u32[]{:S(2)}, u32[]{:S(2)}) collective-permute-start(f32[8,512]{1,0:T(8,128)S(1)} %get-tuple-element.80), channel_id=1, source_target_pairs={{0,1},{1,2},{2,3},{3,0},{4,5},{5,6},{6,7},{7,4},{8,9},{9,10},{10,1... | collective-permute-start | bytes 49160 | tf_op jit(solution)/shard_map/ppermute | solution.py:471
  253.6 5.6 %collective-permute-start.34 = (f32[8,512]{1,0:T(8,128)S(1)}, f32[8,512]{1,0:T(8,128)S(1)}, u32[]{:S(2)}, u32[]{:S(2)}) collective-permute-start(f32[8,512]{1,0:T(8,128)S(1)} %get-tuple-element.83), channel_id=1, source_target_pairs={{0,3},{1,0},{2,1},{3,2},{4,7},{5,4},{6,5},{7,6},{8,11},{9,8},{10,9... | collective-permute-start | bytes 49160 | tf_op jit(solution)/shard_map/ppermute | solution.py:471
  254.1 5.7 %collective-permute-start.32 = (f32[8,512]{1,0:T(8,128)S(1)}, f32[8,512]{1,0:T(8,128)S(1)}, u32[]{:S(2)}, u32[]{:S(2)}) collective-permute-start(f32[8,512]{1,0:T(8,128)S(1)} %get-tuple-element.81), channel_id=1, source_target_pairs={{0,1},{1,2},{2,3},{3,0},{4,5},{5,6},{6,7},{7,4},{8,9},{9,10},{10,1... | collective-permute-start | bytes 49160 | tf_op jit(solution)/shard_map/ppermute | solution.py:471
  259.8 7.3 %copy-start.1 = (bf16[32,64,256]{2,1,0:T(8,128)(2,1)S(1)}, bf16[32,64,256]{2,1,0:T(8,128)(2,1)}, u32[]{:S(2)}) copy-start(bf16[32,64,256]{2,1,0:T(8,128)(2,1)} %param.10) | copy-start | bytes 3145732
  (14 other events, 29.6 us)

commit v2 on v1

--- a/solution.py
+++ b/solution.py
@@ -343,9 +343,18 @@
 LANES = 128
 
 
-def step_kernel(image_ref, grad_ref, spread_ref, out_ref):
-    grad = jnp.concatenate([grad_ref[i] for i in range(grad_ref.shape[0])], 1)
-    out_ref[...] = image_ref[...] - jnp.dot(grad, spread_ref[...], preferred_element_type=F32)
+def step_kernel(image_ref, grad_ref, out_ref):
+    groups, _, m = grad_ref.shape
+    width = groups * m
+    grad = jnp.concatenate([grad_ref[i] for i in range(groups)], 1)
+    wide = 2 * LANES
+    place = lax.broadcasted_iota(jnp.int32, (width, wide), 0)
+    column = (place & (m - 1)) * groups + (place >> bits(m))
+    lane = lax.broadcasted_iota(jnp.int32, (width, wide), 1)
+    for start in range(0, width, wide):
+        spot = (slice(None), slice(start, start + wide))
+        table = (column == lane + start).astype(F32).astype(BF16)
+        out_ref[spot] = image_ref[spot] - jnp.dot(grad, table, preferred_element_type=F32)
 
 
 def edge_kernel(grad_ref, first_ref, last_ref):
@@ -495,7 +504,6 @@
         y = rows_forward_fast(x, wavs, forward_table, twist, half)
         sent.append([part_y.astype(F16) for part_y in y])
         spectra.append(exchange(sent[half]))
-    spectra[0], _ = lax.optimization_barrier((spectra[0], sent[1]))
 
     ids = jnp.stack([dest_owner[:, 0], patch_slot])
     ids, _ = lax.optimization_barrier((ids, sent[1]))
@@ -515,12 +523,8 @@
         far, near = shares_fast(a_block, b_block, y, table, cos_k, sin_k)
         near = near + flip(far.astype(F16), 1).astype(F32)
         ready = [near[0]] + [near[chip].astype(F16) for chip in (1, 2, 3)]
-        if half == 0:
-            spectra[1], ready = lax.optimization_barrier((spectra[1], ready))
-        total = ready[0]
-        for came in to_chips(ready[1:]):
-            total = total + came.astype(F32)
-        patches.append(total.astype(BF16))
+        came = to_chips(ready[1:])
+        patches.append(sum([part_sum.astype(F32) for part_sum in came], ready[0]).astype(BF16))
 
     place = np.arange(PATCH)
     chosen = (place % 8) * vis + np.asarray(ORDER)[place // 8]
@@ -554,11 +558,10 @@
     first = call(rows_inverse_first, [((3, rows, m), F32)], [], *grads[1], *back_table, twist)
     grad = call(rows_inverse_last, [((vis, rows, m), BF16)], [], *grads[0], *first, *back_table, twist)[0]
     grad = lax.all_to_all(grad, "vis", split_axis=0, concat_axis=0, tiled=True)
-    back = spread_matrix(vis, m).T.astype(BF16)
     grad_edges = call(edge_kernel, [edge, edge], [], grad)
     right = ahead(grad_edges[0], wavs - 1)
     left = ahead(grad_edges[1], 1)
-    shifted = call(step_kernel, [((rows, cols), F32)], [], image, grad, back)[0]
+    shifted = call(step_kernel, [((rows, cols), F32)], [], image, grad)[0]
     return haar_mean(shifted, sky_left - left, sky_right - right, thresholds), misfit
 
 

time: 270 us -> 280 us (1.037)
  waiting for transfers between devices: 120 us -> 134 us
    ppermute x19, waiting for transfers between devices: 33.9 us -> 45 us  [flip(): return lax.ppermute(x, 'vis', [(i, i ^ mask) for i in range(vis)])]
    unnamed x51 -> x47, local copies, waits for them, and re-layouts: 8.13 us -> 6.66 us
  transfers between devices with their start and end apart: 37 -> 37, of which waited for: 19 -> 19; matrix products, arithmetic and copies ran while one was open for 9% -> 8% of each run, Pallas kernels for 10% -> 10%
where the time goes in v2:
time: 280 us; the launch traced here: 277 us
  waiting for transfers between devices  134 us (48%)
  Pallas kernels  50.2 us (18%)
  starting transfers between devices  48.6 us (17%)
  other arithmetic  24.3 us (9%)
  between operations  8.73 us (3%)
  local copies, waits for them, and re-layouts  7.59 us (3%)
  matrix products  3.54 us (1%)
    ppermute x16, waiting for transfers between devices, ahead(): return lax.ppermute(x, 'wav', [(i, (i + by) % wavs) for i in range(wavs)])  77.9 us
    ppermute x19, waiting for transfers between devices, flip(): return lax.ppermute(x, 'vis', [(i, i ^ mask) for i in range(vis)])  45 us
    pallas_call x11, Pallas kernels, call(): pl.pallas_call(kernel, in_specs=[pl.BlockSpec(memory_space=pltpu.SMEM)] *...  43 us
    ppermute x16, starting transfers between devices, ahead(): return lax.ppermute(x, 'wav', [(i, (i + by) % wavs) for i in range(wavs)])  22.5 us
    ppermute x19, starting transfers between devices, flip(): return lax.ppermute(x, 'vis', [(i, i ^ mask) for i in range(vis)])  17.1 us
    convert_element_type x2, other arithmetic, split(): return (high.astype(BF16), (x - high).astype(BF16))  15.1 us
    all_to_all x1, waiting for transfers between devices, shards_fast(): x = lax.all_to_all(x, 'vis', split_axis=0, concat_axis=0, tiled=True)  7.78 us
    pallas_call x1, Pallas kernels, haar_mean(): pl.pallas_call(lambda *refs: haar_kernel(*refs, bases=bases), grid=(rows...  7.25 us
  transfers between devices with their start and end apart: 37, of which 19 were waited for; matrix products, arithmetic and copies ran while one was open for 8% of the time, Pallas kernels for 10%

profile of v2, /device:TPU:2, one launch (start us, length us, event | category | flops | bytes accessed | tf_op | source)
XLA Modules:
  0.0 277.4 jit_solution(2947576345908944588)
XLA Ops:
  0.7 1.7 copy-done.13
  2.3 2.6 shard_map.95
  6.1 4.3 %all-to-all-start = ((f16[8,512,128]{2,1,0:T(8,128)(2,1)}), f16[8,512,128]{2,1,0:T(8,128)(2,1)}, u32[]{:S(2)}, u32[]{:S(2)}) async-start(f16[8,512,128]{2,1,0:T(8,128)(2,1)} %convert_element_type.179), calls=%async_computation | async-start | bytes 2097152 | tf_op jit(solution)/shard_map/all_to_all | solution.py:497
  10.7 5.9 %fusion.13 = (bf16[1024,512]{1,0:T(8,128)(2,1)}, bf16[1024,512]{1,0:T(8,128)(2,1)}, bf16[1024,512]{1,0:T(8,128)(2,1)}, bf16[1024,512]{1,0:T(8,128)(2,1)}) fusion(s32[1024]{0:T(1024)S(1)} %get-tuple-element.103, s32[1024]{0:T(1024)S(1)} %get-tuple-element.102, s32[512]{0:T(512)S(1)} %add_and_fusion.1, s32[1024]{0:T(1024)S(1)} %get-tuple-element.101), kind=kLoop, calls=%fused_computation.34 | loop fusion | flops 29360128 | bytes 4208640 | tf_op jit(solution)/shard_map/convert_element_type | solution.py:78
  16.6 7.8 %all-to-all-done = f16[8,512,128]{2,1,0:T(8,128)(2,1)} async-done(((f16[8,512,128]{2,1,0:T(8,128)(2,1)}), f16[8,512,128]{2,1,0:T(8,128)(2,1)}, u32[]{:S(2)}, u32[]{:S(2)}) %all-to-all-start) | async-done | bytes 1048608 | tf_op jit(solution)/shard_map/all_to_all | solution.py:497
  24.3 1.5 convert_element_type.180.refs_0_
  26.2 2.0 shard_map.96
  32.3 1.5 collective-permute-start.1
  33.9 2.1 collective-permute-done.1
  36.6 9.2 %fusion.1 = (bf16[1024,1024]{1,0:T(8,128)(2,1)}, bf16[1024,1024]{1,0:T(8,128)(2,1)}, bf16[1024,1024]{1,0:T(8,128)(2,1)}, bf16[1024,1024]{1,0:T(8,128)(2,1)}) fusion(s32[1024]{0:T(1024)S(1)} %get-tuple-element.106, s32[1024]{0:T(1024)S(1)} %shift-right-arithmetic_and_fusion, s32[1024]{0:T(1024)S(1)} %get-tuple-element.107, s32[1024]{0:T(1024)S(1)} %get-tuple-element.100), kind=kLoop, calls=%fused_computation.5 | loop fusion | flops 62914560 | bytes 8404992 | tf_op jit(solution)/shard_map/convert_element_type | solution.py:78
  45.8 4.1 %collective-permute-start.10 = (f16[3,128,256]{2,1,0:T(8,128)(2,1)}, f16[3,128,256]{2,1,0:T(8,128)(2,1)S(1)}, u32[]{:S(2)}, u32[]{:S(2)}) collective-permute-start(f16[3,128,256]{2,1,0:T(8,128)(2,1)} %convert_element_type.188), channel_id=1, source_target_pairs={{0,3},{1,0},{2,1},{3,2},{4,7},{5,4},{6,5},{7,6},{8,11},{9,8},{10,9... | collective-permute-start | bytes 589832 | tf_op jit(solution)/shard_map/ppermute | solution.py:480
  51.8 3.7 %collective-permute-done.10 = f16[3,128,256]{2,1,0:T(8,128)(2,1)S(1)} collective-permute-done((f16[3,128,256]{2,1,0:T(8,128)(2,1)}, f16[3,128,256]{2,1,0:T(8,128)(2,1)S(1)}, u32[]{:S(2)}, u32[]{:S(2)}) %collective-permute-start.10) | collective-permute-done | bytes 196640 | tf_op jit(solution)/shard_map/ppermute | solution.py:480
  55.6 10.2 %collective-permute-done.11 = f16[3,128,256]{2,1,0:T(8,128)(2,1)S(1)} collective-permute-done((f16[3,128,256]{2,1,0:T(8,128)(2,1)}, f16[3,128,256]{2,1,0:T(8,128)(2,1)S(1)}, u32[]{:S(2)}, u32[]{:S(2)}) %collective-permute-start.11) | collective-permute-done | bytes 196640 | tf_op jit(solution)/shard_map/ppermute | solution.py:480
  65.9 1.6 copy-done.5
  67.5 6.5 %shard_map.99 = (f32[4,32,24,128]{3,2,1,0:T(8,128)S(1)}, f32[4,32,24,128]{3,2,1,0:T(8,128)S(1)}) custom-call(s32[256]{0:T(256)S(1)} %get-tuple-element.71.refs_0_.a_ref, s32[256]{0:T(256)S(1)} %get-tuple-element.95.refs_1_.b_ref, f32[3,128,256]{2,1,0:T(8,128)S(1)} %copy-done.16, f32[3,128,256]{2,1,0:T(8,128)S(1)} %convert_element_type.211.refs_3_, ...), custom_call_target="tpu_custom_call" | custom-call | tf_op jit(solution)/shard_map/pallas_call | solution.py:139
  75.6 2.8 shard_map.97
  78.7 2.5 collective-permute-start.4
  81.3 2.3 collective-permute-start.5
  83.6 4.0 %collective-permute-done.3 = f16[5,128,256]{2,1,0:T(8,128)(2,1)S(1)} collective-permute-done((f16[5,128,256]{2,1,0:T(8,128)(2,1)S(1)}, f16[5,128,256]{2,1,0:T(8,128)(2,1)S(1)}, u32[]{:S(2)}, u32[]{:S(2)}) %collective-permute-start.3) | collective-permute-done | bytes 327712 | tf_op jit(solution)/shard_map/ppermute | solution.py:480
  87.7 21.6 %collective-permute-done.4 = f16[5,128,256]{2,1,0:T(8,128)(2,1)S(1)} collective-permute-done((f16[5,128,256]{2,1,0:T(8,128)(2,1)S(1)}, f16[5,128,256]{2,1,0:T(8,128)(2,1)S(1)}, u32[]{:S(2)}, u32[]{:S(2)}) %collective-permute-start.4) | collective-permute-done | bytes 327712 | tf_op jit(solution)/shard_map/ppermute | solution.py:480
  109.4 8.6 %shard_map.98 = (f32[4,32,40,128]{3,2,1,0:T(8,128)S(1)}, f32[4,32,40,128]{3,2,1,0:T(8,128)S(1)}) custom-call(s32[256]{0:T(256)S(1)} %get-tuple-element.71.refs_0_.a_ref, s32[256]{0:T(256)S(1)} %get-tuple-element.95.refs_1_.b_ref, f32[5,128,256]{2,1,0:T(8,128)S(1)} %convert_convert_fusion.refs_2_, f32[5,128,256]{2,1,0:T(8,128)S(1)} %convert_element_type.192.refs_3_, ...), custom_call_target="tpu_custom_call" | custom-call | tf_op jit(solution)/shard_map/pallas_call | solution.py:139
  120.2 1.5 collective-permute-start.15
  122.7 3.9 %collective-permute-done.14 = f16[32,24,128]{2,1,0:T(8,128)(2,1)S(1)} collective-permute-done((f16[32,24,128]{2,1,0:T(8,128)(2,1)S(1)}, f16[32,24,128]{2,1,0:T(8,128)(2,1)S(1)}, u32[]{:S(2)}, u32[]{:S(2)}) %collective-permute-start.14) | collective-permute-done | bytes 196640 | tf_op jit(solution)/shard_map/ppermute | solution.py:477
  126.6 4.8 %collective-permute-done.15 = f16[32,24,128]{2,1,0:T(8,128)(2,1)S(1)} collective-permute-done((f16[32,24,128]{2,1,0:T(8,128)(2,1)S(1)}, f16[32,24,128]{2,1,0:T(8,128)(2,1)S(1)}, u32[]{:S(2)}, u32[]{:S(2)}) %collective-permute-start.15) | collective-permute-done | bytes 196640 | tf_op jit(solution)/shard_map/ppermute | solution.py:477
  136.4 6.4 %collective-permute-done.7 = f16[32,40,128]{2,1,0:T(8,128)(2,1)S(1)} collective-permute-done((f16[32,40,128]{2,1,0:T(8,128)(2,1)S(1)}, f16[32,40,128]{2,1,0:T(8,128)(2,1)S(1)}, u32[]{:S(2)}, u32[]{:S(2)}) %collective-permute-start.7) | collective-permute-done | bytes 327712 | tf_op jit(solution)/shard_map/ppermute | solution.py:477
  142.9 6.6 %collective-permute-done.8 = f16[32,40,128]{2,1,0:T(8,128)(2,1)S(1)} collective-permute-done((f16[32,40,128]{2,1,0:T(8,128)(2,1)S(1)}, f16[32,40,128]{2,1,0:T(8,128)(2,1)S(1)}, u32[]{:S(2)}, u32[]{:S(2)}) %collective-permute-start.8) | collective-permute-done | bytes 327712 | tf_op jit(solution)/shard_map/ppermute | solution.py:477
  152.1 1.5 collective-permute-start.18
  156.2 2.6 collective-permute-done.17.refs_1_
  158.7 2.9 %collective-permute-done.18.refs_2_ = bf16[32,24,128]{2,1,0:T(8,128)(2,1)S(1)} collective-permute-done((bf16[32,24,128]{2,1,0:T(8,128)(2,1)S(1)}, bf16[32,24,128]{2,1,0:T(8,128)(2,1)S(1)}, u32[]{:S(2)}, u32[]{:S(2)}) %collective-permute-start.18) | collective-permute-done | bytes 196640 | tf_op jit(solution)/shard_map/ppermute | solution.py:477
  163.4 1.7 collective-permute-start.22
  165.1 7.0 %collective-permute-done.20.refs_1_ = bf16[32,40,128]{2,1,0:T(8,128)(2,1)S(1)} collective-permute-done((bf16[32,40,128]{2,1,0:T(8,128)(2,1)S(1)}, bf16[32,40,128]{2,1,0:T(8,128)(2,1)S(1)}, u32[]{:S(2)}, u32[]{:S(2)}) %collective-permute-start.20) | collective-permute-done | bytes 327712 | tf_op jit(solution)/shard_map/ppermute | solution.py:477
  172.1 4.1 %collective-permute-done.21.refs_2_ = bf16[32,40,128]{2,1,0:T(8,128)(2,1)S(1)} collective-permute-done((bf16[32,40,128]{2,1,0:T(8,128)(2,1)S(1)}, bf16[32,40,128]{2,1,0:T(8,128)(2,1)S(1)}, u32[]{:S(2)}, u32[]{:S(2)}) %collective-permute-start.21) | collective-permute-done | bytes 327712 | tf_op jit(solution)/shard_map/ppermute | solution.py:477
  177.3 3.4 %collective-permute-done.27.refs_4_ = bf16[4,32,24,128]{3,2,1,0:T(8,128)(2,1)S(1)} collective-permute-done((bf16[4,32,24,128]{3,2,1,0:T(8,128)(2,1)S(1)}, bf16[4,32,24,128]{3,2,1,0:T(8,128)(2,1)S(1)}, u32[]{:S(2)}, u32[]{:S(2)}) %collective-permute-start.27) | collective-permute-done | bytes 786464 | tf_op jit(solution)/shard_map/ppermute | solution.py:477
  180.7 6.1 %shard_map.101 = (bf16[3,128,256]{2,1,0:T(8,128)(2,1)S(1)}, bf16[3,128,256]{2,1,0:T(8,128)(2,1)S(1)}, bf16[3,128,256]{2,1,0:T(8,128)(2,1)S(1)}, bf16[3,128,256]{2,1,0:T(8,128)(2,1)S(1)}) custom-call(s32[256]{0:T(256)S(1)} %get-tuple-element.71.refs_0_.a_ref, s32[256]{0:T(256)S(1)} %get-tuple-element.95.refs_1_.b_ref, ...), custom_call_target="tpu_custom_call" | custom-call | tf_op jit(solution)/shard_map/pallas_call | solution.py:139
  187.2 7.6 %shard_map.100 = (bf16[5,128,256]{2,1,0:T(8,128)(2,1)S(1)}, bf16[5,128,256]{2,1,0:T(8,128)(2,1)S(1)}, bf16[5,128,256]{2,1,0:T(8,128)(2,1)S(1)}, bf16[5,128,256]{2,1,0:T(8,128)(2,1)S(1)}) custom-call(s32[256]{0:T(256)S(1)} %get-tuple-element.71.refs_0_.a_ref, s32[256]{0:T(256)S(1)} %get-tuple-element.95.refs_1_.b_ref, ...), custom_call_target="tpu_custom_call" | custom-call | tf_op jit(solution)/shard_map/pallas_call | solution.py:139
  194.8 1.6 collective-permute-start.24
  196.5 1.9 collective-permute-start.25
  198.4 1.5 collective-permute-start.29
  199.9 2.8 %collective-permute-start.30 = (bf16[3,128,256]{2,1,0:T(8,128)(2,1)S(1)}, bf16[3,128,256]{2,1,0:T(8,128)(2,1)S(1)}, u32[]{:S(2)}, u32[]{:S(2)}) collective-permute-start(bf16[3,128,256]{2,1,0:T(8,128)(2,1)S(1)} %get-tuple-element.53), channel_id=1, source_target_pairs={{0,1},{1,2},{2,3},{3,0},{4,5},{5,6},{6,7},{7,4},{8,9},{9,10},{10,1... | collective-permute-start | bytes 589832 | tf_op jit(solution)/shard_map/ppermute | solution.py:480
  202.8 36.8 %collective-permute-done.29.refs_2_ = bf16[3,128,256]{2,1,0:T(8,128)(2,1)S(1)} collective-permute-done((bf16[3,128,256]{2,1,0:T(8,128)(2,1)S(1)}, bf16[3,128,256]{2,1,0:T(8,128)(2,1)S(1)}, u32[]{:S(2)}, u32[]{:S(2)}) %collective-permute-start.29) | collective-permute-done | bytes 196640 | tf_op jit(solution)/shard_map/ppermute | solution.py:480
  239.5 1.8 shard_map.102.refs_4_
  241.4 3.2 %shard_map.103 = bf16[8,512,128]{2,1,0:T(8,128)(2,1)S(1)} custom-call(bf16[5,128,256]{2,1,0:T(8,128)(2,1)S(1)} %get-tuple-element.46.refs_0_, bf16[5,128,256]{2,1,0:T(8,128)(2,1)S(1)} %collective-permute-done.24.refs_1_, bf16[5,128,256]{2,1,0:T(8,128)(2,1)S(1)} %collective-permute-done.25.refs_2_, bf16[5,128,256]{2,1,0:T(8,128)(2,1)S(1)} %collective-permute-done.26.refs_3_, ...), custom_call_target="tpu_custom_call" | custom-call | tf_op jit(solution)/shard_map/pallas_call | solution.py:139
  245.6 4.7 %all-to-all-start.1 = ((bf16[8,512,128]{2,1,0:T(8,128)(2,1)}), bf16[8,512,128]{2,1,0:T(8,128)(2,1)S(1)}, u32[]{:S(2)}, u32[]{:S(2)}) async-start(bf16[8,512,128]{2,1,0:T(8,128)(2,1)} %copy-done.15), calls=%async_computation.1 | async-start | bytes 2097152 | tf_op jit(solution)/shard_map/all_to_all | solution.py:560
  258.4 2.0 collective-permute-start.31
  260.4 3.7 %all-to-all-done.1.grad_ref = bf16[8,512,128]{2,1,0:T(8,128)(2,1)S(1)} async-done(((bf16[8,512,128]{2,1,0:T(8,128)(2,1)}), bf16[8,512,128]{2,1,0:T(8,128)(2,1)S(1)}, u32[]{:S(2)}, u32[]{:S(2)}) %all-to-all-start.1) | async-done | bytes 1048608 | tf_op jit(solution)/shard_map/all_to_all | solution.py:560
  264.6 2.0 collective-permute-start.32
  268.6 1.5 collective-permute-done.32
  270.2 7.3 %haar.1 = f32[512,1024]{1,0:T(8,128)} custom-call(f32[512,1024]{1,0:T(8,128)S(1)} %shard_map.104.refs_0_, f32[8,512]{1,0:T(8,128)S(1)} %sub.141.refs_1_, f32[8,512]{1,0:T(8,128)S(1)} %sub.142.refs_2_, f32[4,1152]{1,0:T(4,128)S(1)} %pad_maximum_fusion.6.refs_3_), custom_call_target="tpu_custom_call" | custom-call | tf_op jit(solution)/shard_map/haar/pallas_call | solution.py:444
  (148 shorter events, 30.9 us)
Async XLA Ops:
  0.6 121.7 %copy-start = (bf16[32,64,256]{2,1,0:T(8,128)(2,1)S(1)}, bf16[32,64,256]{2,1,0:T(8,128)(2,1)}, u32[]{:S(2)}) copy-start(bf16[32,64,256]{2,1,0:T(8,128)(2,1)} %param.10) | copy-start | bytes 3145732
  5.0 5.7 %copy-start.21 = (s32[32]{0:T(128)S(1)}, s32[32]{0:T(128)}, u32[]{:S(2)}) copy-start(s32[32]{0:T(128)} %param.13) | copy-start | bytes 388
  5.0 5.7 %copy-start.22 = (s32[32,1]{0,1:T(1,128)S(1)}, s32[32,1]{0,1:T(1,128)}, u32[]{:S(2)}) copy-start(s32[32,1]{0,1:T(1,128)} %param.12) | copy-start | bytes 388
  6.1 18.2 %all-to-all-start = ((f16[8,512,128]{2,1,0:T(8,128)(2,1)}), f16[8,512,128]{2,1,0:T(8,128)(2,1)}, u32[]{:S(2)}, u32[]{:S(2)}) async-start(f16[8,512,128]{2,1,0:T(8,128)(2,1)} %convert_element_type.179), calls=%async_computation | async-start | bytes 2097152 | tf_op jit(solution)/shard_map/all_to_all | solution.py:497
  31.1 1.2 collective-permute-start
  32.3 3.6 %collective-permute-start.1 = (s32[2,64]{1,0:T(2,128)S(1)}, s32[2,64]{1,0:T(2,128)S(1)}, u32[]{:S(2)}, u32[]{:S(2)}) collective-permute-start(s32[2,64]{1,0:T(2,128)S(1)} %pad_add_fusion.2), channel_id=1, source_target_pairs={{0,8},{4,12},{8,0},{12,4},{16,24},{20,28},{24,16},{28,20},{1,9},{5... | collective-permute-start | bytes 1544 | tf_op jit(solution)/shard_map/ppermute | solution.py:477
  36.0 14.9 %collective-permute-start.2 = (s32[2,128]{1,0:T(2,128)S(1)}, s32[2,128]{1,0:T(2,128)S(1)}, u32[]{:S(2)}, u32[]{:S(2)}) collective-permute-start(s32[2,128]{1,0:T(2,128)S(1)} %pad_add_fusion.3), channel_id=1, source_target_pairs={{0,16},{4,20},{8,24},{12,28},{16,0},{20,4},{24,8},{28,12},{1,17},{... | collective-permute-start | bytes 3080 | tf_op jit(solution)/shard_map/ppermute | solution.py:477
  45.8 20.1 %copy-start.4 = (bf16[1024,1024]{1,0:T(8,128)(2,1)S(1)}, bf16[1024,1024]{1,0:T(8,128)(2,1)}, u32[]{:S(2)}) copy-start(bf16[1024,1024]{1,0:T(8,128)(2,1)} %get-tuple-element.81.refs_7_) | copy-start | bytes 6291460
  45.8 20.1 %copy-start.16 = (f32[3,128,256]{2,1,0:T(8,128)S(1)}, f32[3,128,256]{2,1,0:T(8,128)}, u32[]{:S(2)}) copy-start(f32[3,128,256]{2,1,0:T(8,128)} %fusion.66) | copy-start | bytes 1179652
  45.8 9.7 %collective-permute-start.10 = (f16[3,128,256]{2,1,0:T(8,128)(2,1)}, f16[3,128,256]{2,1,0:T(8,128)(2,1)S(1)}, u32[]{:S(2)}, u32[]{:S(2)}) collective-permute-start(f16[3,128,256]{2,1,0:T(8,128)(2,1)} %convert_element_type.188), channel_id=1, source_target_pairs={{0,3},{1,0},{2,1},{3,2},{4,7},{5,4},{6,5},{7,6},{8,11},{9,8},{10,9... | collective-permute-start | bytes 589832 | tf_op jit(solution)/shard_map/ppermute | solution.py:480
  49.9 15.9 %collective-permute-start.11 = (f16[3,128,256]{2,1,0:T(8,128)(2,1)}, f16[3,128,256]{2,1,0:T(8,128)(2,1)S(1)}, u32[]{:S(2)}, u32[]{:S(2)}) collective-permute-start(f16[3,128,256]{2,1,0:T(8,128)(2,1)} %convert_element_type.187), channel_id=1, source_target_pairs={{0,2},{1,3},{2,0},{3,1},{4,6},{5,7},{6,4},{7,5},{8,10},{9,11},{10,... | collective-permute-start | bytes 589832 | tf_op jit(solution)/shard_map/ppermute | solution.py:480
  49.9 16.0 %collective-permute-start.12 = (f16[3,128,256]{2,1,0:T(8,128)(2,1)}, f16[3,128,256]{2,1,0:T(8,128)(2,1)S(1)}, u32[]{:S(2)}, u32[]{:S(2)}) collective-permute-start(f16[3,128,256]{2,1,0:T(8,128)(2,1)} %convert_element_type.186), channel_id=1, source_target_pairs={{0,1},{1,2},{2,3},{3,0},{4,5},{5,6},{6,7},{7,4},{8,9},{9,10},{10,1... | collective-permute-start | bytes 589832 | tf_op jit(solution)/shard_map/ppermute | solution.py:480
  74.1 44.2 %collective-permute-start.13 = (f16[4,32,24,128]{3,2,1,0:T(8,128)(2,1)S(1)}, f16[4,32,24,128]{3,2,1,0:T(8,128)(2,1)S(1)}, u32[]{:S(2)}, u32[]{:S(2)}) collective-permute-start(f16[4,32,24,128]{3,2,1,0:T(8,128)(2,1)S(1)} %convert_element_type.214), channel_id=1, source_target_pairs={{0,4},{4,0},{8,12},{12,8},{16,20},{20,16},{24,28},{28,24},{1,5},{5... | collective-permute-start | bytes 2359304 | tf_op jit(solution)/shard_map/ppermute | solution.py:477
  78.4 9.2 %collective-permute-start.3 = (f16[5,128,256]{2,1,0:T(8,128)(2,1)S(1)}, f16[5,128,256]{2,1,0:T(8,128)(2,1)S(1)}, u32[]{:S(2)}, u32[]{:S(2)}) collective-permute-start(f16[5,128,256]{2,1,0:T(8,128)(2,1)S(1)} %convert_element_type.191), channel_id=1, source_target_pairs={{0,3},{1,0},{2,1},{3,2},{4,7},{5,4},{6,5},{7,6},{8,11},{9,8},{10,9... | collective-permute-start | bytes 983048 | tf_op jit(solution)/shard_map/ppermute | solution.py:480
  78.7 30.6 %collective-permute-start.4 = (f16[5,128,256]{2,1,0:T(8,128)(2,1)S(1)}, f16[5,128,256]{2,1,0:T(8,128)(2,1)S(1)}, u32[]{:S(2)}, u32[]{:S(2)}) collective-permute-start(f16[5,128,256]{2,1,0:T(8,128)(2,1)S(1)} %convert_element_type.193), channel_id=1, source_target_pairs={{0,2},{1,3},{2,0},{3,1},{4,6},{5,7},{6,4},{7,5},{8,10},{9,11},{10,... | collective-permute-start | bytes 983048 | tf_op jit(solution)/shard_map/ppermute | solution.py:480
  81.3 28.1 %collective-permute-start.5 = (f16[5,128,256]{2,1,0:T(8,128)(2,1)S(1)}, f16[5,128,256]{2,1,0:T(8,128)(2,1)S(1)}, u32[]{:S(2)}, u32[]{:S(2)}) collective-permute-start(f16[5,128,256]{2,1,0:T(8,128)(2,1)S(1)} %convert_element_type.195), channel_id=1, source_target_pairs={{0,1},{1,2},{2,3},{3,0},{4,5},{5,6},{6,7},{7,4},{8,9},{9,10},{10,1... | collective-permute-start | bytes 983048 | tf_op jit(solution)/shard_map/ppermute | solution.py:480
  83.5 25.9 %copy-start.6 = (bf16[1024,1024]{1,0:T(8,128)(2,1)S(1)}, bf16[1024,1024]{1,0:T(8,128)(2,1)}, u32[]{:S(2)}) copy-start(bf16[1024,1024]{1,0:T(8,128)(2,1)} %get-tuple-element.83.refs_6_) | copy-start | bytes 6291460
  118.3 13.3 %collective-permute-start.6 = (f16[4,32,40,128]{3,2,1,0:T(8,128)(2,1)S(1)}, f16[4,32,40,128]{3,2,1,0:T(8,128)(2,1)S(1)}, u32[]{:S(2)}, u32[]{:S(2)}) collective-permute-start(f16[4,32,40,128]{3,2,1,0:T(8,128)(2,1)S(1)} %convert_element_type.201), channel_id=1, source_target_pairs={{0,4},{4,0},{8,12},{12,8},{16,20},{20,16},{24,28},{28,24},{1,5},{5... | collective-permute-start | bytes 3932168 | tf_op jit(solution)/shard_map/ppermute | solution.py:477
  118.8 7.8 %collective-permute-start.14 = (f16[32,24,128]{2,1,0:T(8,128)(2,1)S(1)}, f16[32,24,128]{2,1,0:T(8,128)(2,1)S(1)}, u32[]{:S(2)}, u32[]{:S(2)}) collective-permute-start(f16[32,24,128]{2,1,0:T(8,128)(2,1)S(1)} %get-tuple-element.75), channel_id=1, source_target_pairs={{0,8},{4,12},{8,0},{12,4},{16,24},{20,28},{24,16},{28,20},{1,9},{5... | collective-permute-start | bytes 589832 | tf_op jit(solution)/shard_map/ppermute | solution.py:477
  120.2 11.2 %collective-permute-start.15 = (f16[32,24,128]{2,1,0:T(8,128)(2,1)S(1)}, f16[32,24,128]{2,1,0:T(8,128)(2,1)S(1)}, u32[]{:S(2)}, u32[]{:S(2)}) collective-permute-start(f16[32,24,128]{2,1,0:T(8,128)(2,1)S(1)} %get-tuple-element.77), channel_id=1, source_target_pairs={{0,16},{4,20},{8,24},{12,28},{16,0},{20,4},{24,8},{28,12},{1,17},{... | collective-permute-start | bytes 589832 | tf_op jit(solution)/shard_map/ppermute | solution.py:477
  121.8 9.7 %collective-permute-start.16 = (f16[32,24,128]{2,1,0:T(8,128)(2,1)S(1)}, f16[32,24,128]{2,1,0:T(8,128)(2,1)S(1)}, u32[]{:S(2)}, u32[]{:S(2)}) collective-permute-start(f16[32,24,128]{2,1,0:T(8,128)(2,1)S(1)} %get-tuple-element.76), channel_id=1, source_target_pairs={{0,24},{4,28},{8,16},{12,20},{16,8},{20,12},{24,0},{28,4},{1,25},{... | collective-permute-start | bytes 589832 | tf_op jit(solution)/shard_map/ppermute | solution.py:477
  132.2 10.6 %collective-permute-start.7 = (f16[32,40,128]{2,1,0:T(8,128)(2,1)S(1)}, f16[32,40,128]{2,1,0:T(8,128)(2,1)S(1)}, u32[]{:S(2)}, u32[]{:S(2)}) collective-permute-start(f16[32,40,128]{2,1,0:T(8,128)(2,1)S(1)} %get-tuple-element.72), channel_id=1, source_target_pairs={{0,8},{4,12},{8,0},{12,4},{16,24},{20,28},{24,16},{28,20},{1,9},{5... | collective-permute-start | bytes 983048 | tf_op jit(solution)/shard_map/ppermute | solution.py:477
  133.5 16.0 %collective-permute-start.8 = (f16[32,40,128]{2,1,0:T(8,128)(2,1)S(1)}, f16[32,40,128]{2,1,0:T(8,128)(2,1)S(1)}, u32[]{:S(2)}, u32[]{:S(2)}) collective-permute-start(f16[32,40,128]{2,1,0:T(8,128)(2,1)S(1)} %get-tuple-element.74), channel_id=1, source_target_pairs={{0,16},{4,20},{8,24},{12,28},{16,0},{20,4},{24,8},{28,12},{1,17},{... | collective-permute-start | bytes 983048 | tf_op jit(solution)/shard_map/ppermute | solution.py:477
  134.3 15.2 %collective-permute-start.9 = (f16[32,40,128]{2,1,0:T(8,128)(2,1)S(1)}, f16[32,40,128]{2,1,0:T(8,128)(2,1)S(1)}, u32[]{:S(2)}, u32[]{:S(2)}) collective-permute-start(f16[32,40,128]{2,1,0:T(8,128)(2,1)S(1)} %get-tuple-element.73), channel_id=1, source_target_pairs={{0,24},{4,28},{8,16},{12,20},{16,8},{20,12},{24,0},{28,4},{1,25},{... | collective-permute-start | bytes 983048 | tf_op jit(solution)/shard_map/ppermute | solution.py:477
  151.5 7.2 %collective-permute-start.17 = (bf16[32,24,128]{2,1,0:T(8,128)(2,1)S(1)}, bf16[32,24,128]{2,1,0:T(8,128)(2,1)S(1)}, u32[]{:S(2)}, u32[]{:S(2)}) collective-permute-start(bf16[32,24,128]{2,1,0:T(8,128)(2,1)S(1)} %pad_maximum_fusion.3.refs_0_), channel_id=1, source_target_pairs={{0,8},{4,12},{8,0},{12,4},{16,24},{20,28},{24,16},{28,20},{1,9},{5... | collective-permute-start | bytes 589832 | tf_op jit(solution)/shard_map/ppermute | solution.py:477
  152.1 9.5 %collective-permute-start.18 = (bf16[32,24,128]{2,1,0:T(8,128)(2,1)S(1)}, bf16[32,24,128]{2,1,0:T(8,128)(2,1)S(1)}, u32[]{:S(2)}, u32[]{:S(2)}) collective-permute-start(bf16[32,24,128]{2,1,0:T(8,128)(2,1)S(1)} %pad_maximum_fusion.3.refs_0_), channel_id=1, source_target_pairs={{0,16},{4,20},{8,24},{12,28},{16,0},{20,4},{24,8},{28,12},{1,17},{... | collective-permute-start | bytes 589832 | tf_op jit(solution)/shard_map/ppermute | solution.py:477
  153.6 8.1 %collective-permute-start.19 = (bf16[32,24,128]{2,1,0:T(8,128)(2,1)S(1)}, bf16[32,24,128]{2,1,0:T(8,128)(2,1)S(1)}, u32[]{:S(2)}, u32[]{:S(2)}) collective-permute-start(bf16[32,24,128]{2,1,0:T(8,128)(2,1)S(1)} %pad_maximum_fusion.3.refs_0_), channel_id=1, source_target_pairs={{0,24},{4,28},{8,16},{12,20},{16,8},{20,12},{24,0},{28,4},{1,25},{... | collective-permute-start | bytes 589832 | tf_op jit(solution)/shard_map/ppermute | solution.py:477
  161.7 10.5 %collective-permute-start.20 = (bf16[32,40,128]{2,1,0:T(8,128)(2,1)S(1)}, bf16[32,40,128]{2,1,0:T(8,128)(2,1)S(1)}, u32[]{:S(2)}, u32[]{:S(2)}) collective-permute-start(bf16[32,40,128]{2,1,0:T(8,128)(2,1)S(1)} %pad_maximum_fusion.2.refs_0_), channel_id=1, source_target_pairs={{0,8},{4,12},{8,0},{12,4},{16,24},{20,28},{24,16},{28,20},{1,9},{5... | collective-permute-start | bytes 983048 | tf_op jit(solution)/shard_map/ppermute | solution.py:477
  162.9 13.4 %collective-permute-start.21 = (bf16[32,40,128]{2,1,0:T(8,128)(2,1)S(1)}, bf16[32,40,128]{2,1,0:T(8,128)(2,1)S(1)}, u32[]{:S(2)}, u32[]{:S(2)}) collective-permute-start(bf16[32,40,128]{2,1,0:T(8,128)(2,1)S(1)} %pad_maximum_fusion.2.refs_0_), channel_id=1, source_target_pairs={{0,16},{4,20},{8,24},{12,28},{16,0},{20,4},{24,8},{28,12},{1,17},{... | collective-permute-start | bytes 983048 | tf_op jit(solution)/shard_map/ppermute | solution.py:477
  163.4 12.9 %collective-permute-start.22 = (bf16[32,40,128]{2,1,0:T(8,128)(2,1)S(1)}, bf16[32,40,128]{2,1,0:T(8,128)(2,1)S(1)}, u32[]{:S(2)}, u32[]{:S(2)}) collective-permute-start(bf16[32,40,128]{2,1,0:T(8,128)(2,1)S(1)} %pad_maximum_fusion.2.refs_0_), channel_id=1, source_target_pairs={{0,24},{4,28},{8,16},{12,20},{16,8},{20,12},{24,0},{28,4},{1,25},{... | collective-permute-start | bytes 983048 | tf_op jit(solution)/shard_map/ppermute | solution.py:477
  176.5 10.7 %collective-permute-start.23 = (bf16[4,32,40,128]{3,2,1,0:T(8,128)(2,1)S(1)}, bf16[4,32,40,128]{3,2,1,0:T(8,128)(2,1)S(1)}, u32[]{:S(2)}, u32[]{:S(2)}) collective-permute-start(bf16[4,32,40,128]{3,2,1,0:T(8,128)(2,1)S(1)} %pad_maximum_fusion), channel_id=1, source_target_pairs={{0,4},{4,0},{8,12},{12,8},{16,20},{20,16},{24,28},{28,24},{1,5},{5... | collective-permute-start | bytes 3932168 | tf_op jit(solution)/shard_map/ppermute | solution.py:477
  176.7 4.0 %collective-permute-start.27 = (bf16[4,32,24,128]{3,2,1,0:T(8,128)(2,1)S(1)}, bf16[4,32,24,128]{3,2,1,0:T(8,128)(2,1)S(1)}, u32[]{:S(2)}, u32[]{:S(2)}) collective-permute-start(bf16[4,32,24,128]{3,2,1,0:T(8,128)(2,1)S(1)} %pad_maximum_fusion.1), channel_id=1, source_target_pairs={{0,4},{4,0},{8,12},{12,8},{16,20},{20,16},{24,28},{28,24},{1,5},{5... | collective-permute-start | bytes 2359304 | tf_op jit(solution)/shard_map/ppermute | solution.py:477
  186.8 52.7 %copy-start.11 = (bf16[1024,512]{1,0:T(8,128)(2,1)S(1)}, bf16[1024,512]{1,0:T(8,128)(2,1)}, u32[]{:S(2)}) copy-start(bf16[1024,512]{1,0:T(8,128)(2,1)} %get-tuple-element.84.refs_5_.refs_6_) | copy-start | bytes 3145732
  186.9 52.7 %copy-start.12 = (bf16[1024,512]{1,0:T(8,128)(2,1)S(1)}, bf16[1024,512]{1,0:T(8,128)(2,1)}, u32[]{:S(2)}) copy-start(bf16[1024,512]{1,0:T(8,128)(2,1)} %get-tuple-element.85.refs_4_.refs_5_) | copy-start | bytes 3145732
  186.9 13.0 %collective-permute-start.28 = (bf16[3,128,256]{2,1,0:T(8,128)(2,1)S(1)}, bf16[3,128,256]{2,1,0:T(8,128)(2,1)S(1)}, u32[]{:S(2)}, u32[]{:S(2)}) collective-permute-start(bf16[3,128,256]{2,1,0:T(8,128)(2,1)S(1)} %get-tuple-element.51), channel_id=1, source_target_pairs={{0,3},{1,0},{2,1},{3,2},{4,7},{5,4},{6,5},{7,6},{8,11},{9,8},{10,9... | collective-permute-start | bytes 589832 | tf_op jit(solution)/shard_map/ppermute | solution.py:480
  194.8 46.5 %collective-permute-start.24 = (bf16[5,128,256]{2,1,0:T(8,128)(2,1)S(1)}, bf16[5,128,256]{2,1,0:T(8,128)(2,1)S(1)}, u32[]{:S(2)}, u32[]{:S(2)}) collective-permute-start(bf16[5,128,256]{2,1,0:T(8,128)(2,1)S(1)} %get-tuple-element.47), channel_id=1, source_target_pairs={{0,3},{1,0},{2,1},{3,2},{4,7},{5,4},{6,5},{7,6},{8,11},{9,8},{10,9... | collective-permute-start | bytes 983048 | tf_op jit(solution)/shard_map/ppermute | solution.py:480
  196.5 44.9 %collective-permute-start.25 = (bf16[5,128,256]{2,1,0:T(8,128)(2,1)S(1)}, bf16[5,128,256]{2,1,0:T(8,128)(2,1)S(1)}, u32[]{:S(2)}, u32[]{:S(2)}) collective-permute-start(bf16[5,128,256]{2,1,0:T(8,128)(2,1)S(1)} %get-tuple-element.48), channel_id=1, source_target_pairs={{0,2},{1,3},{2,0},{3,1},{4,6},{5,7},{6,4},{7,5},{8,10},{9,11},{10,... | collective-permute-start | bytes 983048 | tf_op jit(solution)/shard_map/ppermute | solution.py:480
  198.4 43.0 %collective-permute-start.26 = (bf16[5,128,256]{2,1,0:T(8,128)(2,1)S(1)}, bf16[5,128,256]{2,1,0:T(8,128)(2,1)S(1)}, u32[]{:S(2)}, u32[]{:S(2)}) collective-permute-start(bf16[5,128,256]{2,1,0:T(8,128)(2,1)S(1)} %get-tuple-element.49), channel_id=1, source_target_pairs={{0,1},{1,2},{2,3},{3,0},{4,5},{5,6},{6,7},{7,4},{8,9},{9,10},{10,1... | collective-permute-start | bytes 983048 | tf_op jit(solution)/shard_map/ppermute | solution.py:480
  198.4 41.1 %collective-permute-start.29 = (bf16[3,128,256]{2,1,0:T(8,128)(2,1)S(1)}, bf16[3,128,256]{2,1,0:T(8,128)(2,1)S(1)}, u32[]{:S(2)}, u32[]{:S(2)}) collective-permute-start(bf16[3,128,256]{2,1,0:T(8,128)(2,1)S(1)} %get-tuple-element.52), channel_id=1, source_target_pairs={{0,2},{1,3},{2,0},{3,1},{4,6},{5,7},{6,4},{7,5},{8,10},{9,11},{10,... | collective-permute-start | bytes 589832 | tf_op jit(solution)/shard_map/ppermute | solution.py:480
  199.9 39.6 %collective-permute-start.30 = (bf16[3,128,256]{2,1,0:T(8,128)(2,1)S(1)}, bf16[3,128,256]{2,1,0:T(8,128)(2,1)S(1)}, u32[]{:S(2)}, u32[]{:S(2)}) collective-permute-start(bf16[3,128,256]{2,1,0:T(8,128)(2,1)S(1)} %get-tuple-element.53), channel_id=1, source_target_pairs={{0,1},{1,2},{2,3},{3,0},{4,5},{5,6},{6,7},{7,4},{8,9},{9,10},{10,1... | collective-permute-start | bytes 589832 | tf_op jit(solution)/shard_map/ppermute | solution.py:480
  241.4 8.9 %copy-start.20 = (f32[4]{0:T(128)S(1)}, f32[4]{0:T(128)}, u32[]{:S(2)}) copy-start(f32[4]{0:T(128)} %param.14) | copy-start | bytes 52
  245.6 21.8 %copy-start.14 = (f32[512,1024]{1,0:T(8,128)S(1)}, f32[512,1024]{1,0:T(8,128)}, u32[]{:S(2)}) copy-start(f32[512,1024]{1,0:T(8,128)} %image_ref.3) | copy-start | bytes 6291460
  245.6 18.6 %all-to-all-start.1 = ((bf16[8,512,128]{2,1,0:T(8,128)(2,1)}), bf16[8,512,128]{2,1,0:T(8,128)(2,1)S(1)}, u32[]{:S(2)}, u32[]{:S(2)}) async-start(bf16[8,512,128]{2,1,0:T(8,128)(2,1)} %copy-done.15), calls=%async_computation.1 | async-start | bytes 2097152 | tf_op jit(solution)/shard_map/all_to_all | solution.py:560
  258.4 10.2 %collective-permute-start.33 = (f32[8,512]{1,0:T(8,128)S(1)}, f32[8,512]{1,0:T(8,128)S(1)}, u32[]{:S(2)}, u32[]{:S(2)}) collective-permute-start(f32[8,512]{1,0:T(8,128)S(1)} %get-tuple-element.58), channel_id=1, source_target_pairs={{0,3},{1,0},{2,1},{3,2},{4,7},{5,4},{6,5},{7,6},{8,11},{9,8},{10,9... | collective-permute-start | bytes 49160 | tf_op jit(solution)/shard_map/ppermute | solution.py:480
  258.4 10.2 %collective-permute-start.31 = (f32[8,512]{1,0:T(8,128)S(1)}, f32[8,512]{1,0:T(8,128)S(1)}, u32[]{:S(2)}, u32[]{:S(2)}) collective-permute-start(f32[8,512]{1,0:T(8,128)S(1)} %get-tuple-element.56), channel_id=1, source_target_pairs={{0,1},{1,2},{2,3},{3,0},{4,5},{5,6},{6,7},{7,4},{8,9},{9,10},{10,1... | collective-permute-start | bytes 49160 | tf_op jit(solution)/shard_map/ppermute | solution.py:480
  264.5 4.1 %collective-permute-start.34 = (f32[8,512]{1,0:T(8,128)S(1)}, f32[8,512]{1,0:T(8,128)S(1)}, u32[]{:S(2)}, u32[]{:S(2)}) collective-permute-start(f32[8,512]{1,0:T(8,128)S(1)} %get-tuple-element.59), channel_id=1, source_target_pairs={{0,3},{1,0},{2,1},{3,2},{4,7},{5,4},{6,5},{7,6},{8,11},{9,8},{10,9... | collective-permute-start | bytes 49160 | tf_op jit(solution)/shard_map/ppermute | solution.py:480
  264.6 5.6 %collective-permute-start.32 = (f32[8,512]{1,0:T(8,128)S(1)}, f32[8,512]{1,0:T(8,128)S(1)}, u32[]{:S(2)}, u32[]{:S(2)}) collective-permute-start(f32[8,512]{1,0:T(8,128)S(1)} %get-tuple-element.57), channel_id=1, source_target_pairs={{0,1},{1,2},{2,3},{3,0},{4,5},{5,6},{6,7},{7,4},{8,9},{9,10},{10,1... | collective-permute-start | bytes 49160 | tf_op jit(solution)/shard_map/ppermute | solution.py:480
  270.2 7.3 %copy-start.1 = (bf16[32,64,256]{2,1,0:T(8,128)(2,1)S(1)}, bf16[32,64,256]{2,1,0:T(8,128)(2,1)}, u32[]{:S(2)}) copy-start(bf16[32,64,256]{2,1,0:T(8,128)(2,1)} %param.10) | copy-start | bytes 3145732
  (12 other events, 27.8 us)

commit v3 on v2

--- a/solution.py
+++ b/solution.py
@@ -131,6 +131,7 @@
 
 
 AT_ONCE = 8
+SHARES_AT_ONCE = 16
 HALVES = ((0, 1, 7, 2, 6), (4, 3, 5))
 ORDER = HALVES[0] + HALVES[1]
 
@@ -232,10 +233,10 @@
         z_ref[a + 1] = z[:, wide:].reshape(groups, part, wide)
     for core, out_ref in ((1, far_ref), (0, near_ref)):
 
-        @pl.loop(0, 4 * blocks // AT_ONCE)
+        @pl.loop(0, 4 * blocks // SHARES_AT_ONCE)
         def _(step):
-            chip, first = step // (blocks // AT_ONCE), step % (blocks // AT_ONCE) * AT_ONCE
-            for i in range(AT_ONCE):
+            chip, first = step // (blocks // SHARES_AT_ONCE), step % (blocks // SHARES_AT_ONCE) * SHARES_AT_ONCE
+            for i in range(SHARES_AT_ONCE):
                 at = first + i
                 n = (2 * chip + core) * blocks + at
                 start = pl.multiple_of(b_ref[n] * low, low)

time: 280 us -> 278 us (level)
  no operation moved by 1% of the time
where the time goes in v3:
time: 278 us; the launch traced here: 275 us
  waiting for transfers between devices  134 us (48%)
  starting transfers between devices  48.6 us (17%)
  Pallas kernels  47.8 us (17%)
  other arithmetic  24.3 us (9%)
  between operations  8.73 us (3%)
  local copies, waits for them, and re-layouts  7.59 us (3%)
  matrix products  3.55 us (1%)
    ppermute x16, waiting for transfers between devices, ahead(): return lax.ppermute(x, 'wav', [(i, (i + by) % wavs) for i in range(wavs)])  77.9 us
    ppermute x19, waiting for transfers between devices, flip(): return lax.ppermute(x, 'vis', [(i, i ^ mask) for i in range(vis)])  45 us
    pallas_call x11, Pallas kernels, call(): pl.pallas_call(kernel, in_specs=[pl.BlockSpec(memory_space=pltpu.SMEM)] *...  40.6 us
    ppermute x16, starting transfers between devices, ahead(): return lax.ppermute(x, 'wav', [(i, (i + by) % wavs) for i in range(wavs)])  22.5 us
    ppermute x19, starting transfers between devices, flip(): return lax.ppermute(x, 'vis', [(i, i ^ mask) for i in range(vis)])  17.1 us
    convert_element_type x2, other arithmetic, split(): return (high.astype(BF16), (x - high).astype(BF16))  15.1 us
    all_to_all x1, waiting for transfers between devices, shards_fast(): x = lax.all_to_all(x, 'vis', split_axis=0, concat_axis=0, tiled=True)  7.78 us
    pallas_call x1, Pallas kernels, haar_mean(): pl.pallas_call(lambda *refs: haar_kernel(*refs, bases=bases), grid=(rows...  7.25 us
  transfers between devices with their start and end apart: 37, of which 19 were waited for; matrix products, arithmetic and copies ran while one was open for 8% of the time, Pallas kernels for 10%

profile of v3, /device:TPU:2, one launch (start us, length us, event | category | flops | bytes accessed | tf_op | source)
XLA Modules:
  0.0 275.0 jit_solution(7762353853720222147)
XLA Ops:
  0.7 1.7 copy-done.13
  2.3 2.6 shard_map.95
  6.1 4.3 %all-to-all-start = ((f16[8,512,128]{2,1,0:T(8,128)(2,1)}), f16[8,512,128]{2,1,0:T(8,128)(2,1)}, u32[]{:S(2)}, u32[]{:S(2)}) async-start(f16[8,512,128]{2,1,0:T(8,128)(2,1)} %convert_element_type.179), calls=%async_computation | async-start | bytes 2097152 | tf_op jit(solution)/shard_map/all_to_all | solution.py:498
  10.7 5.9 %fusion.13 = (bf16[1024,512]{1,0:T(8,128)(2,1)}, bf16[1024,512]{1,0:T(8,128)(2,1)}, bf16[1024,512]{1,0:T(8,128)(2,1)}, bf16[1024,512]{1,0:T(8,128)(2,1)}) fusion(s32[1024]{0:T(1024)S(1)} %get-tuple-element.103, s32[1024]{0:T(1024)S(1)} %get-tuple-element.102, s32[512]{0:T(512)S(1)} %add_and_fusion.1, s32[1024]{0:T(1024)S(1)} %get-tuple-element.101), kind=kLoop, calls=%fused_computation.34 | loop fusion | flops 29360128 | bytes 4208640 | tf_op jit(solution)/shard_map/convert_element_type | solution.py:78
  16.6 7.8 %all-to-all-done = f16[8,512,128]{2,1,0:T(8,128)(2,1)} async-done(((f16[8,512,128]{2,1,0:T(8,128)(2,1)}), f16[8,512,128]{2,1,0:T(8,128)(2,1)}, u32[]{:S(2)}, u32[]{:S(2)}) %all-to-all-start) | async-done | bytes 1048608 | tf_op jit(solution)/shard_map/all_to_all | solution.py:498
  24.3 1.5 convert_element_type.180.refs_0_
  26.2 2.0 shard_map.96
  32.3 1.5 collective-permute-start.1
  33.9 2.1 collective-permute-done.1
  36.6 9.2 %fusion.1 = (bf16[1024,1024]{1,0:T(8,128)(2,1)}, bf16[1024,1024]{1,0:T(8,128)(2,1)}, bf16[1024,1024]{1,0:T(8,128)(2,1)}, bf16[1024,1024]{1,0:T(8,128)(2,1)}) fusion(s32[1024]{0:T(1024)S(1)} %get-tuple-element.106, s32[1024]{0:T(1024)S(1)} %shift-right-arithmetic_and_fusion, s32[1024]{0:T(1024)S(1)} %get-tuple-element.107, s32[1024]{0:T(1024)S(1)} %get-tuple-element.100), kind=kLoop, calls=%fused_computation.5 | loop fusion | flops 62914560 | bytes 8404992 | tf_op jit(solution)/shard_map/convert_element_type | solution.py:78
  45.8 4.1 %collective-permute-start.10 = (f16[3,128,256]{2,1,0:T(8,128)(2,1)}, f16[3,128,256]{2,1,0:T(8,128)(2,1)S(1)}, u32[]{:S(2)}, u32[]{:S(2)}) collective-permute-start(f16[3,128,256]{2,1,0:T(8,128)(2,1)} %convert_element_type.188), channel_id=1, source_target_pairs={{0,3},{1,0},{2,1},{3,2},{4,7},{5,4},{6,5},{7,6},{8,11},{9,8},{10,9... | collective-permute-start | bytes 589832 | tf_op jit(solution)/shard_map/ppermute | solution.py:481
  51.8 3.7 %collective-permute-done.10 = f16[3,128,256]{2,1,0:T(8,128)(2,1)S(1)} collective-permute-done((f16[3,128,256]{2,1,0:T(8,128)(2,1)}, f16[3,128,256]{2,1,0:T(8,128)(2,1)S(1)}, u32[]{:S(2)}, u32[]{:S(2)}) %collective-permute-start.10) | collective-permute-done | bytes 196640 | tf_op jit(solution)/shard_map/ppermute | solution.py:481
  55.6 10.2 %collective-permute-done.11 = f16[3,128,256]{2,1,0:T(8,128)(2,1)S(1)} collective-permute-done((f16[3,128,256]{2,1,0:T(8,128)(2,1)}, f16[3,128,256]{2,1,0:T(8,128)(2,1)S(1)}, u32[]{:S(2)}, u32[]{:S(2)}) %collective-permute-start.11) | collective-permute-done | bytes 196640 | tf_op jit(solution)/shard_map/ppermute | solution.py:481
  65.9 1.6 copy-done.5
  67.5 5.2 %shard_map.99 = (f32[4,32,24,128]{3,2,1,0:T(8,128)S(1)}, f32[4,32,24,128]{3,2,1,0:T(8,128)S(1)}) custom-call(s32[256]{0:T(256)S(1)} %get-tuple-element.71.refs_0_.a_ref, s32[256]{0:T(256)S(1)} %get-tuple-element.95.refs_1_.b_ref, f32[3,128,256]{2,1,0:T(8,128)S(1)} %copy-done.16, f32[3,128,256]{2,1,0:T(8,128)S(1)} %convert_element_type.211.refs_3_, ...), custom_call_target="tpu_custom_call" | custom-call | tf_op jit(solution)/shard_map/pallas_call | solution.py:140
  74.3 2.8 %shard_map.97 = (f32[5,128,256]{2,1,0:T(8,128)S(1)}, f32[5,128,256]{2,1,0:T(8,128)S(1)}, f32[5,128,256]{2,1,0:T(8,128)S(1)}, f32[5,128,256]{2,1,0:T(8,128)S(1)}) custom-call(f32[8,512,128]{2,1,0:T(8,128)S(1)} %convert_element_type.180.refs_0_, bf16[1024,512]{1,0:T(8,128)(2,1)S(1)} %copy-done.8, bf16[1024,512]{1,0:T(8,128)(2,1)S(1)} %copy-done.10, ...), custom_call_target="tpu_custom_call" | custom-call | tf_op jit(solution)/shard_map/pallas_call | solution.py:140
  77.4 2.5 collective-permute-start.4
  80.0 2.3 collective-permute-start.5
  82.3 4.0 %collective-permute-done.3 = f16[5,128,256]{2,1,0:T(8,128)(2,1)S(1)} collective-permute-done((f16[5,128,256]{2,1,0:T(8,128)(2,1)S(1)}, f16[5,128,256]{2,1,0:T(8,128)(2,1)S(1)}, u32[]{:S(2)}, u32[]{:S(2)}) %collective-permute-start.3) | collective-permute-done | bytes 327712 | tf_op jit(solution)/shard_map/ppermute | solution.py:481
  86.4 21.6 %collective-permute-done.4 = f16[5,128,256]{2,1,0:T(8,128)(2,1)S(1)} collective-permute-done((f16[5,128,256]{2,1,0:T(8,128)(2,1)S(1)}, f16[5,128,256]{2,1,0:T(8,128)(2,1)S(1)}, u32[]{:S(2)}, u32[]{:S(2)}) %collective-permute-start.4) | collective-permute-done | bytes 327712 | tf_op jit(solution)/shard_map/ppermute | solution.py:481
  108.2 7.5 %shard_map.98 = (f32[4,32,40,128]{3,2,1,0:T(8,128)S(1)}, f32[4,32,40,128]{3,2,1,0:T(8,128)S(1)}) custom-call(s32[256]{0:T(256)S(1)} %get-tuple-element.71.refs_0_.a_ref, s32[256]{0:T(256)S(1)} %get-tuple-element.95.refs_1_.b_ref, f32[5,128,256]{2,1,0:T(8,128)S(1)} %convert_convert_fusion.refs_2_, f32[5,128,256]{2,1,0:T(8,128)S(1)} %convert_element_type.192.refs_3_, ...), custom_call_target="tpu_custom_call" | custom-call | tf_op jit(solution)/shard_map/pallas_call | solution.py:140
  117.8 1.5 collective-permute-start.15
  120.4 3.9 %collective-permute-done.14 = f16[32,24,128]{2,1,0:T(8,128)(2,1)S(1)} collective-permute-done((f16[32,24,128]{2,1,0:T(8,128)(2,1)S(1)}, f16[32,24,128]{2,1,0:T(8,128)(2,1)S(1)}, u32[]{:S(2)}, u32[]{:S(2)}) %collective-permute-start.14) | collective-permute-done | bytes 196640 | tf_op jit(solution)/shard_map/ppermute | solution.py:478
  124.2 4.8 %collective-permute-done.15 = f16[32,24,128]{2,1,0:T(8,128)(2,1)S(1)} collective-permute-done((f16[32,24,128]{2,1,0:T(8,128)(2,1)S(1)}, f16[32,24,128]{2,1,0:T(8,128)(2,1)S(1)}, u32[]{:S(2)}, u32[]{:S(2)}) %collective-permute-start.15) | collective-permute-done | bytes 196640 | tf_op jit(solution)/shard_map/ppermute | solution.py:478
  134.0 6.4 %collective-permute-done.7 = f16[32,40,128]{2,1,0:T(8,128)(2,1)S(1)} collective-permute-done((f16[32,40,128]{2,1,0:T(8,128)(2,1)S(1)}, f16[32,40,128]{2,1,0:T(8,128)(2,1)S(1)}, u32[]{:S(2)}, u32[]{:S(2)}) %collective-permute-start.7) | collective-permute-done | bytes 327712 | tf_op jit(solution)/shard_map/ppermute | solution.py:478
  140.5 6.6 %collective-permute-done.8 = f16[32,40,128]{2,1,0:T(8,128)(2,1)S(1)} collective-permute-done((f16[32,40,128]{2,1,0:T(8,128)(2,1)S(1)}, f16[32,40,128]{2,1,0:T(8,128)(2,1)S(1)}, u32[]{:S(2)}, u32[]{:S(2)}) %collective-permute-start.8) | collective-permute-done | bytes 327712 | tf_op jit(solution)/shard_map/ppermute | solution.py:478
  149.7 1.5 collective-permute-start.18
  153.8 2.6 collective-permute-done.17.refs_1_
  156.3 2.9 %collective-permute-done.18.refs_2_ = bf16[32,24,128]{2,1,0:T(8,128)(2,1)S(1)} collective-permute-done((bf16[32,24,128]{2,1,0:T(8,128)(2,1)S(1)}, bf16[32,24,128]{2,1,0:T(8,128)(2,1)S(1)}, u32[]{:S(2)}, u32[]{:S(2)}) %collective-permute-start.18) | collective-permute-done | bytes 196640 | tf_op jit(solution)/shard_map/ppermute | solution.py:478
  161.0 1.7 collective-permute-start.22
  162.8 7.0 %collective-permute-done.20.refs_1_ = bf16[32,40,128]{2,1,0:T(8,128)(2,1)S(1)} collective-permute-done((bf16[32,40,128]{2,1,0:T(8,128)(2,1)S(1)}, bf16[32,40,128]{2,1,0:T(8,128)(2,1)S(1)}, u32[]{:S(2)}, u32[]{:S(2)}) %collective-permute-start.20) | collective-permute-done | bytes 327712 | tf_op jit(solution)/shard_map/ppermute | solution.py:478
  169.7 4.1 %collective-permute-done.21.refs_2_ = bf16[32,40,128]{2,1,0:T(8,128)(2,1)S(1)} collective-permute-done((bf16[32,40,128]{2,1,0:T(8,128)(2,1)S(1)}, bf16[32,40,128]{2,1,0:T(8,128)(2,1)S(1)}, u32[]{:S(2)}, u32[]{:S(2)}) %collective-permute-start.21) | collective-permute-done | bytes 327712 | tf_op jit(solution)/shard_map/ppermute | solution.py:478
  174.9 3.4 %collective-permute-done.27.refs_4_ = bf16[4,32,24,128]{3,2,1,0:T(8,128)(2,1)S(1)} collective-permute-done((bf16[4,32,24,128]{3,2,1,0:T(8,128)(2,1)S(1)}, bf16[4,32,24,128]{3,2,1,0:T(8,128)(2,1)S(1)}, u32[]{:S(2)}, u32[]{:S(2)}) %collective-permute-start.27) | collective-permute-done | bytes 786464 | tf_op jit(solution)/shard_map/ppermute | solution.py:478
  178.3 6.1 %shard_map.101 = (bf16[3,128,256]{2,1,0:T(8,128)(2,1)S(1)}, bf16[3,128,256]{2,1,0:T(8,128)(2,1)S(1)}, bf16[3,128,256]{2,1,0:T(8,128)(2,1)S(1)}, bf16[3,128,256]{2,1,0:T(8,128)(2,1)S(1)}) custom-call(s32[256]{0:T(256)S(1)} %get-tuple-element.71.refs_0_.a_ref, s32[256]{0:T(256)S(1)} %get-tuple-element.95.refs_1_.b_ref, ...), custom_call_target="tpu_custom_call" | custom-call | tf_op jit(solution)/shard_map/pallas_call | solution.py:140
  184.8 7.6 %shard_map.100 = (bf16[5,128,256]{2,1,0:T(8,128)(2,1)S(1)}, bf16[5,128,256]{2,1,0:T(8,128)(2,1)S(1)}, bf16[5,128,256]{2,1,0:T(8,128)(2,1)S(1)}, bf16[5,128,256]{2,1,0:T(8,128)(2,1)S(1)}) custom-call(s32[256]{0:T(256)S(1)} %get-tuple-element.71.refs_0_.a_ref, s32[256]{0:T(256)S(1)} %get-tuple-element.95.refs_1_.b_ref, ...), custom_call_target="tpu_custom_call" | custom-call | tf_op jit(solution)/shard_map/pallas_call | solution.py:140
  192.5 1.6 collective-permute-start.24
  194.1 1.9 collective-permute-start.25
  196.0 1.5 collective-permute-start.29
  197.5 2.8 %collective-permute-start.30 = (bf16[3,128,256]{2,1,0:T(8,128)(2,1)S(1)}, bf16[3,128,256]{2,1,0:T(8,128)(2,1)S(1)}, u32[]{:S(2)}, u32[]{:S(2)}) collective-permute-start(bf16[3,128,256]{2,1,0:T(8,128)(2,1)S(1)} %get-tuple-element.53), channel_id=1, source_target_pairs={{0,1},{1,2},{2,3},{3,0},{4,5},{5,6},{6,7},{7,4},{8,9},{9,10},{10,1... | collective-permute-start | bytes 589832 | tf_op jit(solution)/shard_map/ppermute | solution.py:481
  200.4 36.8 %collective-permute-done.29.refs_2_ = bf16[3,128,256]{2,1,0:T(8,128)(2,1)S(1)} collective-permute-done((bf16[3,128,256]{2,1,0:T(8,128)(2,1)S(1)}, bf16[3,128,256]{2,1,0:T(8,128)(2,1)S(1)}, u32[]{:S(2)}, u32[]{:S(2)}) %collective-permute-start.29) | collective-permute-done | bytes 196640 | tf_op jit(solution)/shard_map/ppermute | solution.py:481
  237.1 1.8 shard_map.102.refs_4_
  239.0 3.2 %shard_map.103 = bf16[8,512,128]{2,1,0:T(8,128)(2,1)S(1)} custom-call(bf16[5,128,256]{2,1,0:T(8,128)(2,1)S(1)} %get-tuple-element.46.refs_0_, bf16[5,128,256]{2,1,0:T(8,128)(2,1)S(1)} %collective-permute-done.24.refs_1_, bf16[5,128,256]{2,1,0:T(8,128)(2,1)S(1)} %collective-permute-done.25.refs_2_, bf16[5,128,256]{2,1,0:T(8,128)(2,1)S(1)} %collective-permute-done.26.refs_3_, ...), custom_call_target="tpu_custom_call" | custom-call | tf_op jit(solution)/shard_map/pallas_call | solution.py:140
  243.2 4.7 %all-to-all-start.1 = ((bf16[8,512,128]{2,1,0:T(8,128)(2,1)}), bf16[8,512,128]{2,1,0:T(8,128)(2,1)S(1)}, u32[]{:S(2)}, u32[]{:S(2)}) async-start(bf16[8,512,128]{2,1,0:T(8,128)(2,1)} %copy-done.15), calls=%async_computation.1 | async-start | bytes 2097152 | tf_op jit(solution)/shard_map/all_to_all | solution.py:561
  256.0 2.0 collective-permute-start.31
  258.0 3.7 %all-to-all-done.1.grad_ref = bf16[8,512,128]{2,1,0:T(8,128)(2,1)S(1)} async-done(((bf16[8,512,128]{2,1,0:T(8,128)(2,1)}), bf16[8,512,128]{2,1,0:T(8,128)(2,1)S(1)}, u32[]{:S(2)}, u32[]{:S(2)}) %all-to-all-start.1) | async-done | bytes 1048608 | tf_op jit(solution)/shard_map/all_to_all | solution.py:561
  262.2 2.0 collective-permute-start.32
  266.2 1.6 collective-permute-done.32
  267.8 7.3 %haar.1 = f32[512,1024]{1,0:T(8,128)} custom-call(f32[512,1024]{1,0:T(8,128)S(1)} %shard_map.104.refs_0_, f32[8,512]{1,0:T(8,128)S(1)} %sub.141.refs_1_, f32[8,512]{1,0:T(8,128)S(1)} %sub.142.refs_2_, f32[4,1152]{1,0:T(4,128)S(1)} %pad_maximum_fusion.6.refs_3_), custom_call_target="tpu_custom_call" | custom-call | tf_op jit(solution)/shard_map/haar/pallas_call | solution.py:445
  (148 shorter events, 31.0 us)
Async XLA Ops:
  0.6 119.3 %copy-start = (bf16[32,64,256]{2,1,0:T(8,128)(2,1)S(1)}, bf16[32,64,256]{2,1,0:T(8,128)(2,1)}, u32[]{:S(2)}) copy-start(bf16[32,64,256]{2,1,0:T(8,128)(2,1)} %param.10) | copy-start | bytes 3145732
  5.0 5.7 %copy-start.21 = (s32[32]{0:T(128)S(1)}, s32[32]{0:T(128)}, u32[]{:S(2)}) copy-start(s32[32]{0:T(128)} %param.13) | copy-start | bytes 388
  5.0 5.7 %copy-start.22 = (s32[32,1]{0,1:T(1,128)S(1)}, s32[32,1]{0,1:T(1,128)}, u32[]{:S(2)}) copy-start(s32[32,1]{0,1:T(1,128)} %param.12) | copy-start | bytes 388
  6.1 18.2 %all-to-all-start = ((f16[8,512,128]{2,1,0:T(8,128)(2,1)}), f16[8,512,128]{2,1,0:T(8,128)(2,1)}, u32[]{:S(2)}, u32[]{:S(2)}) async-start(f16[8,512,128]{2,1,0:T(8,128)(2,1)} %convert_element_type.179), calls=%async_computation | async-start | bytes 2097152 | tf_op jit(solution)/shard_map/all_to_all | solution.py:498
  31.1 1.2 collective-permute-start
  32.3 3.6 %collective-permute-start.1 = (s32[2,64]{1,0:T(2,128)S(1)}, s32[2,64]{1,0:T(2,128)S(1)}, u32[]{:S(2)}, u32[]{:S(2)}) collective-permute-start(s32[2,64]{1,0:T(2,128)S(1)} %pad_add_fusion.2), channel_id=1, source_target_pairs={{0,8},{4,12},{8,0},{12,4},{16,24},{20,28},{24,16},{28,20},{1,9},{5... | collective-permute-start | bytes 1544 | tf_op jit(solution)/shard_map/ppermute | solution.py:478
  36.0 14.9 %collective-permute-start.2 = (s32[2,128]{1,0:T(2,128)S(1)}, s32[2,128]{1,0:T(2,128)S(1)}, u32[]{:S(2)}, u32[]{:S(2)}) collective-permute-start(s32[2,128]{1,0:T(2,128)S(1)} %pad_add_fusion.3), channel_id=1, source_target_pairs={{0,16},{4,20},{8,24},{12,28},{16,0},{20,4},{24,8},{28,12},{1,17},{... | collective-permute-start | bytes 3080 | tf_op jit(solution)/shard_map/ppermute | solution.py:478
  45.8 20.1 %copy-start.4 = (bf16[1024,1024]{1,0:T(8,128)(2,1)S(1)}, bf16[1024,1024]{1,0:T(8,128)(2,1)}, u32[]{:S(2)}) copy-start(bf16[1024,1024]{1,0:T(8,128)(2,1)} %get-tuple-element.81.refs_7_) | copy-start | bytes 6291460
  45.8 20.1 %copy-start.16 = (f32[3,128,256]{2,1,0:T(8,128)S(1)}, f32[3,128,256]{2,1,0:T(8,128)}, u32[]{:S(2)}) copy-start(f32[3,128,256]{2,1,0:T(8,128)} %fusion.66) | copy-start | bytes 1179652
  45.8 9.7 %collective-permute-start.10 = (f16[3,128,256]{2,1,0:T(8,128)(2,1)}, f16[3,128,256]{2,1,0:T(8,128)(2,1)S(1)}, u32[]{:S(2)}, u32[]{:S(2)}) collective-permute-start(f16[3,128,256]{2,1,0:T(8,128)(2,1)} %convert_element_type.188), channel_id=1, source_target_pairs={{0,3},{1,0},{2,1},{3,2},{4,7},{5,4},{6,5},{7,6},{8,11},{9,8},{10,9... | collective-permute-start | bytes 589832 | tf_op jit(solution)/shard_map/ppermute | solution.py:481
  49.9 15.9 %collective-permute-start.11 = (f16[3,128,256]{2,1,0:T(8,128)(2,1)}, f16[3,128,256]{2,1,0:T(8,128)(2,1)S(1)}, u32[]{:S(2)}, u32[]{:S(2)}) collective-permute-start(f16[3,128,256]{2,1,0:T(8,128)(2,1)} %convert_element_type.187), channel_id=1, source_target_pairs={{0,2},{1,3},{2,0},{3,1},{4,6},{5,7},{6,4},{7,5},{8,10},{9,11},{10,... | collective-permute-start | bytes 589832 | tf_op jit(solution)/shard_map/ppermute | solution.py:481
  49.9 16.0 %collective-permute-start.12 = (f16[3,128,256]{2,1,0:T(8,128)(2,1)}, f16[3,128,256]{2,1,0:T(8,128)(2,1)S(1)}, u32[]{:S(2)}, u32[]{:S(2)}) collective-permute-start(f16[3,128,256]{2,1,0:T(8,128)(2,1)} %convert_element_type.186), channel_id=1, source_target_pairs={{0,1},{1,2},{2,3},{3,0},{4,5},{5,6},{6,7},{7,4},{8,9},{9,10},{10,1... | collective-permute-start | bytes 589832 | tf_op jit(solution)/shard_map/ppermute | solution.py:481
  72.9 43.1 %collective-permute-start.13 = (f16[4,32,24,128]{3,2,1,0:T(8,128)(2,1)S(1)}, f16[4,32,24,128]{3,2,1,0:T(8,128)(2,1)S(1)}, u32[]{:S(2)}, u32[]{:S(2)}) collective-permute-start(f16[4,32,24,128]{3,2,1,0:T(8,128)(2,1)S(1)} %convert_element_type.214), channel_id=1, source_target_pairs={{0,4},{4,0},{8,12},{12,8},{16,20},{20,16},{24,28},{28,24},{1,5},{5... | collective-permute-start | bytes 2359304 | tf_op jit(solution)/shard_map/ppermute | solution.py:478
  77.2 9.2 %collective-permute-start.3 = (f16[5,128,256]{2,1,0:T(8,128)(2,1)S(1)}, f16[5,128,256]{2,1,0:T(8,128)(2,1)S(1)}, u32[]{:S(2)}, u32[]{:S(2)}) collective-permute-start(f16[5,128,256]{2,1,0:T(8,128)(2,1)S(1)} %convert_element_type.191), channel_id=1, source_target_pairs={{0,3},{1,0},{2,1},{3,2},{4,7},{5,4},{6,5},{7,6},{8,11},{9,8},{10,9... | collective-permute-start | bytes 983048 | tf_op jit(solution)/shard_map/ppermute | solution.py:481
  77.4 30.6 %collective-permute-start.4 = (f16[5,128,256]{2,1,0:T(8,128)(2,1)S(1)}, f16[5,128,256]{2,1,0:T(8,128)(2,1)S(1)}, u32[]{:S(2)}, u32[]{:S(2)}) collective-permute-start(f16[5,128,256]{2,1,0:T(8,128)(2,1)S(1)} %convert_element_type.193), channel_id=1, source_target_pairs={{0,2},{1,3},{2,0},{3,1},{4,6},{5,7},{6,4},{7,5},{8,10},{9,11},{10,... | collective-permute-start | bytes 983048 | tf_op jit(solution)/shard_map/ppermute | solution.py:481
  80.0 28.1 %collective-permute-start.5 = (f16[5,128,256]{2,1,0:T(8,128)(2,1)S(1)}, f16[5,128,256]{2,1,0:T(8,128)(2,1)S(1)}, u32[]{:S(2)}, u32[]{:S(2)}) collective-permute-start(f16[5,128,256]{2,1,0:T(8,128)(2,1)S(1)} %convert_element_type.195), channel_id=1, source_target_pairs={{0,1},{1,2},{2,3},{3,0},{4,5},{5,6},{6,7},{7,4},{8,9},{9,10},{10,1... | collective-permute-start | bytes 983048 | tf_op jit(solution)/shard_map/ppermute | solution.py:481
  82.3 25.9 %copy-start.6 = (bf16[1024,1024]{1,0:T(8,128)(2,1)S(1)}, bf16[1024,1024]{1,0:T(8,128)(2,1)}, u32[]{:S(2)}) copy-start(bf16[1024,1024]{1,0:T(8,128)(2,1)} %get-tuple-element.83.refs_6_) | copy-start | bytes 6291460
  115.9 13.3 %collective-permute-start.6 = (f16[4,32,40,128]{3,2,1,0:T(8,128)(2,1)S(1)}, f16[4,32,40,128]{3,2,1,0:T(8,128)(2,1)S(1)}, u32[]{:S(2)}, u32[]{:S(2)}) collective-permute-start(f16[4,32,40,128]{3,2,1,0:T(8,128)(2,1)S(1)} %convert_element_type.201), channel_id=1, source_target_pairs={{0,4},{4,0},{8,12},{12,8},{16,20},{20,16},{24,28},{28,24},{1,5},{5... | collective-permute-start | bytes 3932168 | tf_op jit(solution)/shard_map/ppermute | solution.py:478
  116.4 7.8 %collective-permute-start.14 = (f16[32,24,128]{2,1,0:T(8,128)(2,1)S(1)}, f16[32,24,128]{2,1,0:T(8,128)(2,1)S(1)}, u32[]{:S(2)}, u32[]{:S(2)}) collective-permute-start(f16[32,24,128]{2,1,0:T(8,128)(2,1)S(1)} %get-tuple-element.75), channel_id=1, source_target_pairs={{0,8},{4,12},{8,0},{12,4},{16,24},{20,28},{24,16},{28,20},{1,9},{5... | collective-permute-start | bytes 589832 | tf_op jit(solution)/shard_map/ppermute | solution.py:478
  117.8 11.2 %collective-permute-start.15 = (f16[32,24,128]{2,1,0:T(8,128)(2,1)S(1)}, f16[32,24,128]{2,1,0:T(8,128)(2,1)S(1)}, u32[]{:S(2)}, u32[]{:S(2)}) collective-permute-start(f16[32,24,128]{2,1,0:T(8,128)(2,1)S(1)} %get-tuple-element.77), channel_id=1, source_target_pairs={{0,16},{4,20},{8,24},{12,28},{16,0},{20,4},{24,8},{28,12},{1,17},{... | collective-permute-start | bytes 589832 | tf_op jit(solution)/shard_map/ppermute | solution.py:478
  119.4 9.7 %collective-permute-start.16 = (f16[32,24,128]{2,1,0:T(8,128)(2,1)S(1)}, f16[32,24,128]{2,1,0:T(8,128)(2,1)S(1)}, u32[]{:S(2)}, u32[]{:S(2)}) collective-permute-start(f16[32,24,128]{2,1,0:T(8,128)(2,1)S(1)} %get-tuple-element.76), channel_id=1, source_target_pairs={{0,24},{4,28},{8,16},{12,20},{16,8},{20,12},{24,0},{28,4},{1,25},{... | collective-permute-start | bytes 589832 | tf_op jit(solution)/shard_map/ppermute | solution.py:478
  129.8 10.6 %collective-permute-start.7 = (f16[32,40,128]{2,1,0:T(8,128)(2,1)S(1)}, f16[32,40,128]{2,1,0:T(8,128)(2,1)S(1)}, u32[]{:S(2)}, u32[]{:S(2)}) collective-permute-start(f16[32,40,128]{2,1,0:T(8,128)(2,1)S(1)} %get-tuple-element.72), channel_id=1, source_target_pairs={{0,8},{4,12},{8,0},{12,4},{16,24},{20,28},{24,16},{28,20},{1,9},{5... | collective-permute-start | bytes 983048 | tf_op jit(solution)/shard_map/ppermute | solution.py:478
  131.1 16.0 %collective-permute-start.8 = (f16[32,40,128]{2,1,0:T(8,128)(2,1)S(1)}, f16[32,40,128]{2,1,0:T(8,128)(2,1)S(1)}, u32[]{:S(2)}, u32[]{:S(2)}) collective-permute-start(f16[32,40,128]{2,1,0:T(8,128)(2,1)S(1)} %get-tuple-element.74), channel_id=1, source_target_pairs={{0,16},{4,20},{8,24},{12,28},{16,0},{20,4},{24,8},{28,12},{1,17},{... | collective-permute-start | bytes 983048 | tf_op jit(solution)/shard_map/ppermute | solution.py:478
  131.9 15.2 %collective-permute-start.9 = (f16[32,40,128]{2,1,0:T(8,128)(2,1)S(1)}, f16[32,40,128]{2,1,0:T(8,128)(2,1)S(1)}, u32[]{:S(2)}, u32[]{:S(2)}) collective-permute-start(f16[32,40,128]{2,1,0:T(8,128)(2,1)S(1)} %get-tuple-element.73), channel_id=1, source_target_pairs={{0,24},{4,28},{8,16},{12,20},{16,8},{20,12},{24,0},{28,4},{1,25},{... | collective-permute-start | bytes 983048 | tf_op jit(solution)/shard_map/ppermute | solution.py:478
  149.1 7.2 %collective-permute-start.17 = (bf16[32,24,128]{2,1,0:T(8,128)(2,1)S(1)}, bf16[32,24,128]{2,1,0:T(8,128)(2,1)S(1)}, u32[]{:S(2)}, u32[]{:S(2)}) collective-permute-start(bf16[32,24,128]{2,1,0:T(8,128)(2,1)S(1)} %pad_maximum_fusion.3.refs_0_), channel_id=1, source_target_pairs={{0,8},{4,12},{8,0},{12,4},{16,24},{20,28},{24,16},{28,20},{1,9},{5... | collective-permute-start | bytes 589832 | tf_op jit(solution)/shard_map/ppermute | solution.py:478
  149.7 9.5 %collective-permute-start.18 = (bf16[32,24,128]{2,1,0:T(8,128)(2,1)S(1)}, bf16[32,24,128]{2,1,0:T(8,128)(2,1)S(1)}, u32[]{:S(2)}, u32[]{:S(2)}) collective-permute-start(bf16[32,24,128]{2,1,0:T(8,128)(2,1)S(1)} %pad_maximum_fusion.3.refs_0_), channel_id=1, source_target_pairs={{0,16},{4,20},{8,24},{12,28},{16,0},{20,4},{24,8},{28,12},{1,17},{... | collective-permute-start | bytes 589832 | tf_op jit(solution)/shard_map/ppermute | solution.py:478
  151.2 8.1 %collective-permute-start.19 = (bf16[32,24,128]{2,1,0:T(8,128)(2,1)S(1)}, bf16[32,24,128]{2,1,0:T(8,128)(2,1)S(1)}, u32[]{:S(2)}, u32[]{:S(2)}) collective-permute-start(bf16[32,24,128]{2,1,0:T(8,128)(2,1)S(1)} %pad_maximum_fusion.3.refs_0_), channel_id=1, source_target_pairs={{0,24},{4,28},{8,16},{12,20},{16,8},{20,12},{24,0},{28,4},{1,25},{... | collective-permute-start | bytes 589832 | tf_op jit(solution)/shard_map/ppermute | solution.py:478
  159.3 10.5 %collective-permute-start.20 = (bf16[32,40,128]{2,1,0:T(8,128)(2,1)S(1)}, bf16[32,40,128]{2,1,0:T(8,128)(2,1)S(1)}, u32[]{:S(2)}, u32[]{:S(2)}) collective-permute-start(bf16[32,40,128]{2,1,0:T(8,128)(2,1)S(1)} %pad_maximum_fusion.2.refs_0_), channel_id=1, source_target_pairs={{0,8},{4,12},{8,0},{12,4},{16,24},{20,28},{24,16},{28,20},{1,9},{5... | collective-permute-start | bytes 983048 | tf_op jit(solution)/shard_map/ppermute | solution.py:478
  160.5 13.4 %collective-permute-start.21 = (bf16[32,40,128]{2,1,0:T(8,128)(2,1)S(1)}, bf16[32,40,128]{2,1,0:T(8,128)(2,1)S(1)}, u32[]{:S(2)}, u32[]{:S(2)}) collective-permute-start(bf16[32,40,128]{2,1,0:T(8,128)(2,1)S(1)} %pad_maximum_fusion.2.refs_0_), channel_id=1, source_target_pairs={{0,16},{4,20},{8,24},{12,28},{16,0},{20,4},{24,8},{28,12},{1,17},{... | collective-permute-start | bytes 983048 | tf_op jit(solution)/shard_map/ppermute | solution.py:478
  161.0 12.9 %collective-permute-start.22 = (bf16[32,40,128]{2,1,0:T(8,128)(2,1)S(1)}, bf16[32,40,128]{2,1,0:T(8,128)(2,1)S(1)}, u32[]{:S(2)}, u32[]{:S(2)}) collective-permute-start(bf16[32,40,128]{2,1,0:T(8,128)(2,1)S(1)} %pad_maximum_fusion.2.refs_0_), channel_id=1, source_target_pairs={{0,24},{4,28},{8,16},{12,20},{16,8},{20,12},{24,0},{28,4},{1,25},{... | collective-permute-start | bytes 983048 | tf_op jit(solution)/shard_map/ppermute | solution.py:478
  174.1 10.7 %collective-permute-start.23 = (bf16[4,32,40,128]{3,2,1,0:T(8,128)(2,1)S(1)}, bf16[4,32,40,128]{3,2,1,0:T(8,128)(2,1)S(1)}, u32[]{:S(2)}, u32[]{:S(2)}) collective-permute-start(bf16[4,32,40,128]{3,2,1,0:T(8,128)(2,1)S(1)} %pad_maximum_fusion), channel_id=1, source_target_pairs={{0,4},{4,0},{8,12},{12,8},{16,20},{20,16},{24,28},{28,24},{1,5},{5... | collective-permute-start | bytes 3932168 | tf_op jit(solution)/shard_map/ppermute | solution.py:478
  174.3 4.0 %collective-permute-start.27 = (bf16[4,32,24,128]{3,2,1,0:T(8,128)(2,1)S(1)}, bf16[4,32,24,128]{3,2,1,0:T(8,128)(2,1)S(1)}, u32[]{:S(2)}, u32[]{:S(2)}) collective-permute-start(bf16[4,32,24,128]{3,2,1,0:T(8,128)(2,1)S(1)} %pad_maximum_fusion.1), channel_id=1, source_target_pairs={{0,4},{4,0},{8,12},{12,8},{16,20},{20,16},{24,28},{28,24},{1,5},{5... | collective-permute-start | bytes 2359304 | tf_op jit(solution)/shard_map/ppermute | solution.py:478
  184.5 52.7 %copy-start.11 = (bf16[1024,512]{1,0:T(8,128)(2,1)S(1)}, bf16[1024,512]{1,0:T(8,128)(2,1)}, u32[]{:S(2)}) copy-start(bf16[1024,512]{1,0:T(8,128)(2,1)} %get-tuple-element.84.refs_5_.refs_6_) | copy-start | bytes 3145732
  184.5 52.7 %copy-start.12 = (bf16[1024,512]{1,0:T(8,128)(2,1)S(1)}, bf16[1024,512]{1,0:T(8,128)(2,1)}, u32[]{:S(2)}) copy-start(bf16[1024,512]{1,0:T(8,128)(2,1)} %get-tuple-element.85.refs_4_.refs_5_) | copy-start | bytes 3145732
  184.5 13.0 %collective-permute-start.28 = (bf16[3,128,256]{2,1,0:T(8,128)(2,1)S(1)}, bf16[3,128,256]{2,1,0:T(8,128)(2,1)S(1)}, u32[]{:S(2)}, u32[]{:S(2)}) collective-permute-start(bf16[3,128,256]{2,1,0:T(8,128)(2,1)S(1)} %get-tuple-element.51), channel_id=1, source_target_pairs={{0,3},{1,0},{2,1},{3,2},{4,7},{5,4},{6,5},{7,6},{8,11},{9,8},{10,9... | collective-permute-start | bytes 589832 | tf_op jit(solution)/shard_map/ppermute | solution.py:481
  192.5 46.5 %collective-permute-start.24 = (bf16[5,128,256]{2,1,0:T(8,128)(2,1)S(1)}, bf16[5,128,256]{2,1,0:T(8,128)(2,1)S(1)}, u32[]{:S(2)}, u32[]{:S(2)}) collective-permute-start(bf16[5,128,256]{2,1,0:T(8,128)(2,1)S(1)} %get-tuple-element.47), channel_id=1, source_target_pairs={{0,3},{1,0},{2,1},{3,2},{4,7},{5,4},{6,5},{7,6},{8,11},{9,8},{10,9... | collective-permute-start | bytes 983048 | tf_op jit(solution)/shard_map/ppermute | solution.py:481
  194.1 44.9 %collective-permute-start.25 = (bf16[5,128,256]{2,1,0:T(8,128)(2,1)S(1)}, bf16[5,128,256]{2,1,0:T(8,128)(2,1)S(1)}, u32[]{:S(2)}, u32[]{:S(2)}) collective-permute-start(bf16[5,128,256]{2,1,0:T(8,128)(2,1)S(1)} %get-tuple-element.48), channel_id=1, source_target_pairs={{0,2},{1,3},{2,0},{3,1},{4,6},{5,7},{6,4},{7,5},{8,10},{9,11},{10,... | collective-permute-start | bytes 983048 | tf_op jit(solution)/shard_map/ppermute | solution.py:481
  196.0 43.0 %collective-permute-start.26 = (bf16[5,128,256]{2,1,0:T(8,128)(2,1)S(1)}, bf16[5,128,256]{2,1,0:T(8,128)(2,1)S(1)}, u32[]{:S(2)}, u32[]{:S(2)}) collective-permute-start(bf16[5,128,256]{2,1,0:T(8,128)(2,1)S(1)} %get-tuple-element.49), channel_id=1, source_target_pairs={{0,1},{1,2},{2,3},{3,0},{4,5},{5,6},{6,7},{7,4},{8,9},{9,10},{10,1... | collective-permute-start | bytes 983048 | tf_op jit(solution)/shard_map/ppermute | solution.py:481
  196.0 41.1 %collective-permute-start.29 = (bf16[3,128,256]{2,1,0:T(8,128)(2,1)S(1)}, bf16[3,128,256]{2,1,0:T(8,128)(2,1)S(1)}, u32[]{:S(2)}, u32[]{:S(2)}) collective-permute-start(bf16[3,128,256]{2,1,0:T(8,128)(2,1)S(1)} %get-tuple-element.52), channel_id=1, source_target_pairs={{0,2},{1,3},{2,0},{3,1},{4,6},{5,7},{6,4},{7,5},{8,10},{9,11},{10,... | collective-permute-start | bytes 589832 | tf_op jit(solution)/shard_map/ppermute | solution.py:481
  197.5 39.6 %collective-permute-start.30 = (bf16[3,128,256]{2,1,0:T(8,128)(2,1)S(1)}, bf16[3,128,256]{2,1,0:T(8,128)(2,1)S(1)}, u32[]{:S(2)}, u32[]{:S(2)}) collective-permute-start(bf16[3,128,256]{2,1,0:T(8,128)(2,1)S(1)} %get-tuple-element.53), channel_id=1, source_target_pairs={{0,1},{1,2},{2,3},{3,0},{4,5},{5,6},{6,7},{7,4},{8,9},{9,10},{10,1... | collective-permute-start | bytes 589832 | tf_op jit(solution)/shard_map/ppermute | solution.py:481
  239.0 8.9 %copy-start.20 = (f32[4]{0:T(128)S(1)}, f32[4]{0:T(128)}, u32[]{:S(2)}) copy-start(f32[4]{0:T(128)} %param.14) | copy-start | bytes 52
  243.2 21.7 %copy-start.14 = (f32[512,1024]{1,0:T(8,128)S(1)}, f32[512,1024]{1,0:T(8,128)}, u32[]{:S(2)}) copy-start(f32[512,1024]{1,0:T(8,128)} %image_ref.3) | copy-start | bytes 6291460
  243.2 18.6 %all-to-all-start.1 = ((bf16[8,512,128]{2,1,0:T(8,128)(2,1)}), bf16[8,512,128]{2,1,0:T(8,128)(2,1)S(1)}, u32[]{:S(2)}, u32[]{:S(2)}) async-start(bf16[8,512,128]{2,1,0:T(8,128)(2,1)} %copy-done.15), calls=%async_computation.1 | async-start | bytes 2097152 | tf_op jit(solution)/shard_map/all_to_all | solution.py:561
  256.0 10.2 %collective-permute-start.33 = (f32[8,512]{1,0:T(8,128)S(1)}, f32[8,512]{1,0:T(8,128)S(1)}, u32[]{:S(2)}, u32[]{:S(2)}) collective-permute-start(f32[8,512]{1,0:T(8,128)S(1)} %get-tuple-element.58), channel_id=1, source_target_pairs={{0,3},{1,0},{2,1},{3,2},{4,7},{5,4},{6,5},{7,6},{8,11},{9,8},{10,9... | collective-permute-start | bytes 49160 | tf_op jit(solution)/shard_map/ppermute | solution.py:481
  256.0 10.2 %collective-permute-start.31 = (f32[8,512]{1,0:T(8,128)S(1)}, f32[8,512]{1,0:T(8,128)S(1)}, u32[]{:S(2)}, u32[]{:S(2)}) collective-permute-start(f32[8,512]{1,0:T(8,128)S(1)} %get-tuple-element.56), channel_id=1, source_target_pairs={{0,1},{1,2},{2,3},{3,0},{4,5},{5,6},{6,7},{7,4},{8,9},{9,10},{10,1... | collective-permute-start | bytes 49160 | tf_op jit(solution)/shard_map/ppermute | solution.py:481
  262.1 4.1 %collective-permute-start.34 = (f32[8,512]{1,0:T(8,128)S(1)}, f32[8,512]{1,0:T(8,128)S(1)}, u32[]{:S(2)}, u32[]{:S(2)}) collective-permute-start(f32[8,512]{1,0:T(8,128)S(1)} %get-tuple-element.59), channel_id=1, source_target_pairs={{0,3},{1,0},{2,1},{3,2},{4,7},{5,4},{6,5},{7,6},{8,11},{9,8},{10,9... | collective-permute-start | bytes 49160 | tf_op jit(solution)/shard_map/ppermute | solution.py:481
  262.2 5.6 %collective-permute-start.32 = (f32[8,512]{1,0:T(8,128)S(1)}, f32[8,512]{1,0:T(8,128)S(1)}, u32[]{:S(2)}, u32[]{:S(2)}) collective-permute-start(f32[8,512]{1,0:T(8,128)S(1)} %get-tuple-element.57), channel_id=1, source_target_pairs={{0,1},{1,2},{2,3},{3,0},{4,5},{5,6},{6,7},{7,4},{8,9},{9,10},{10,1... | collective-permute-start | bytes 49160 | tf_op jit(solution)/shard_map/ppermute | solution.py:481
  267.8 7.3 %copy-start.1 = (bf16[32,64,256]{2,1,0:T(8,128)(2,1)S(1)}, bf16[32,64,256]{2,1,0:T(8,128)(2,1)}, u32[]{:S(2)}) copy-start(bf16[32,64,256]{2,1,0:T(8,128)(2,1)} %param.10) | copy-start | bytes 3145732
  (12 other events, 27.8 us)
